TPU v7x, 32 devices: a whole 2x2x4 slice. The times are simulated.
32 devices in a mesh: fsdp: 8 (over z, core), context: 2 (over x), tensor: 2 (over y).
Axes of the slice: x: 2, y: 2, z: 4, core: 2. Of those that a mesh axis runs over, the one named last changes fastest.
Arguments:
- tokens: bfloat16 [16, 2048, 1024], P('fsdp', 'context'), may hold values from -6 to 6
- segment_ids: int32 [16, 2048], P('fsdp', 'context'), may hold values from 0 to 7, never falling along the last dimension, each value on 1 to 1024 neighbouring positions
- qkv_weight: bfloat16 [3, 1024, 1024], P(None, 'fsdp', 'tensor'), may hold values from -0.1875 to 0.1875
- qv_bias: bfloat16 [2, 16, 64], P(None, 'tensor', 'fsdp'), may hold values from -1.5 to 1.5
- proj_weight: bfloat16 [1024, 1024], P('tensor', 'fsdp'), may hold values from -0.75 to 0.75
- proj_bias: bfloat16 [1024], P('fsdp'), may hold values from -1.5 to 1.5
- first_gain: bfloat16 [1024], P('fsdp'), may hold values from 0.5 to 1.5
- first_shift: bfloat16 [1024], P('fsdp'), may hold values from -1.5 to 1.5
- up_weight: bfloat16 [1024, 4096], P('fsdp', 'tensor'), may hold values from -0.1875 to 0.1875
- up_bias: bfloat16 [64, 64], P('tensor', 'fsdp'), may hold values from -1.5 to 1.5
- down_weight: bfloat16 [4096, 1024], P('tensor', 'fsdp'), may hold values from -0.09375 to 0.09375
- down_bias: bfloat16 [1024], P('fsdp'), may hold values from -1.5 to 1.5
- second_gain: bfloat16 [1024], P('fsdp'), may hold values from 0.5 to 1.5
- second_shift: bfloat16 [1024], P('fsdp'), may hold values from -1.5 to 1.5
- out_grad: bfloat16 [16, 2048, 1024], P('fsdp', 'context'), may hold values from -6 to 6
Outputs:
- layer_output: bfloat16 [16, 2048, 1024], P('fsdp', 'context')
- tokens_grad: bfloat16 [16, 2048, 1024], P('fsdp', 'context')
- qkv_grad: float32 [3, 1024, 1024], P(None, 'fsdp', 'tensor')
- qv_bias_grad: float32 [2, 16, 64], P(None, 'tensor', 'fsdp')
- proj_grad: float32 [1024, 1024], P('tensor', 'fsdp')
- proj_bias_grad: float32 [1024], P('fsdp')
- first_gain_grad: float32 [1024], P('fsdp')
- first_shift_grad: float32 [1024], P('fsdp')
- up_grad: float32 [1024, 4096], P('fsdp', 'tensor')
- up_bias_grad: float32 [64, 64], P('tensor', 'fsdp')
- down_grad: float32 [4096, 1024], P('tensor', 'fsdp')
- down_bias_grad: float32 [1024], P('fsdp')
- second_gain_grad: float32 [1024], P('fsdp')
- second_shift_grad: float32 [1024], P('fsdp')
Inputs may be any that keep to these rules, and one draw needn't show every extreme that they name: `segment_ids`: within each sequence the ids never fall; each of the 8 segments covers 1 to 1024 positions and one covers exactly 1024.
All inputs are finite; a program needn't handle non-finite values.
Results may differ from a plain program's by a relative error of at most 0.019.
Values may be sent and summed in bfloat16 or wider, within the bound.
A program may use at most 384 MiB of HBM per device.

v0:
```python
import jax
import jax.numpy as jnp
from jax import lax
from jax.sharding import PartitionSpec as P

NORM_EPS = 1e-05


def layer_norm(hidden_rows, norm_gain, norm_shift):
    row_mean = jnp.mean(hidden_rows, axis=-1, keepdims=True)
    centred = hidden_rows - row_mean
    variance = jnp.mean(centred * centred, axis=-1, keepdims=True)
    return centred * lax.rsqrt(variance + NORM_EPS) * norm_gain + norm_shift


def exact_gelu(values):
    return jax.nn.gelu(values, approximate=False)


def masked_logits(query_heads, key_heads, seg_query, seg_key, score_scale):
    logits = (
        jnp.einsum("qhe,khe->hqk", query_heads, key_heads, preferred_element_type=jnp.float32)
        * score_scale
    )
    same_doc = (seg_query[:, None] == seg_key[None, :])[None, :, :]
    return jnp.where(same_doc, logits, -1e30)


def on_device(
    tokens,
    segment_ids,
    qkv_weight,
    qv_bias,
    proj_weight,
    proj_bias,
    first_gain,
    first_shift,
    up_weight,
    up_bias,
    down_weight,
    down_bias,
    second_gain,
    second_shift,
    out_grad,
):
    seq_count, span, width = tokens.shape
    total_rows = seq_count * span
    share = total_rows // lax.axis_size("tensor")
    row_start = lax.axis_index("tensor") * share
    token_rows = tokens.reshape(total_rows, width)
    gathered = (
        lax.all_gather(qkv_weight, "fsdp", axis=1, tiled=True),
        lax.all_gather(qv_bias, "fsdp", axis=2, tiled=True),
        lax.all_gather(proj_weight, "fsdp", axis=1, tiled=True),
        lax.all_gather(proj_bias, "fsdp", axis=0, tiled=True),
        lax.all_gather(first_gain, "fsdp", axis=0, tiled=True),
        lax.all_gather(first_shift, "fsdp", axis=0, tiled=True),
        lax.all_gather(up_weight, "fsdp", axis=0, tiled=True),
        lax.all_gather(up_bias, "fsdp", axis=1, tiled=True),
        lax.all_gather(down_weight, "fsdp", axis=1, tiled=True),
        lax.all_gather(down_bias, "fsdp", axis=0, tiled=True),
        lax.all_gather(second_gain, "fsdp", axis=0, tiled=True),
        lax.all_gather(second_shift, "fsdp", axis=0, tiled=True),
    )
    qkv_full, qv_full, proj_full, proj_add, gain_one, shift_one = (
        gathered[0],
        gathered[1],
        gathered[2],
        gathered[3],
        gathered[4],
        gathered[5],
    )
    up_full, up_add, down_full, down_add, gain_two, shift_two = (
        gathered[6],
        gathered[7],
        gathered[8],
        gathered[9],
        gathered[10],
        gathered[11],
    )
    local_width = qkv_full.shape[2]
    head_count = qv_full.shape[1]
    head_size = qv_full.shape[2]
    score_scale = float(head_size) ** (-0.5)
    projected = jnp.einsum("rd,cde->cre", token_rows, qkv_full, preferred_element_type=jnp.float32)
    bias_rows = qv_full.reshape(2, local_width).astype(jnp.float32)
    head_shape = (seq_count, span, head_count, head_size)
    query_heads = (projected[0] + bias_rows[0]).astype(jnp.bfloat16).reshape(head_shape)
    key_heads = projected[1].astype(jnp.bfloat16).reshape(head_shape)
    value_heads = (projected[2] + bias_rows[1]).astype(jnp.bfloat16).reshape(head_shape)
    key_all, value_all, seg_all = (
        lax.all_gather(key_heads, "context", axis=1, tiled=True),
        lax.all_gather(value_heads, "context", axis=1, tiled=True),
        lax.all_gather(segment_ids, "context", axis=1, tiled=True),
    )

    def attend_forward(pieces):
        query_one, key_one, value_one, seg_query, seg_key = pieces
        logits = masked_logits(query_one, key_one, seg_query, seg_key, score_scale)
        row_top = jnp.max(logits, axis=-1, keepdims=True)
        weights = jnp.exp(logits - row_top)
        row_total = jnp.sum(weights, axis=-1, keepdims=True)
        soft_low = (weights / row_total).astype(jnp.bfloat16)
        mixed_one = jnp.einsum(
            "hqk,khe->qhe", soft_low, value_one, preferred_element_type=jnp.float32
        )
        return (mixed_one.astype(jnp.bfloat16), row_top + jnp.log(row_total))

    mixed, log_totals = lax.map(
        attend_forward, (query_heads, key_all, value_all, segment_ids, seg_all)
    )
    context_low = mixed.reshape(total_rows, local_width)
    attn_part = jnp.dot(context_low, proj_full, preferred_element_type=jnp.float32)
    attn_share = lax.psum_scatter(
        attn_part, "tensor", scatter_dimension=0, tiled=True
    ) + proj_add.astype(jnp.float32)
    token_share = lax.dynamic_slice_in_dim(token_rows, row_start, share, 0).astype(jnp.float32)
    first_share, first_pull = jax.vjp(
        layer_norm,
        token_share + attn_share,
        gain_one.astype(jnp.float32),
        shift_one.astype(jnp.float32),
    )
    first_low = lax.all_gather(first_share.astype(jnp.bfloat16), "tensor", axis=0, tiled=True)
    hidden_pre = jnp.dot(first_low, up_full, preferred_element_type=jnp.float32) + up_add.reshape(
        -1
    ).astype(jnp.float32)
    activation, gelu_pull = jax.vjp(exact_gelu, hidden_pre)
    act_low = activation.astype(jnp.bfloat16)
    down_part = jnp.dot(act_low, down_full, preferred_element_type=jnp.float32)
    branch_share = lax.psum_scatter(
        down_part, "tensor", scatter_dimension=0, tiled=True
    ) + down_add.astype(jnp.float32)
    output_share, second_pull = jax.vjp(
        layer_norm,
        first_share + branch_share,
        gain_two.astype(jnp.float32),
        shift_two.astype(jnp.float32),
    )
    qkv_back, proj_back, up_back, down_back = (
        lax.all_gather(qkv_weight, "fsdp", axis=1, tiled=True),
        lax.all_gather(proj_weight, "fsdp", axis=1, tiled=True),
        lax.all_gather(up_weight, "fsdp", axis=0, tiled=True),
        lax.all_gather(down_weight, "fsdp", axis=1, tiled=True),
    )
    cot_share = lax.dynamic_slice_in_dim(
        out_grad.reshape(total_rows, width), row_start, share, 0
    ).astype(jnp.float32)
    grad_second, gain_two_part, shift_two_part = second_pull(cot_share)
    branch_low = lax.all_gather(grad_second.astype(jnp.bfloat16), "tensor", axis=0, tiled=True)
    grad_down_bias = jnp.sum(branch_low.astype(jnp.float32), axis=0)
    grad_down = jnp.einsum("rf,rd->fd", act_low, branch_low, preferred_element_type=jnp.float32)
    grad_act = jnp.einsum("rd,fd->rf", branch_low, down_back, preferred_element_type=jnp.float32)
    hidden_low = gelu_pull(grad_act)[0].astype(jnp.bfloat16)
    grad_up_bias = jnp.sum(hidden_low.astype(jnp.float32), axis=0).reshape(up_add.shape)
    grad_up = jnp.einsum("rd,rf->df", first_low, hidden_low, preferred_element_type=jnp.float32)
    norm_part = jnp.einsum("rf,df->rd", hidden_low, up_back, preferred_element_type=jnp.float32)
    grad_first = grad_second + lax.psum_scatter(
        norm_part, "tensor", scatter_dimension=0, tiled=True
    )
    grad_in_one, gain_one_part, shift_one_part = first_pull(grad_first)
    attn_low = lax.all_gather(grad_in_one.astype(jnp.bfloat16), "tensor", axis=0, tiled=True)
    grad_proj_bias = jnp.sum(attn_low.astype(jnp.float32), axis=0)
    grad_proj = jnp.einsum("rl,rd->ld", context_low, attn_low, preferred_element_type=jnp.float32)
    grad_context = (
        jnp.einsum("rd,ld->rl", attn_low, proj_back, preferred_element_type=jnp.float32)
        .astype(jnp.bfloat16)
        .reshape(head_shape)
    )

    def attend_backward(pieces):
        query_one, key_one, value_one, seg_query, seg_key, log_total, context_grad = pieces
        logits = masked_logits(query_one, key_one, seg_query, seg_key, score_scale)
        soft_again = jnp.exp(logits - log_total)
        grad_soft = jnp.einsum(
            "qhe,khe->hqk", context_grad, value_one, preferred_element_type=jnp.float32
        )
        row_delta = jnp.sum(grad_soft * soft_again, axis=-1, keepdims=True)
        grad_logits = (soft_again * (grad_soft - row_delta)).astype(jnp.bfloat16)
        query_grad = (
            jnp.einsum("hqk,khe->qhe", grad_logits, key_one, preferred_element_type=jnp.float32)
            * score_scale
        ).astype(jnp.bfloat16)
        key_part = (
            jnp.einsum("hqk,qhe->khe", grad_logits, query_one, preferred_element_type=jnp.float32)
            * score_scale
        )
        value_part = jnp.einsum(
            "hqk,qhe->khe",
            soft_again.astype(jnp.bfloat16),
            context_grad,
            preferred_element_type=jnp.float32,
        )
        return (query_grad, key_part, value_part)

    grad_query, key_terms, value_terms = lax.map(
        attend_backward,
        (query_heads, key_all, value_all, segment_ids, seg_all, log_totals, grad_context),
    )
    key_grad, value_grad = (
        lax.psum_scatter(
            key_terms.astype(jnp.bfloat16), "context", scatter_dimension=1, tiled=True
        ).astype(jnp.float32),
        lax.psum_scatter(
            value_terms.astype(jnp.bfloat16), "context", scatter_dimension=1, tiled=True
        ).astype(jnp.float32),
    )
    grad_stack = jnp.stack(
        [
            grad_query.reshape(total_rows, local_width),
            key_grad.astype(jnp.bfloat16).reshape(total_rows, local_width),
            value_grad.astype(jnp.bfloat16).reshape(total_rows, local_width),
        ]
    )
    stack_sums = jnp.sum(grad_stack.astype(jnp.float32), axis=1)
    grad_qv_bias = jnp.stack([stack_sums[0], stack_sums[2]]).reshape(qv_full.shape)
    grad_qkv = jnp.einsum("rd,cre->cde", token_rows, grad_stack, preferred_element_type=jnp.float32)
    input_part = jnp.einsum("cre,cde->rd", grad_stack, qkv_back, preferred_element_type=jnp.float32)
    norm_parts = jnp.tile(
        jnp.stack([gain_one_part, shift_one_part, gain_two_part, shift_two_part]),
        (lax.axis_size("tensor"), 1),
    )
    input_share, norm_sums = (
        lax.psum_scatter(
            input_part.astype(jnp.bfloat16), "tensor", scatter_dimension=0, tiled=True
        ).astype(jnp.float32),
        lax.psum_scatter(
            norm_parts.astype(jnp.bfloat16), "tensor", scatter_dimension=0, tiled=True
        ).astype(jnp.float32),
    )
    grad_share_low = (grad_in_one + input_share).astype(jnp.bfloat16)
    out_rows, grad_rows = (
        lax.all_gather(output_share.astype(jnp.bfloat16), "tensor", axis=0, tiled=True),
        lax.all_gather(grad_share_low, "tensor", axis=0, tiled=True),
    )
    local_grads = (
        grad_qkv,
        grad_qv_bias,
        grad_proj,
        grad_proj_bias,
        norm_sums[0],
        norm_sums[1],
        grad_up,
        grad_up_bias,
        grad_down,
        grad_down_bias,
        norm_sums[2],
        norm_sums[3],
    )
    summed = (
        lax.psum(local_grads[0].astype(jnp.bfloat16), "context").astype(jnp.float32),
        lax.psum(local_grads[1].astype(jnp.bfloat16), "context").astype(jnp.float32),
        lax.psum(local_grads[2].astype(jnp.bfloat16), "context").astype(jnp.float32),
        lax.psum(local_grads[3].astype(jnp.bfloat16), "context").astype(jnp.float32),
        lax.psum(local_grads[4].astype(jnp.bfloat16), "context").astype(jnp.float32),
        lax.psum(local_grads[5].astype(jnp.bfloat16), "context").astype(jnp.float32),
        lax.psum(local_grads[6].astype(jnp.bfloat16), "context").astype(jnp.float32),
        lax.psum(local_grads[7].astype(jnp.bfloat16), "context").astype(jnp.float32),
        lax.psum(local_grads[8].astype(jnp.bfloat16), "context").astype(jnp.float32),
        lax.psum(local_grads[9].astype(jnp.bfloat16), "context").astype(jnp.float32),
        lax.psum(local_grads[10].astype(jnp.bfloat16), "context").astype(jnp.float32),
        lax.psum(local_grads[11].astype(jnp.bfloat16), "context").astype(jnp.float32),
    )
    owned = (
        lax.psum_scatter(
            summed[0].astype(jnp.bfloat16), "fsdp", scatter_dimension=1, tiled=True
        ).astype(jnp.float32),
        lax.psum_scatter(
            summed[1].astype(jnp.bfloat16), "fsdp", scatter_dimension=2, tiled=True
        ).astype(jnp.float32),
        lax.psum_scatter(
            summed[2].astype(jnp.bfloat16), "fsdp", scatter_dimension=1, tiled=True
        ).astype(jnp.float32),
        lax.psum_scatter(
            summed[3].astype(jnp.bfloat16), "fsdp", scatter_dimension=0, tiled=True
        ).astype(jnp.float32),
        lax.psum_scatter(
            summed[4].astype(jnp.bfloat16), "fsdp", scatter_dimension=0, tiled=True
        ).astype(jnp.float32),
        lax.psum_scatter(
            summed[5].astype(jnp.bfloat16), "fsdp", scatter_dimension=0, tiled=True
        ).astype(jnp.float32),
        lax.psum_scatter(
            summed[6].astype(jnp.bfloat16), "fsdp", scatter_dimension=0, tiled=True
        ).astype(jnp.float32),
        lax.psum_scatter(
            summed[7].astype(jnp.bfloat16), "fsdp", scatter_dimension=1, tiled=True
        ).astype(jnp.float32),
        lax.psum_scatter(
            summed[8].astype(jnp.bfloat16), "fsdp", scatter_dimension=1, tiled=True
        ).astype(jnp.float32),
        lax.psum_scatter(
            summed[9].astype(jnp.bfloat16), "fsdp", scatter_dimension=0, tiled=True
        ).astype(jnp.float32),
        lax.psum_scatter(
            summed[10].astype(jnp.bfloat16), "fsdp", scatter_dimension=0, tiled=True
        ).astype(jnp.float32),
        lax.psum_scatter(
            summed[11].astype(jnp.bfloat16), "fsdp", scatter_dimension=0, tiled=True
        ).astype(jnp.float32),
    )
    layer_output = out_rows.reshape(seq_count, span, width)
    tokens_grad = grad_rows.reshape(seq_count, span, width)
    return (
        layer_output,
        tokens_grad,
        owned[0],
        owned[1],
        owned[2],
        owned[3],
        owned[4],
        owned[5],
        owned[6],
        owned[7],
        owned[8],
        owned[9],
        owned[10],
        owned[11],
    )


def solution(mesh):
    return jax.shard_map(
        on_device,
        mesh=mesh,
        in_specs=(
            P("fsdp", "context", None),
            P("fsdp", "context"),
            P(None, "fsdp", "tensor"),
            P(None, "tensor", "fsdp"),
            P("tensor", "fsdp"),
            P("fsdp"),
            P("fsdp"),
            P("fsdp"),
            P("fsdp", "tensor"),
            P("tensor", "fsdp"),
            P("tensor", "fsdp"),
            P("fsdp"),
            P("fsdp"),
            P("fsdp"),
            P("fsdp", "context", None),
        ),
        out_specs=(
            P("fsdp", "context", None),
            P("fsdp", "context", None),
            P(None, "fsdp", "tensor"),
            P(None, "tensor", "fsdp"),
            P("tensor", "fsdp"),
            P("fsdp"),
            P("fsdp"),
            P("fsdp"),
            P("fsdp", "tensor"),
            P("tensor", "fsdp"),
            P("tensor", "fsdp"),
            P("fsdp"),
            P("fsdp"),
            P("fsdp"),
        ),
        check_vma=False,
    )
```

profile of v0, /device:TPU:28, one launch (start us, length us, event | category | flops | bytes accessed | tf_op | source)
XLA Modules:
  0.0 1935.7 jit_solution(8706955827385667597)
XLA Ops:
  9.2 38.4 %all-gather.18.cloned.1.call-done = bf16[3,1024,512]{1,2,0:T(8,128)(2,1)} async-done(((bf16[3,128,512]{1,2,0:T(8,128)(2,1)}), bf16[3,1024,512]{1,2,0:T(8,128)(2,1)}) %all-gather.18.cloned.1.call-update) | async-done | bytes 3145744 | tf_op jit(solution)/shard_map/all_gather | solution.py:52
  126.6 58.3 %all-gather.20.cloned.1.call-done = bf16[2,2048,8,64]{1,3,2,0:T(8,128)(2,1)} async-done(((bf16[2,1024,8,64]{1,3,2,0:T(8,128)(2,1)}), bf16[2,2048,8,64]{1,3,2,0:T(8,128)(2,1)}) %all-gather.20.cloned.1.call-update) | async-done | bytes 4194320 | tf_op jit(solution)/shard_map/all_gather | solution.py:93
  186.6 156.6 %while.26 = (s32[]{:T(128)}, bf16[2,1024,8,64]{1,3,2,0:T(8,128)(2,1)}, f32[2,8,1024,1]{2,1,3,0:T(8,128)}, bf16[2,2048,8,64]{1,3,2,0:T(8,128)(2,1)}, s32[2,1024]{...) while((s32[]{:T(128)}, ...), condition=%wide.region_3.4_spmd, body=%wide.region_0.3_spmd.sunk | while | flops 4498907136 | bytes 216307824 | solution.py:109
  383.2 70.6 %reduce-scatter.19.cloned.1.call-done = f32[1024,1024]{1,0:T(8,128)} async-done(((f32[2048,1024]{1,0:T(8,128)}), f32[1024,1024]{1,0:T(8,128)}) %reduce-scatter.19.cloned.1.call-update) | async-done | bytes 4194320 | tf_op jit(solution)/shard_map/reduce_scatter | solution.py:114
  474.0 27.3 %all-gather.28.cloned.1.call-done = bf16[1024,2048]{1,0:T(8,128)(2,1)} async-done(((bf16[128,2048]{1,0:T(8,128)(2,1)}), bf16[1024,2048]{1,0:T(8,128)(2,1)}) %all-gather.28.cloned.1.call-update) | async-done | bytes 4194320 | tf_op jit(solution)/shard_map/all_gather | solution.py:58
  501.3 59.0 %all-gather.26.cloned.1.call-done = bf16[2048,1024]{1,0:T(8,128)(2,1)} async-done(((bf16[1024,1024]{1,0:T(8,128)(2,1)}), bf16[2048,1024]{1,0:T(8,128)(2,1)}) %all-gather.26.cloned.1.call-update) | async-done | bytes 4194320 | tf_op jit(solution)/shard_map/all_gather | solution.py:124
  560.3 49.4 %multiply_convert_fusion.2 = (bf16[2048,2048]{1,0:T(8,128)(2,1)}, f32[2048,2048]{1,0:T(8,128)}, f32[2048,2048]{1,0:T(8,128)}) fusion(f32[2048]{0:T(1024)S(1)} %reshape.260, bf16[2048,1024]{1,0:T(8,128)(2,1)} %all-gather.26.cloned.1.call-done, bf16[1024,2048]{1,0:T(8,128)(2,1)} %all-gather.28.cloned.1.call-done), kind=kOutput, calls=%fused_computation.66 | convolution fusion | flops 8866758656 | bytes 50339840 | tf_op jit(solution)/shard_map/dot_general | solution.py:125
  652.0 71.5 %reduce-scatter.21.cloned.1.call-done = f32[1024,1024]{1,0:T(8,128)} async-done(((f32[2048,1024]{1,0:T(8,128)}), f32[1024,1024]{1,0:T(8,128)}) %reduce-scatter.21.cloned.1.call-update) | async-done | bytes 4194320 | tf_op jit(solution)/shard_map/reduce_scatter | solution.py:131
  739.9 56.9 %all-gather.34.cloned.1.call-done = bf16[2048,1024]{1,0:T(8,128)(2,1)} async-done(((bf16[1024,1024]{1,0:T(8,128)(2,1)}), bf16[2048,1024]{1,0:T(8,128)(2,1)}) %all-gather.34.cloned.1.call-update) | async-done | bytes 4194320 | tf_op jit(solution)/shard_map/all_gather | solution.py:150
  834.8 99.3 %reduce-scatter.23.cloned.1.call-done = f32[1024,1024]{1,0:T(8,128)} async-done(((f32[2048,1024]{1,0:T(8,128)}), f32[1024,1024]{1,0:T(8,128)}) %reduce-scatter.23.cloned.1.call-update) | async-done | bytes 4194320 | tf_op jit(solution)/shard_map/reduce_scatter | solution.py:158
  946.0 56.8 %all-gather.36.cloned.1.call-done = bf16[2048,1024]{1,0:T(8,128)(2,1)} async-done(((bf16[1024,1024]{1,0:T(8,128)(2,1)}), bf16[2048,1024]{1,0:T(8,128)(2,1)}) %all-gather.36.cloned.1.call-update) | async-done | bytes 4194320 | tf_op jit(solution)/shard_map/all_gather | solution.py:162
  1018.2 385.2 %while.27 = (s32[]{:T(128)}, bf16[2,1024,8,64]{1,3,2,0:T(8,128)(2,1)}, bf16[2,2048,8,64]{1,3,2,0:T(8,128)(2,1)}, bf16[2,2048,8,64]{1,3,2,0:T(8,128)(2,1)}, bf16[...) while((s32[]{:T(128)}, ...), condition=%wide.region_17.18_spmd, body=%wide.region_15.17_spmd.sunk | while | flops 10993262592 | bytes 540288128 | solution.py:196
  1046.8 27.4 %bitcast_dynamic-update-slice_fusion.8 = bf16[2,2048,8,64]{1,3,2,0:T(8,128)(2,1)} fusion(bf16[2,2048,8,64]{1,3,2,0:T(8,128)(2,1)} %get-tuple-element.504, s32[]{:T(128)S(6)} %copy.167, f32[8,1024,2048]{2,1,0:T(8,128)} %fusion.140, f32[8,1024]{1,0:T(8,128)S(1)} %dynamic-slice_bitcast_fusion.2, pred[1024,2048]{1,0:T(8,128)(4,1)S(1)} %broadcast_compare_fusion.5, ...), kind=kOutput, calls=%fused_computation.30.clone.1 | convolution fusion | flops 2214592512 | bytes 74482688 | tf_op jit(solution)/shard_map/while/body/eval_jaxpr/hqk,qhe->khe/dot_general | solution.py:188
  1074.2 50.7 %multiply_reduce_fusion.6 = (f32[8,1024]{1,0:T(8,128)S(1)}, f32[8,1024,2048]{2,1,0:T(8,128)}) fusion(f32[8,1024,2048]{2,1,0:T(8,128)} %fusion.140, f32[8,1024]{1,0:T(8,128)S(1)} %dynamic-slice_bitcast_fusion.2, pred[1024,2048]{1,0:T(8,128)(4,1)S(1)} %broadcast_compare_fusion.5, bf16[2,2048,8,64]{1,3,2,0:T(8,128)(2,1)} %get-tuple-element.523, ...), kind=kOutput, calls=%fused_computation.25.clone.3 | convolution fusion | flops 2231361536 | bytes 139527168 | tf_op jit(solution)/shard_map/while/body/eval_jaxpr/qhe,khe->hqk/dot_general | solution.py:175
  1124.9 52.9 %multiply_convert_fusion.4 = bf16[8,1024,2048]{2,1,0:T(8,128)(2,1)} fusion(f32[8,1024,2048]{2,1,0:T(8,128)} %get-tuple-element.460, f32[8,1024,2048]{2,1,0:T(8,128)} %fusion.140, f32[8,1024]{1,0:T(8,128)S(1)} %get-tuple-element.461, f32[8,1024]{1,0:T(8,128)S(1)} %dynamic-slice_bitcast_fusion.2, pred[1024,2048]{1,0:T(8,128)(4,1)S(1)} %broadcast_compare_fusion.5), kind=kLoop, calls=%fused_computation.24.clone.1 | loop fusion | flops 100663296 | bytes 169934848 | tf_op jit(solution)/shard_map/while/body/eval_jaxpr/convert_element_type | solution.py:179
  1239.1 27.3 %bitcast_dynamic-update-slice_fusion.8 = bf16[2,2048,8,64]{1,3,2,0:T(8,128)(2,1)} fusion(bf16[2,2048,8,64]{1,3,2,0:T(8,128)(2,1)} %get-tuple-element.504, s32[]{:T(128)S(6)} %copy.167, f32[8,1024,2048]{2,1,0:T(8,128)} %fusion.140, f32[8,1024]{1,0:T(8,128)S(1)} %dynamic-slice_bitcast_fusion.2, pred[1024,2048]{1,0:T(8,128)(4,1)S(1)} %broadcast_compare_fusion.5, ...), kind=kOutput, calls=%fused_computation.30.clone.1 | convolution fusion | flops 2214592512 | bytes 74482688 | tf_op jit(solution)/shard_map/while/body/eval_jaxpr/hqk,qhe->khe/dot_general | solution.py:188
  1266.4 50.8 %multiply_reduce_fusion.6 = (f32[8,1024]{1,0:T(8,128)S(1)}, f32[8,1024,2048]{2,1,0:T(8,128)}) fusion(f32[8,1024,2048]{2,1,0:T(8,128)} %fusion.140, f32[8,1024]{1,0:T(8,128)S(1)} %dynamic-slice_bitcast_fusion.2, pred[1024,2048]{1,0:T(8,128)(4,1)S(1)} %broadcast_compare_fusion.5, bf16[2,2048,8,64]{1,3,2,0:T(8,128)(2,1)} %get-tuple-element.523, ...), kind=kOutput, calls=%fused_computation.25.clone.3 | convolution fusion | flops 2231361536 | bytes 139527168 | tf_op jit(solution)/shard_map/while/body/eval_jaxpr/qhe,khe->hqk/dot_general | solution.py:175
  1317.2 52.9 %multiply_convert_fusion.4 = bf16[8,1024,2048]{2,1,0:T(8,128)(2,1)} fusion(f32[8,1024,2048]{2,1,0:T(8,128)} %get-tuple-element.460, f32[8,1024,2048]{2,1,0:T(8,128)} %fusion.140, f32[8,1024]{1,0:T(8,128)S(1)} %get-tuple-element.461, f32[8,1024]{1,0:T(8,128)S(1)} %dynamic-slice_bitcast_fusion.2, pred[1024,2048]{1,0:T(8,128)(4,1)S(1)} %broadcast_compare_fusion.5), kind=kLoop, calls=%fused_computation.24.clone.1 | loop fusion | flops 100663296 | bytes 169934848 | tf_op jit(solution)/shard_map/while/body/eval_jaxpr/convert_element_type | solution.py:179
  1469.8 46.0 %reduce-scatter.27.cloned.1.call-done = bf16[2,1024,8,64]{1,3,2,0:T(8,128)(2,1)} async-done(((bf16[2,2048,8,64]{1,3,2,0:T(8,128)(2,1)}), bf16[2,1024,8,64]{1,3,2,0:T(8,128)(2,1)}) %reduce-scatter.27.cloned.1.call-update) | async-done | bytes 2097168 | tf_op jit(solution)/shard_map/reduce_scatter | solution.py:204
  1599.2 39.8 %reduce-scatter.33.cloned.1.call-done = bf16[128,1536]{1,0:T(8,128)(2,1)} async-done(((bf16[1024,1536]{1,0:T(8,128)(2,1)}), bf16[128,1536]{1,0:T(8,128)(2,1)}) %reduce-scatter.33.cloned.1.call-update) | async-done | bytes 393232
  1641.8 49.0 %reduce-scatter.31.cloned.1.call-done = bf16[128,2048]{1,0:T(8,128)(2,1)} async-done(((bf16[1024,2048]{1,0:T(8,128)(2,1)}), bf16[128,2048]{1,0:T(8,128)(2,1)}) %reduce-scatter.31.cloned.1.call-update) | async-done | bytes 524304 | tf_op jit(solution)/shard_map/reduce_scatter | solution.py:283
  1690.9 57.8 %reduce-scatter.29.cloned.1.call-done = bf16[1024,1024]{1,0:T(8,128)(2,1)} async-done(((bf16[2048,1024]{1,0:T(8,128)(2,1)}), bf16[1024,1024]{1,0:T(8,128)(2,1)}) %reduce-scatter.29.cloned.1.call-update) | async-done | bytes 2097168 | tf_op jit(solution)/shard_map/reduce_scatter | solution.py:224
  1758.8 48.0 %all-gather.32.cloned.1.call-done = bf16[2048,1024]{1,0:T(8,128)(2,1)} async-done(((bf16[1024,1024]{1,0:T(8,128)(2,1)}), bf16[2048,1024]{1,0:T(8,128)(2,1)}) %all-gather.32.cloned.1.call-update) | async-done | bytes 4194320 | tf_op jit(solution)/shard_map/all_gather | solution.py:233
  1871.7 50.2 %all-gather.38.cloned.1.call-done = bf16[2048,1024]{1,0:T(8,128)(2,1)} async-done(((bf16[1024,1024]{1,0:T(8,128)(2,1)}), bf16[2048,1024]{1,0:T(8,128)(2,1)}) %all-gather.38.cloned.1.call-update) | async-done | bytes 4194320 | tf_op jit(solution)/shard_map/all_gather | solution.py:234
  (275 shorter events, 777.5 us)
Async XLA Ops:
  7.2 40.4 %all-gather.18.cloned.1.call-start = ((), (), s32[]{:S(2)}) async-start(), calls=%async_computation.10 | async-start | bytes 3538944 | tf_op jit(solution)/shard_map/all_gather | solution.py:52
  9.2 117.5 %all-gather.22.cloned.1.call-start = ((), (), s32[]{:S(2)}) async-start(), calls=%async_computation.12 | async-start | bytes 6291456 | tf_op jit(solution)/shard_map/all_gather | solution.py:92
  68.6 116.4 %all-gather.20.cloned.1.call-start = ((), (), s32[]{:S(2)}) async-start(), calls=%async_computation.11 | async-start | bytes 6291456 | tf_op jit(solution)/shard_map/all_gather | solution.py:93
  102.3 245.3 %all-gather.24.cloned.1.call-start = ((), (), s32[]{:S(2)}) async-start(), calls=%async_computation.13 | async-start | bytes 1179648 | tf_op jit(solution)/shard_map/all_gather | solution.py:54
  102.8 350.9 %reduce-scatter.19.cloned.1.call-start = ((), (), s32[]{:S(2)}) async-start(), calls=%async_computation.14 | async-start | bytes 12582912 | tf_op jit(solution)/shard_map/reduce_scatter | solution.py:114
  355.2 146.1 %all-gather.28.cloned.1.call-start = ((), (), s32[]{:S(2)}) async-start(), calls=%async_computation.16 | async-start | bytes 4718592 | tf_op jit(solution)/shard_map/all_gather | solution.py:58
  355.8 204.5 %all-gather.26.cloned.1.call-start = ((), (), s32[]{:S(2)}) async-start(), calls=%async_computation.15 | async-start | bytes 6291456 | tf_op jit(solution)/shard_map/all_gather | solution.py:124
  461.3 148.3 %all-gather.30.cloned.1.call-start = ((), (), s32[]{:S(2)}) async-start(), calls=%async_computation.17 | async-start | bytes 4718592 | tf_op jit(solution)/shard_map/all_gather | solution.py:60
  462.1 261.4 %reduce-scatter.21.cloned.1.call-start = ((), (), s32[]{:S(2)}) async-start(), calls=%async_computation.18 | async-start | bytes 12582912 | tf_op jit(solution)/shard_map/reduce_scatter | solution.py:131
  624.1 172.7 %all-gather.34.cloned.1.call-start = ((), (), s32[]{:S(2)}) async-start(), calls=%async_computation.20 | async-start | bytes 6291456 | tf_op jit(solution)/shard_map/all_gather | solution.py:150
  739.8 194.3 %reduce-scatter.23.cloned.1.call-start = ((), (), s32[]{:S(2)}) async-start(), calls=%async_computation.21 | async-start | bytes 12582912 | tf_op jit(solution)/shard_map/reduce_scatter | solution.py:158
  834.7 105.8 %copy-start.15 = (f32[1024]{0:T(1024)S(1)}, f32[1024]{0:T(1024)}, u32[]{:S(2)}) copy-start(f32[1024]{0:T(1024)} %copy-done.14) | copy-start | bytes 12292
  834.8 168.1 %all-gather.36.cloned.1.call-start = ((), (), s32[]{:S(2)}) async-start(), calls=%async_computation.22 | async-start | bytes 6291456 | tf_op jit(solution)/shard_map/all_gather | solution.py:162
  945.9 512.8 %reduce-scatter.25.cloned.1.call-start = ((), (), s32[]{:S(2)}) async-start(), calls=%async_computation.23 | async-start | bytes 6291456 | tf_op jit(solution)/shard_map/reduce_scatter | solution.py:201
  1403.3 112.4 %reduce-scatter.27.cloned.1.call-start = ((), (), s32[]{:S(2)}) async-start(), calls=%async_computation.24 | async-start | bytes 6291456 | tf_op jit(solution)/shard_map/reduce_scatter | solution.py:204
  1403.9 175.4 %reduce-scatter.37.cloned.1.call-start = ((), (), s32[]{:S(2)}) async-start(), calls=%async_computation.30 | async-start | bytes 4718592
  1424.5 173.1 %reduce-scatter.35.cloned.1.call-start = ((), (), s32[]{:S(2)}) async-start(), calls=%async_computation.29 | async-start | bytes 1179648
  1441.1 198.0 %reduce-scatter.33.cloned.1.call-start = ((), (), s32[]{:S(2)}) async-start(), calls=%async_computation.28 | async-start | bytes 3538944
  1551.6 139.2 %reduce-scatter.31.cloned.1.call-start = ((), (), s32[]{:S(2)}) async-start(), calls=%async_computation.27 | async-start | bytes 4718592 | tf_op jit(solution)/shard_map/reduce_scatter | solution.py:283
  1565.8 182.9 %reduce-scatter.29.cloned.1.call-start = ((), (), s32[]{:S(2)}) async-start(), calls=%async_computation.25 | async-start | bytes 6291456 | tf_op jit(solution)/shard_map/reduce_scatter | solution.py:224
  1578.7 170.0 %copy-start.13 = (f32[1024]{0:T(1024)S(1)}, f32[1024]{0:T(1024)}, u32[]{:S(2)}) copy-start(f32[1024]{0:T(1024)} %copy-done.12) | copy-start | bytes 12292
  1578.7 228.2 %all-gather.32.cloned.1.call-start = ((), (), s32[]{:S(2)}) async-start(), calls=%async_computation.19 | async-start | bytes 6291456 | tf_op jit(solution)/shard_map/all_gather | solution.py:233
  1579.3 284.5 %all-reduce.14.cloned.1.call-start = ((), (), s32[]{:S(2)}) async-start(), calls=%async_computation.31 | async-start | bytes 3145728 | tf_op jit(solution)/shard_map/psum | solution.py:251
  1690.9 231.0 %all-gather.38.cloned.1.call-start = ((), (), s32[]{:S(2)}) async-start(), calls=%async_computation.26 | async-start | bytes 6291456 | tf_op jit(solution)/shard_map/all_gather | solution.py:234
  (31 other events, 506.5 us)
Sparse Core Ops, SparseCore 0:
  10.2 37.3 all-gather.17
  68.7 57.8 all-gather.21
  128.2 56.7 all-gather.19
  186.4 21.6 all-gather.23
  355.4 98.3 reduce-scatter.18
  455.3 45.9 all-gather.27
  503.5 56.7 all-gather.25
  561.9 45.9 all-gather.29
  624.2 99.2 reduce-scatter.20
  740.0 56.7 all-gather.33
  834.9 99.2 reduce-scatter.22
  946.1 56.7 all-gather.35
  1403.5 55.1 reduce-scatter.24
  1461.4 54.3 reduce-scatter.26
  1518.0 46.6 reduce-scatter.36
  1567.5 29.9 reduce-scatter.34
  1599.8 39.1 reduce-scatter.32
  1641.9 48.8 reduce-scatter.30
  1693.8 54.8 reduce-scatter.28
  1750.0 56.7 all-gather.31
  1810.4 53.3 all-reduce.13
  1866.0 55.8 all-gather.37
where the time goes:
time: 1950 us; the launch traced here: 1940 us
  waiting for transfers between devices  875 us (45%)
  matrix products  554 us (28%)
  other arithmetic  220 us (11%)
  local copies, waits for them, and re-layouts  143 us (7%)
  blocking collectives  124 us (6%)
    convert_element_type x2, other arithmetic, attend_backward(): grad_logits = (soft_again * (grad_soft - row_delta)).astype(jnp.bfloat16)  106 us
    dot_general x2, matrix products, attend_backward(): jnp.einsum('qhe,khe->hqk', context_grad, value_one, preferred_element_typ...  101 us
    dot_general x4, matrix products, masked_logits(): jnp.einsum('qhe,khe->hqk', query_heads, key_heads, preferred_element_type...  101 us
    reduce_scatter x1, waiting for transfers between devices, on_device(): lax.psum_scatter(norm_part, 'tensor', scatter_dimension=0, tiled=True)  99.3 us
    reduce_scatter x1, waiting for transfers between devices, on_device(): lax.psum_scatter(down_part, 'tensor', scatter_dimension=0, tiled=True)  71.5 us
    reduce_scatter x1, waiting for transfers between devices, on_device(): lax.psum_scatter(attn_part, 'tensor', scatter_dimension=0, tiled=True)  70.6 us
    unnamed x25, waiting for transfers between devices  59.1 us
    all_gather x1, waiting for transfers between devices, on_device(): lax.all_gather(first_share.astype(jnp.bfloat16), 'tensor', axis=0, tiled=...  59 us
  transfers between devices with their start and end apart: 22, of which 19 were waited for; matrix products, arithmetic and copies ran while one was open for 20% of the time, Pallas kernels for 0%

commit v1 on v0

--- a/solution.py
+++ b/solution.py
@@ -1,6 +1,10 @@
+import functools
+
 import jax
 import jax.numpy as jnp
 from jax import lax
+from jax.experimental import pallas as pl
+from jax.experimental.pallas import tpu as pltpu
 from jax.sharding import PartitionSpec as P
 
 NORM_EPS = 1e-05
@@ -26,7 +30,7 @@
     return jnp.where(same_doc, logits, -1e30)
 
 
-def on_device(
+def on_device_general(
     tokens,
     segment_ids,
     qkv_weight,
@@ -319,42 +323,675 @@
     )
 
 
+AXES = ("z", "core", "context", "tensor")
+BF = jnp.bfloat16
+F32 = jnp.float32
+SUB = 2
+MASKED = -1e30
+NT = (((1,), (1,)), ((), ()))
+NN = (((1,), (0,)), ((), ()))
+
+def _dot(a, b, dims):
+    return lax.dot_general(a, b, dims, preferred_element_type=jnp.float32)
+
+def attn_fwd_kernel(lo_ref, hi_ref, shift_ref, q_ref, k_ref, v_ref, segk_ref, segq_ref, o_ref, lse_ref, vt_ref, *, bq, bk, hd, scale, nblk):
+    qb = pl.program_id(0)
+    shift = shift_ref[0]
+    pair = q_ref.shape[1]
+    heads = pair // hd
+
+    @pl.when(qb == 0)
+    def _():
+        for j in range(nblk):
+            vt_ref[j] = v_ref[j * bk:(j + 1) * bk, :].T
+
+    gq = lax.rem(qb + shift // (bq // bk), nblk * bk // bq)
+    lane = lax.broadcasted_iota(jnp.int32, (bq, pair), 1) // hd
+    q = q_ref[...] * jnp.asarray(scale, q_ref.dtype)
+    qs = [jnp.where(lane == h, q, jnp.zeros_like(q)) for h in range(heads)]
+    segq = segq_ref[0:1, :]
+
+    def body(i, carry):
+        j = lo_ref[gq] + i * SUB
+        sbs = [lax.rem(j + u + shift, nblk) for u in range(SUB)]
+        sc = [[None] * SUB for _ in range(heads)]
+        for u in range(SUB):
+            ks = pl.multiple_of(sbs[u] * bk, bk)
+            kb = k_ref[pl.ds(ks, bk), :]
+            same = segk_ref[pl.ds(ks, bk), :]
+            same = jnp.concatenate([same] * (bq // same.shape[1]), axis=1) == segq
+            for h in range(heads):
+                sc[h][u] = jnp.where(same, _dot(kb, qs[h], NT), MASKED)
+        out = []
+        for h in range(heads):
+            m, l, acc = carry[h]
+            mn = m
+            for u in range(SUB):
+                mn = jnp.maximum(mn, jnp.max(sc[h][u], axis=0, keepdims=True))
+            a = jnp.exp(m - mn)
+            l = l * a
+            acc = acc * a
+            for u in range(SUB):
+                p = jnp.exp(sc[h][u] - mn)
+                l = l + jnp.sum(p, axis=0, keepdims=True)
+                acc = acc + _dot(vt_ref[sbs[u], h * hd:(h + 1) * hd, :], p.astype(jnp.bfloat16), NN)
+            out.append((mn, l, acc))
+        return tuple(out)
+
+    init = tuple((jnp.full((1, bq), MASKED, jnp.float32), jnp.zeros((1, bq), jnp.float32), jnp.zeros((hd, bq), jnp.float32)) for _ in range(heads))
+    res = lax.fori_loop(0, (hi_ref[gq] - lo_ref[gq] + SUB - 1) // SUB, body, init)
+    o_ref[...] = jnp.concatenate([acc / l for (m, l, acc) in res], axis=0).T.astype(o_ref.dtype)
+    lse_ref[0] = jnp.concatenate([m + jnp.log(l) for (m, l, acc) in res], axis=0)
+
+def attn_bwd_kernel(lo_ref, hi_ref, shift_ref, q_ref, k_ref, v_ref, o_ref, do_ref, lse_ref, segk_ref, segq_ref, out_ref,
+                    qs_ref, dos_ref, kt_ref, delta_ref, dqt_ref, dk_ref, dv_ref, *, bq, bk, hd, scale, nblk):
+    w = pl.program_id(0)
+    shift = shift_ref[0]
+    rows, pair = q_ref.shape
+    heads = pair // hd
+
+    @pl.when(w == 0)
+    def _():
+        lane = lax.broadcasted_iota(jnp.int32, (bk, pair), 1) // hd
+        pick = (lax.broadcasted_iota(jnp.int32, (8, pair), 0) == lax.broadcasted_iota(jnp.int32, (8, pair), 1) // hd).astype(jnp.float32)
+        sc = jnp.asarray(scale, q_ref.dtype)
+        for j in range(nblk):
+            r = slice(j * bk, (j + 1) * bk)
+            q = q_ref[r, :] * sc
+            do = do_ref[r, :]
+            for h in range(heads):
+                qs_ref[h, r, :] = jnp.where(lane == h, q, jnp.zeros_like(q))
+                dos_ref[h, r, :] = jnp.where(lane == h, do, jnp.zeros_like(do))
+            kt_ref[j] = (k_ref[r, :] * sc).T
+            prod = do.astype(jnp.float32) * o_ref[r, :].astype(jnp.float32)
+            delta_ref[:, r] = lax.dot_general(pick, prod, NT, preferred_element_type=jnp.float32, precision=lax.Precision.HIGHEST)
+
+
+        dqt_ref[...] = jnp.zeros(dqt_ref.shape, jnp.float32)
+
+        def outer(kb, _):
+            gk = lax.rem(kb + shift, nblk)
+            nq = nblk * bk // bq
+            ks = pl.multiple_of(kb * bk, bk)
+            kblk = k_ref[pl.ds(ks, bk), :]
+            vblk = v_ref[pl.ds(ks, bk), :]
+            segk = segk_ref[pl.ds(ks, bk), :]
+            segk = jnp.concatenate([segk] * (bq // segk.shape[1]), axis=1)
+
+            def inner(j, carry):
+                dk, dv = carry
+                sb = lax.rem(j + shift // (bq // bk) if bq >= bk else j + shift * (bk // bq), nq)
+                qo = pl.multiple_of(sb * bq, bq)
+                same = segk == segq_ref[0:1, pl.ds(qo, bq)]
+                qh = [qs_ref[h, pl.ds(qo, bq), :] for h in range(heads)]
+                doh = [dos_ref[h, pl.ds(qo, bq), :] for h in range(heads)]
+                s = [_dot(kblk, qh[h], NT) for h in range(heads)]
+                dp = [_dot(vblk, doh[h], NT) for h in range(heads)]
+                p = [jnp.exp(jnp.where(same, s[h] - lse_ref[0, h:h + 1, pl.ds(qo, bq)], MASKED)) for h in range(heads)]
+                pb = [p[h].astype(jnp.bfloat16) for h in range(heads)]
+                ds = [(p[h] * (dp[h] - delta_ref[h:h + 1, pl.ds(qo, bq)])).astype(jnp.bfloat16) for h in range(heads)]
+                for h in range(heads):
+                    hs = slice(h * hd, (h + 1) * hd)
+                    dv = dv + _dot(pb[h], doh[h], NN)
+                    dk = dk + _dot(ds[h], qh[h], NN)
+                    dqt_ref[sb, hs, :] += _dot(kt_ref[kb, hs, :], ds[h], NN)
+                return dk, dv
+
+            zero = jnp.zeros((bk, pair), jnp.float32)
+            dk, dv = lax.fori_loop(lo_ref[gk], hi_ref[gk], inner, (zero, zero))
+            dk_ref[pl.ds(ks, bk), :] = dk.astype(jnp.bfloat16)
+            dv_ref[pl.ds(ks, bk), :] = dv.astype(jnp.bfloat16)
+            return 0
+
+        lax.fori_loop(0, nblk, outer, 0)
+        for j in range(nblk * bk // bq):
+            out_ref[j * bq:(j + 1) * bq, :] = dqt_ref[j].T.astype(out_ref.dtype)
+
+    @pl.when(w == 1)
+    def _():
+        out_ref[...] = dk_ref[...]
+
+    @pl.when(w == 2)
+    def _():
+        out_ref[...] = dv_ref[...]
+
+def pair_block(which, pair, group):
+    return (pair // group) * 3 * group + which * group + pair % group
+
+
+def attn_fwd(qkv, seg_k, seg_q, low, high, shift, pair, pairs, group, head_size, bq, bk):
+    rows, wide = qkv.shape[0], 2 * head_size
+    blocks = rows // bk
+    spec = lambda which: pair_block(which, pair, group)
+    return pl.pallas_call(
+        functools.partial(attn_fwd_kernel, bq=bq, bk=bk, hd=head_size, scale=float(head_size) ** -0.5, nblk=blocks),
+        out_shape=(
+            jax.ShapeDtypeStruct((rows, wide), BF),
+            jax.ShapeDtypeStruct((1, 2, rows), F32),
+        ),
+        grid_spec=pltpu.PrefetchScalarGridSpec(
+            num_scalar_prefetch=3,
+            grid=(rows // bq,),
+            in_specs=[
+                pl.BlockSpec((bq, wide), lambda i, *_: (i, spec(0))),
+                pl.BlockSpec((rows, wide), lambda i, *_: (0, spec(1))),
+                pl.BlockSpec((rows, wide), lambda i, *_: (0, spec(2))),
+                pl.BlockSpec((rows, 128), lambda i, *_: (0, 0)),
+                pl.BlockSpec((8, bq), lambda i, *_: (0, i)),
+            ],
+            out_specs=(
+                pl.BlockSpec((bq, wide), lambda i, *_: (i, 0)),
+                pl.BlockSpec((1, 2, bq), lambda i, *_: (0, 0, i)),
+            ),
+            scratch_shapes=[pltpu.VMEM((blocks, wide, bk), BF)],
+        ),
+        compiler_params=pltpu.CompilerParams(vmem_limit_bytes=24 << 20),
+        cost_estimate=pl.CostEstimate(
+            flops=15_000_000_000, bytes_accessed=rows * wide * 8, transcendentals=rows * rows // 2
+        ),
+        name="attn_fwd",
+    )(low, high, shift, qkv, qkv, qkv, seg_k, seg_q)
+
+
+def attn_bwd(before, qkv, mixed, dctx, lse, seg_k, seg_q, low, high, shift, pair, pairs, group, head_size, bq, bk):
+    rows, wide = qkv.shape[0], 2 * head_size
+    blocks = rows // bk
+    column = lambda which: pl.BlockSpec((rows, wide), lambda w, *_: (0, pair_block(which, pair, group)))
+    in_specs = [
+        column(0),
+        column(1),
+        column(2),
+        pl.BlockSpec((rows, wide), lambda w, *_: (0, 0)),
+        pl.BlockSpec((rows, wide), lambda w, *_: (0, pair)),
+        pl.BlockSpec((1, 2, rows), lambda w, *_: (0, 0, 0)),
+        pl.BlockSpec((rows, 128), lambda w, *_: (0, 0)),
+        pl.BlockSpec((8, rows), lambda w, *_: (0, 0)),
+    ]
+    operands = [low, high, shift, qkv, qkv, qkv, mixed, dctx, lse, seg_k, seg_q]
+    aliases = {}
+    kernel = functools.partial(
+        attn_bwd_kernel, bq=bq, bk=bk, hd=head_size, scale=float(head_size) ** -0.5, nblk=blocks
+    )
+    body = kernel
+    if before is not None:
+        aliases = {len(operands): 0}
+        in_specs.append(pl.BlockSpec(memory_space=pl.ANY))
+        operands.append(before)
+
+        def body(*refs):
+            kernel(*refs[:11], *refs[12:])
+
+    return pl.pallas_call(
+        body,
+        out_shape=jax.ShapeDtypeStruct(qkv.shape, BF),
+        grid_spec=pltpu.PrefetchScalarGridSpec(
+            num_scalar_prefetch=3,
+            grid=(3,),
+            in_specs=in_specs,
+            out_specs=pl.BlockSpec((rows, wide), lambda w, *_: (0, (pair // group) * 3 * group + w * group + pair % group)),
+            scratch_shapes=[
+                pltpu.VMEM((2, rows, wide), BF),
+                pltpu.VMEM((2, rows, wide), BF),
+                pltpu.VMEM((blocks, wide, bk), BF),
+                pltpu.VMEM((8, rows), F32),
+                pltpu.VMEM((rows // bq, wide, bq), F32),
+                pltpu.VMEM((rows, wide), BF),
+                pltpu.VMEM((rows, wide), BF),
+            ],
+        ),
+        input_output_aliases=aliases,
+        compiler_params=pltpu.CompilerParams(vmem_limit_bytes=32 << 20),
+        cost_estimate=pl.CostEstimate(
+            flops=25_000_000_000, bytes_accessed=rows * wide * 16, transcendentals=rows * rows // 2
+        ),
+        name="attn_bwd",
+    )(*operands)
+
+
+def assemble_kernel(*refs, per, place):
+    stacks = len(refs) - 4
+    out, buf, in_sem, out_sem = refs[stacks:]
+    count = stacks * per
+    blocks = [refs[i // per].at[i % per] for i in range(count)]
+    for i in range(count):
+        pltpu.make_async_copy(blocks[i], buf.at[i], in_sem.at[i]).start()
+    outs = []
+    for i in range(count):
+        pltpu.make_async_copy(blocks[i], buf.at[i], in_sem.at[i]).wait()
+        outs.append(pltpu.make_async_copy(buf.at[i], place(out, i), out_sem.at[i]))
+        outs[-1].start()
+    for one in outs:
+        one.wait()
+
+
+def assemble(stacks, shape, place):
+    per = stacks[0].shape[0]
+    count = per * len(stacks)
+    return pl.pallas_call(
+        functools.partial(assemble_kernel, per=per, place=place),
+        out_shape=jax.ShapeDtypeStruct(shape, stacks[0].dtype),
+        in_specs=[pl.BlockSpec(memory_space=pl.ANY)] * len(stacks),
+        out_specs=pl.BlockSpec(memory_space=pl.ANY),
+        scratch_shapes=[
+            pltpu.VMEM((count,) + stacks[0].shape[1:], stacks[0].dtype),
+            pltpu.SemaphoreType.DMA((count,)),
+            pltpu.SemaphoreType.DMA((count,)),
+        ],
+        compiler_params=pltpu.CompilerParams(vmem_limit_bytes=32 << 20),
+        cost_estimate=pl.CostEstimate(flops=0, bytes_accessed=2 * 2 * shape[0] * shape[1], transcendentals=0),
+        name="assemble",
+    )(*stacks)
+
+
+def segment_bounds(seg_rows, row_block, col_block):
+    blocks = seg_rows.reshape(-1, row_block)
+    low = jnp.sum(seg_rows[None, :] < blocks[:, :1], axis=1) // col_block
+    high = (jnp.sum(seg_rows[None, :] <= blocks[:, -1:], axis=1) + col_block - 1) // col_block
+    return low.astype(jnp.int32), high.astype(jnp.int32)
+
+
+def norm_forward(rows):
+    mean = jnp.mean(rows, axis=-1, keepdims=True)
+    centred = rows - mean
+    inv = lax.rsqrt(jnp.mean(centred * centred, axis=-1, keepdims=True) + NORM_EPS)
+    return centred * inv, inv
+
+
+def norm_backward(grad, normed, inv):
+    return inv * (
+        grad
+        - jnp.mean(grad, axis=-1, keepdims=True)
+        - normed * jnp.mean(grad * normed, axis=-1, keepdims=True)
+    )
+
+
+def after(value, *others):
+    return lax.optimization_barrier((value,) + others)[0]
+
+
+def mm(a, b):
+    return jnp.dot(a, b, preferred_element_type=F32)
+
+
+def mm_nt(a, b):
+    return lax.dot_general(a, b, (((1,), (1,)), ((), ())), preferred_element_type=F32)
+
+
+def mm_tn(a, b):
+    return lax.dot_general(a, b, (((0,), (0,)), ((), ())), preferred_element_type=F32)
+
+
+def on_device_rows(
+    sizes,
+    tokens,
+    segment_ids,
+    qkv_weight,
+    qv_bias,
+    proj_weight,
+    proj_bias,
+    first_gain,
+    first_shift,
+    up_weight,
+    up_bias,
+    down_weight,
+    down_bias,
+    second_gain,
+    second_shift,
+    out_grad,
+):
+    nf, nc, nt = sizes
+    nz = nf // 2
+    zbits = nz.bit_length() - 1
+    z, k, c, t = (lax.axis_index(name) for name in AXES)
+    f = z * 2 + k
+
+    def send(value, target):
+        pairs = []
+        for fi in range(nf):
+            for ci in range(nc):
+                for ti in range(nt):
+                    to = target(fi // 2, fi % 2, ci, ti)
+                    if to is not None:
+                        zo, ko, co, tto = to
+                        pairs.append(((fi * nc + ci) * nt + ti, ((zo * 2 + ko) * nc + co) * nt + tto))
+        return lax.ppermute(value, AXES, pairs)
+
+    def over_x(v):
+        return send(v, lambda zi, ki, ci, ti: (zi, ki, 1 - ci, ti))
+
+    def over_y(v):
+        return send(v, lambda zi, ki, ci, ti: (zi, ki, ci, 1 - ti))
+
+    def over_core(v):
+        return send(v, lambda zi, ki, ci, ti: (zi, 1 - ki, ci, ti))
+
+    def over_z(v):
+        return send(v, lambda zi, ki, ci, ti: ((zi + 1) % nz, ki, ci, ti))
+
+    def over_zbit(v, bit):
+        return send(v, lambda zi, ki, ci, ti: (zi ^ (1 << bit), ki, ci, ti))
+
+    def z_all(v):
+        return [v] + [
+            send(v, lambda zi, ki, ci, ti, d=d: ((zi + d) % nz, ki, ci, ti)) for d in range(1, nz)
+        ]
+
+    def z_ring(v):
+        out = [v]
+        for _ in range(nz - 1):
+            out.append(over_z(out[-1]))
+        return out
+
+    def ordered(index, own, other, axis=0):
+        return jnp.where(index == 0, jnp.concatenate([own, other], axis), jnp.concatenate([other, own], axis))
+
+    seq_count, span, width = tokens.shape
+    heads = qv_bias.shape[1]
+    head_size = qv_bias.shape[2] * nf
+    cols = heads * head_size
+    hidden = up_weight.shape[1] * nt
+    dblk = width // nf
+
+    pairs = heads // 2
+    group = max(1, pairs // 2)
+    wide = 2 * head_size
+
+    pieces = [qv_bias, up_bias, proj_bias, first_gain, first_shift, down_bias, second_gain, second_shift]
+    small = jnp.concatenate([p.reshape(-1, 128) for p in pieces])
+    up_at, vec_at = qv_bias.size // 128, (qv_bias.size + up_bias.size) // 128
+    small = jnp.pad(small, ((0, -small.shape[0] % 16), (0, 0)))
+    small = lax.all_gather(small, AXES[:2] + AXES[3:])
+    small = small.reshape(nf, nt, -1, 128)
+
+    own_rows = jnp.where(t == 0, tokens[0], tokens[1])
+    own_seg = jnp.where(t == 0, segment_ids[0], segment_ids[1])
+    other_rows = over_x(own_rows)
+    other_seg = over_x(own_seg)
+    columns = []
+    for first in range(0, pairs, group):
+        for which in range(3):
+            columns.append(qkv_weight[which][:, first * wide : (first + group) * wide])
+    qkv_shard = jnp.concatenate(columns, axis=1)
+    swapped = send(qkv_shard, lambda zi, ki, ci, ti: (zi, ki, ci, 1 - ti) if ti == ci else None)
+    qkv_shard = jnp.where(t == c, qkv_shard, swapped)
+    qkv_near = z_all(qkv_shard)
+    qkv_blocks = qkv_near + [over_core(b) for b in qkv_near]
+
+    def place_rows(out, i):
+        kk, d = i // nz, i % nz
+        src = lax.rem(lax.axis_index("z") + nz - d, nz) * 2 + lax.rem(lax.axis_index("core") + kk, 2)
+        return out.at[pl.ds(pl.multiple_of(src * dblk, dblk), dblk), :]
+
+    qkv_full = assemble([b[None] for b in qkv_blocks], (width, 3 * cols), place_rows)
+
+    edge = head_size // nf
+
+    def interleave(rows, columns):
+        col = lax.broadcasted_iota(jnp.int32, (rows.shape[1], columns), 1)
+        source = lax.broadcasted_iota(jnp.int32, (rows.shape[1], columns), 0)
+        spread_out = mm(rows, (source == col // head_size * edge + col % edge).astype(BF))
+        col = lax.broadcasted_iota(jnp.int32, (nf, columns), 1)
+        mine = col % head_size // edge == lax.broadcasted_iota(jnp.int32, (nf, columns), 0)
+        return jnp.sum(jnp.where(mine, spread_out, 0.0), axis=0)
+
+    qv_rows = jnp.where(c == 0, small[:, 0, :up_at], small[:, 1, :up_at]).reshape(nf, -1)
+    per_kind = qv_rows.shape[1] // 2
+    qv_all = [interleave(qv_rows[:, i * per_kind : (i + 1) * per_kind], cols) for i in range(2)]
+    up_add = jnp.concatenate(
+        [interleave(small[:, i, up_at:vec_at].reshape(nf, -1), hidden // nt) for i in range(nt)]
+    )
+    proj_add, gain_one, shift_one, down_add, gain_two, shift_two = (
+        small[:, 0, vec_at + i].reshape(width).astype(F32) for i in range(6)
+    )
+    add_parts = [qv_all[0], jnp.zeros_like(qv_all[0]), qv_all[1]]
+    qkv_add = jnp.concatenate(
+        [add_parts[w][i * wide : (i + group) * wide] for i in range(0, pairs, group) for w in range(3)]
+    )
+
+    def place_grid(rows_by_f, rows, columns):
+        def place(out, i):
+            kk, zi, ti = i // (nz * nt), i // nt % nz, i % nt
+            src = zi * 2 + lax.rem(lax.axis_index("core") + kk, 2)
+            first, second = (src, ti) if rows_by_f else (ti, src)
+            return out.at[
+                pl.ds(pl.multiple_of(first * rows, rows), rows),
+                pl.ds(pl.multiple_of(second * columns, columns), columns),
+            ]
+
+        return place
+
+    def spread(shard):
+        mine = lax.all_gather(shard, ("z", "tensor"))
+        return mine, over_core(mine)
+
+    def settle(halves, shape, place):
+        return assemble(halves, shape, place)
+
+    proj_all = spread(proj_weight)
+    up_all = spread(up_weight)
+    down_all = spread(down_weight)
+    proj_full = settle(proj_all, (width, width), place_grid(False, *proj_weight.shape))
+    up_full = settle(up_all, (width, hidden), place_grid(True, *up_weight.shape))
+    down_full = settle(down_all, (hidden, width), place_grid(False, *down_weight.shape))
+
+    rows_all = jnp.concatenate([own_rows, other_rows])
+    seg_store = jnp.concatenate([own_seg, other_seg])
+    seg_global = ordered(c, own_seg, other_seg)
+    qkv = (mm(rows_all, qkv_full) + qkv_add).astype(BF)
+    total = 2 * span
+    blk = 256
+    low, high = segment_bounds(seg_global, blk, blk)
+    shift = jnp.reshape(c * (total // blk // 2), (1,)).astype(jnp.int32)
+    seg_k = jnp.broadcast_to(seg_store[:, None], (total, 128))
+    seg_q = jnp.broadcast_to(seg_store[None, :], (8, total))
+    attn_args = (seg_k, seg_q, low, high, shift)
+    mixed, lse, mixed_other = [], [], []
+    for p in range(pairs):
+        out, one = attn_fwd(qkv, *attn_args, p, pairs, group, head_size, blk, blk)
+        mixed.append(out)
+        lse.append(one)
+        mixed_other.append(over_x(out[span:]))
+    context_rows = ordered(
+        c, jnp.concatenate([m[:span] for m in mixed], 1), jnp.concatenate(mixed_other, 1), 1
+    )
+
+    token_f32 = own_rows.astype(F32)
+    n_one, inv_one = norm_forward(token_f32 + (mm(context_rows, proj_full) + proj_add))
+    first = n_one * gain_one + shift_one
+    first_low = first.astype(BF)
+    hidden_pre = mm(first_low, up_full) + up_add
+    act, gelu_pull = jax.vjp(exact_gelu, hidden_pre)
+    act_low = act.astype(BF)
+    n_two, inv_two = norm_forward(first + (mm(act_low, down_full) + down_add))
+    out_low = (n_two * gain_two + shift_two).astype(BF)
+    layer_output = ordered(t, out_low[None], over_y(out_low)[None])
+
+    cot = jnp.where(t == 0, out_grad[0], out_grad[1]).astype(F32)
+    grad_gain_two = jnp.sum(cot * n_two, axis=0)
+    grad_shift_two = jnp.sum(cot, axis=0)
+    grad_second = norm_backward(cot * gain_two, n_two, inv_two)
+    branch_low = grad_second.astype(BF)
+    grad_down_bias = jnp.sum(branch_low.astype(F32), axis=0)
+    hidden_low = gelu_pull(mm_nt(branch_low, down_full))[0].astype(BF)
+    grad_up_bias = jnp.sum(hidden_low.astype(F32), axis=0)
+    grad_first = grad_second + mm_nt(hidden_low, up_full)
+    grad_gain_one = jnp.sum(grad_first * n_one, axis=0)
+    grad_shift_one = jnp.sum(grad_first, axis=0)
+    grad_in = norm_backward(grad_first * gain_one, n_one, inv_one)
+    attn_low = grad_in.astype(BF)
+    grad_proj_bias = jnp.sum(attn_low.astype(F32), axis=0)
+    grad_context = mm_nt(attn_low, proj_full).astype(BF)
+    halves = grad_context[:, :cols], grad_context[:, cols:]
+    dctx_own = jnp.where(c == 0, halves[0], halves[1])
+    dctx_other = over_x(jnp.where(c == 0, halves[1], halves[0]))
+    dctx = jnp.concatenate([dctx_own, dctx_other])
+
+    zorder = sorted(range(nz), key=lambda zi: int(format(zi, "0%db" % zbits)[::-1], 2)) if zbits else [0]
+
+    def pick_k(a, kk):
+        even = jnp.concatenate([a[:, (2 * zi) * dblk : (2 * zi + 1) * dblk] for zi in zorder], axis=1)
+        odd = jnp.concatenate([a[:, (2 * zi + 1) * dblk : (2 * zi + 2) * dblk] for zi in zorder], axis=1)
+        return jnp.where(kk == 0, even, odd)
+
+    def pick_plain(a, kk):
+        even = jnp.concatenate([a[:, (2 * zi) * dblk : (2 * zi + 1) * dblk] for zi in range(nz)], axis=1)
+        odd = jnp.concatenate([a[:, (2 * zi + 1) * dblk : (2 * zi + 2) * dblk] for zi in range(nz)], axis=1)
+        return jnp.where(kk == 0, even, odd)
+
+    def half(a, index, axis):
+        size = a.shape[axis] // 2
+        return lax.dynamic_slice_in_dim(a, index * size, size, axis)
+
+    def halve(a, index, axis, across):
+        got = across(half(a, 1 - index, axis))
+        return (half(a, index, axis).astype(F32) + got.astype(F32)).astype(BF)
+
+    def z_halve(a, axis):
+        for bit in range(zbits):
+            a = halve(a, (z >> bit) & 1, axis, functools.partial(over_zbit, bit=bit))
+        return a
+
+    def tensor_sum(left, right):
+        out = []
+        for kk in (1 - k, k):
+            mine = pick_plain(left, kk)
+            size = right.shape[1] // nt
+            out.append([mm_tn(mine, right[:, i * size : (i + 1) * size]) for i in range(nt)])
+        got = over_core(jnp.concatenate(out[0]).astype(BF))
+        return (jnp.concatenate(out[1]) + got.astype(F32)).astype(BF)
+
+    down_sum = tensor_sum(branch_low, act_low)
+    up_sum = tensor_sum(first_low, hidden_low)
+    proj_sum = tensor_sum(attn_low, context_rows)
+    dctx, down_sum, up_sum, proj_sum = lax.optimization_barrier((dctx, down_sum, up_sum, proj_sum))
+    widths = [p.shape[1] for p in (down_sum, up_sum, proj_sum)]
+    packed = jnp.concatenate([down_sum, up_sum, proj_sum], axis=1)
+    gather = lax.psum_scatter(packed, ("tensor", "z", "context"), scatter_dimension=0, tiled=True)
+    gather = ordered(c, gather, over_x(gather), 0).astype(F32)
+    grad_down = gather[:, : widths[0]].T
+    grad_up = gather[:, widths[0] : widths[0] + widths[1]]
+    grad_proj = gather[:, widths[0] + widths[1] :].T
+
+    def total_sum(v):
+        v = v + over_core(v)
+        for bit in range(zbits):
+            v = v + over_zbit(v, bit)
+        return v + over_y(v)
+
+    vectors = [grad_proj_bias, grad_gain_one, grad_shift_one, grad_down_bias, grad_gain_two, grad_shift_two]
+    sums = jnp.concatenate(vectors + [grad_up_bias]).reshape(-1, 128)
+    sums = total_sum(sums)
+    sums = (sums + over_x(sums)).reshape(-1)
+    vector_out = [
+        lax.dynamic_slice_in_dim(sums[i * width : (i + 1) * width], f * dblk, dblk) for i in range(6)
+    ]
+    up_rows, up_cols = up_bias.shape
+    bias_up = sums[6 * width :].reshape(nt * up_rows, nf * up_cols)
+    bias_up = lax.dynamic_slice(bias_up, (t * up_rows, f * up_cols), (up_rows, up_cols))
+
+    def reduce_qkv(part):
+        sent = mm_tn(pick_k(rows_all, 1 - k), part).astype(BF)
+        kept = mm_tn(pick_k(rows_all, k), part)
+        g = (kept + over_core(sent).astype(F32)).astype(BF)
+        g = z_halve(g, 0)
+        g = halve(g, t, 0, over_y)
+        near = send(g, lambda zi, ki, ci, ti: (zi, ki, 1 - ci, ci) if ci == ti else (zi, ki, ci, ci))
+        far = send(g, lambda zi, ki, ci, ti: (zi, ki, 1 - ci, ci) if ci != ti else None)
+        return jnp.where(
+            c == t,
+            jnp.where(t == 0, jnp.concatenate([g, near]), jnp.concatenate([near, g])),
+            jnp.where(t == 0, jnp.concatenate([near, far]), jnp.concatenate([far, near])),
+        )
+
+    dqkv, qkv_parts = None, []
+    for p in range(pairs):
+        dqkv = attn_bwd(dqkv, qkv, mixed[p], dctx, lse[p], *attn_args, p, pairs, group, head_size, blk, blk)
+        if (p + 1) % group == 0 and p + 1 < pairs:
+            lo_col = (p + 1 - group) * 3 * wide
+            part = reduce_qkv(dqkv[:, lo_col : lo_col + 3 * group * wide])
+            qkv_parts.append(part)
+    chunks = 4
+    step = span // chunks
+    away = mm_nt(dqkv[span:], qkv_full).astype(BF)
+    got = [over_x(away[i * step : (i + 1) * step]) for i in range(chunks)]
+    stay = mm_nt(dqkv[:span], qkv_full) + grad_in
+    final = [
+        (stay[i * step : (i + 1) * step] + got[i].astype(F32)).astype(BF) for i in range(chunks)
+    ]
+    final_other = [over_y(part) for part in final]
+    tokens_grad = ordered(t, jnp.concatenate(final)[None], jnp.concatenate(final_other)[None])
+    qkv_parts.append(reduce_qkv(dqkv[:, (pairs - group) * 3 * wide :]))
+    qkv_rows = jnp.concatenate(qkv_parts, axis=1)
+
+    def unpack(rows, which):
+        return jnp.concatenate(
+            [rows[..., (3 * i + which * group) * wide :][..., : group * wide] for i in range(0, pairs, group)],
+            axis=-1,
+        )
+
+    grad_qkv = jnp.stack([unpack(qkv_rows, which) for which in range(3)]).astype(F32)
+    qv_sum = jnp.sum(dqkv.astype(F32), axis=0)
+    qv_sum = total_sum(jnp.concatenate([unpack(qv_sum, 0), unpack(qv_sum, 2)]).reshape(-1, 128))
+    qv_sum = jnp.where(t == c, qv_sum, over_x(qv_sum)).reshape(2, heads, head_size)
+    grad_qv = lax.dynamic_slice_in_dim(qv_sum, f * (head_size // nf), head_size // nf, 2)
+
+    return (
+        layer_output,
+        tokens_grad,
+        grad_qkv,
+        grad_qv,
+        grad_proj,
+        vector_out[0],
+        vector_out[1],
+        vector_out[2],
+        grad_up,
+        bias_up,
+        grad_down,
+        vector_out[3],
+        vector_out[4],
+        vector_out[5],
+    )
+
+
 def solution(mesh):
-    return jax.shard_map(
-        on_device,
-        mesh=mesh,
-        in_specs=(
-            P("fsdp", "context", None),
-            P("fsdp", "context"),
-            P(None, "fsdp", "tensor"),
-            P(None, "tensor", "fsdp"),
-            P("tensor", "fsdp"),
-            P("fsdp"),
-            P("fsdp"),
-            P("fsdp"),
-            P("fsdp", "tensor"),
-            P("tensor", "fsdp"),
-            P("tensor", "fsdp"),
-            P("fsdp"),
-            P("fsdp"),
-            P("fsdp"),
-            P("fsdp", "context", None),
-        ),
-        out_specs=(
-            P("fsdp", "context", None),
-            P("fsdp", "context", None),
-            P(None, "fsdp", "tensor"),
-            P(None, "tensor", "fsdp"),
-            P("tensor", "fsdp"),
-            P("fsdp"),
-            P("fsdp"),
-            P("fsdp"),
-            P("fsdp", "tensor"),
-            P("tensor", "fsdp"),
-            P("tensor", "fsdp"),
-            P("fsdp"),
-            P("fsdp"),
-            P("fsdp"),
-        ),
-        check_vma=False,
-    )
+    sizes = tuple(mesh.shape[name] for name in ("fsdp", "context", "tensor"))
+    nf, nc, nt = sizes
+    shards = (
+        P("fsdp", "context", None),
+        P("fsdp", "context"),
+        P(None, "fsdp", "tensor"),
+        P(None, "tensor", "fsdp"),
+        P("tensor", "fsdp"),
+        P("fsdp"),
+        P("fsdp"),
+        P("fsdp"),
+        P("fsdp", "tensor"),
+        P("tensor", "fsdp"),
+        P("tensor", "fsdp"),
+        P("fsdp"),
+        P("fsdp"),
+        P("fsdp"),
+    )
+    in_specs = (shards[0],) + shards[1:] + (shards[0],)
+    out_specs = (shards[0], shards[0]) + shards[2:]
+    nz = nf // 2
+    by_rows = nc == nt == 2 and nf % 2 == 0 and nz & (nz - 1) == 0
+    rows_mesh = jax.sharding.Mesh(mesh.devices.reshape(nz, 2, nc, nt), AXES) if by_rows else None
+
+    def finer(spec):
+        return P(*(("z", "core") if name == "fsdp" else name for name in spec))
+
+    def program(*args):
+        if by_rows and args[0].shape[0] // nf == nt:
+            return jax.shard_map(
+                functools.partial(on_device_rows, sizes),
+                mesh=rows_mesh,
+                in_specs=tuple(finer(spec) for spec in in_specs),
+                out_specs=tuple(finer(spec) for spec in out_specs),
+                check_vma=False,
+            )(*args)
+        return jax.shard_map(
+            on_device_general, mesh=mesh, in_specs=in_specs, out_specs=out_specs, check_vma=False
+        )(*args)
+
+    return program

time: 1950 us -> 779 us (0.40)
  waiting for transfers between devices: 875 us -> 157 us
  matrix products: 554 us -> 184 us
  Pallas kernels: 0 us -> 160 us
  other arithmetic: 220 us -> 60.7 us
  blocking collectives: 124 us -> 25.5 us
  starting transfers between devices: 1.07 us -> 70 us
  local copies, waits for them, and re-layouts: 143 us -> 94.5 us
    reduce_scatter x7 -> x1, waiting for transfers between devices: 410 us -> 0.02 us  [on_device_rows(): lax.psum_scatter(packed, ('tensor', 'z', 'context'), scatter_dimension=0,...]
    all_gather x11 -> x3, waiting for transfers between devices: 402 us -> 0.02 us  [spread(): mine = lax.all_gather(shard, ('z', 'tensor'))]
    dot_general x26 -> x29, matrix products: 554 us -> 184 us  [the longest x8 78.8 us: mm(): return jnp.dot(a, b, preferred_element_type=F32)]
    pallas_call x0 -> x12, Pallas kernels: none -> 160 us  [the longest x4 87.3 us: attn_bwd(): pl.pallas_call(body, out_shape=jax.ShapeDtypeStruct(qkv.shape, BF), grid_...]
    ppermute x0 -> x53, waiting for transfers between devices: none -> 155 us  [send(): return lax.ppermute(value, AXES, pairs)]
    convert_element_type x24 -> x14, other arithmetic: 135 us -> 18.4 us  [the longest x3 10 us: tensor_sum(): return (jnp.concatenate(out[1]) + got.astype(F32)).astype(BF)]
    ppermute x0 -> x53, starting transfers between devices: none -> 69.8 us  [send(): return lax.ppermute(value, AXES, pairs)]
    reduce_sum x14 -> x8, other arithmetic: 77.8 us -> 16.8 us  [the longest x1 4.14 us: on_device_rows(): grad_shift_two = jnp.sum(cot, axis=0)]
  transfers between devices with their start and end apart: 22 -> 57, of which waited for: 19 -> 23; matrix products, arithmetic and copies ran while one was open for 20% -> 28% of each run, Pallas kernels for 0% -> 20%
where the time goes in v1:
time: 779 us; the launch traced here: 768 us
  matrix products  184 us (24%)
  Pallas kernels  160 us (21%)
  waiting for transfers between devices  157 us (20%)
  local copies, waits for them, and re-layouts  94.5 us (12%)
  starting transfers between devices  70 us (9%)
  other arithmetic  60.7 us (8%)
  blocking collectives  25.5 us (3%)
  between operations  16.7 us (2%)
    ppermute x53, waiting for transfers between devices, send(): return lax.ppermute(value, AXES, pairs)  155 us
    pallas_call x4, Pallas kernels, attn_bwd(): pl.pallas_call(body, out_shape=jax.ShapeDtypeStruct(qkv.shape, BF), grid_...  87.3 us
    dot_general x8, matrix products, mm(): return jnp.dot(a, b, preferred_element_type=F32)  78.8 us
    unnamed x351, local copies, waits for them, and re-layouts  71.1 us
    ppermute x53, starting transfers between devices, send(): return lax.ppermute(value, AXES, pairs)  69.8 us
    pallas_call x4, Pallas kernels, attn_fwd(): pl.pallas_call(functools.partial(attn_fwd_kernel, bq=bq, bk=bk, hd=head_s...  60.1 us
    dot_general x5, matrix products, mm_nt(): lax.dot_general(a, b, (((1,), (1,)), ((), ())), preferred_element_type=F32)  53.7 us
    dot_general x16, matrix products, mm_tn(): lax.dot_general(a, b, (((0,), (0,)), ((), ())), preferred_element_type=F32)  51.5 us
  transfers between devices with their start and end apart: 57, of which 23 were waited for; matrix products, arithmetic and copies ran while one was open for 28% of the time, Pallas kernels for 20%

profile of v1, /device:TPU:28, one launch (start us, length us, event | category | flops | bytes accessed | tf_op | source)
XLA Modules:
  0.0 767.9 jit_solution(9579242435522828058)
XLA Ops:
  30.4 25.5 %all-gather = bf16[256,128]{1,0:T(8,128)(2,1)S(1)} all-gather(bf16[16,128]{1,0:T(8,128)(2,1)S(1)} %pad.4), channel_id=2, replica_groups=mesh['z'=4,'core'=2,'context'=2,'tensor'=2] {'z','core','tensor'}, dimensions={0}, use_global_device_ids=true | all-gather | bytes 69632 | tf_op jit(solution)/shard_map/all_gather | solution.py:703
  86.4 14.8 %collective-permute-done.3 = bf16[128,1536]{1,0:T(8,128)(2,1)S(1)} collective-permute-done((bf16[128,1536]{1,0:T(8,128)(2,1)S(1)}, bf16[128,1536]{1,0:T(8,128)(2,1)S(1)}, u32[]{:S(2)}, u32[]{:S(2)}) %collective-permute-start.3) | collective-permute-done | bytes 393248 | tf_op jit(solution)/shard_map/ppermute | solution.py:657
  104.2 37.3 %collective-permute-done.4 = bf16[128,1536]{1,0:T(8,128)(2,1)S(1)} collective-permute-done((bf16[128,1536]{1,0:T(8,128)(2,1)S(1)}, bf16[128,1536]{1,0:T(8,128)(2,1)S(1)}, u32[]{:S(2)}, u32[]{:S(2)}) %collective-permute-start.4) | collective-permute-done | bytes 393248 | tf_op jit(solution)/shard_map/ppermute | solution.py:657
  150.8 10.1 %add_convert_fusion.1.q_ref.k_ref.v_ref.refs_3_.refs_4_.refs_5_ = bf16[2048,1536]{1,0:T(8,128)(2,1)S(1)} fusion(bf16[1024,1536]{1,0:T(8,128)(2,1)S(1)} %assemble.4, f32[1536]{0:T(1024)} %constant_dynamic-update-slice_fusion.15, bf16[1024,1024]{0,1:T(8,128)(2,1)} %collective-permute-done.1, bf16[1024,1024]{0,1:T(8,128)(2,1)} %select_bitcast_fusion), kind=kOutput, calls=%fused_computation.19 | convolution fusion | flops 6457131008 | bytes 13637632 | tf_op jit(solution)/shard_map/dot_general | solution.py:613
  161.3 15.0 %attn_fwd.4 = (bf16[2048,128]{1,0:T(8,128)(2,1)S(1)}, f32[1,2,2048]{2,1,0:T(2,128)S(1)}) custom-call(s32[8]{0:T(128)S(1)} %get-tuple-element.214.lo_ref.refs_0_, s32[8]{0:T(128)S(1)} %get-tuple-element.213.hi_ref.refs_1_, s32[1]{0:T(128)} %bitcast.2.shift_ref.refs_2_, bf16[2048,1536]{1,0:T(8,128)(2,1)S(1)} %add_convert_fusion.1.q_ref.k_ref.v_ref.refs_3_.refs_4_.refs_5_, ...), custom_call_target="tpu_custom_call" | custom-call | flops 15000000512 | bytes 2097152 | tf_op jit(solution)/shard_map/attn_fwd/pallas_call | solution.py:466
  176.3 15.0 %attn_fwd.5 = (bf16[2048,128]{1,0:T(8,128)(2,1)S(1)}, f32[1,2,2048]{2,1,0:T(2,128)S(1)}) custom-call(s32[8]{0:T(128)S(1)} %get-tuple-element.214.lo_ref.refs_0_, s32[8]{0:T(128)S(1)} %get-tuple-element.213.hi_ref.refs_1_, s32[1]{0:T(128)} %bitcast.2.shift_ref.refs_2_, bf16[2048,1536]{1,0:T(8,128)(2,1)S(1)} %add_convert_fusion.1.q_ref.k_ref.v_ref.refs_3_.refs_4_.refs_5_, ...), custom_call_target="tpu_custom_call" | custom-call | flops 15000000512 | bytes 2097152 | tf_op jit(solution)/shard_map/attn_fwd/pallas_call | solution.py:466
  193.6 15.0 %attn_fwd.6 = (bf16[2048,128]{1,0:T(8,128)(2,1)S(1)}, f32[1,2,2048]{2,1,0:T(2,128)S(1)}) custom-call(s32[8]{0:T(128)S(1)} %get-tuple-element.214.lo_ref.refs_0_, s32[8]{0:T(128)S(1)} %get-tuple-element.213.hi_ref.refs_1_, s32[1]{0:T(128)} %bitcast.2.shift_ref.refs_2_, bf16[2048,1536]{1,0:T(8,128)(2,1)S(1)} %add_convert_fusion.1.q_ref.k_ref.v_ref.refs_3_.refs_4_.refs_5_, ...), custom_call_target="tpu_custom_call" | custom-call | flops 15000000512 | bytes 2097152 | tf_op jit(solution)/shard_map/attn_fwd/pallas_call | solution.py:466
  210.1 15.0 %attn_fwd.7 = (bf16[2048,128]{1,0:T(8,128)(2,1)S(1)}, f32[1,2,2048]{2,1,0:T(2,128)S(1)}) custom-call(s32[8]{0:T(128)S(1)} %get-tuple-element.214.lo_ref.refs_0_, s32[8]{0:T(128)S(1)} %get-tuple-element.213.hi_ref.refs_1_, s32[1]{0:T(128)} %bitcast.2.shift_ref.refs_2_, bf16[2048,1536]{1,0:T(8,128)(2,1)S(1)} %add_convert_fusion.1.q_ref.k_ref.v_ref.refs_3_.refs_4_.refs_5_, ...), custom_call_target="tpu_custom_call" | custom-call | flops 15000000512 | bytes 2097152 | tf_op jit(solution)/shard_map/attn_fwd/pallas_call | solution.py:466
  254.3 46.4 %multiply_convert_fusion = (bf16[1024,4096]{1,0:T(8,128)(2,1)}, f32[1024,4096]{1,0:T(8,128)}, f32[1024,4096]{1,0:T(8,128)}) fusion(f32[4096]{0:T(1024)S(1)} %copy-done.135, bf16[1024,1024]{0,1:T(8,128)(2,1)S(1)} %fusion.17, bf16[1024,4096]{1,0:T(8,128)(2,1)S(1)} %assemble.6), kind=kOutput, calls=%fused_computation.4 | convolution fusion | flops 8866758656 | bytes 52445184 | tf_op jit(solution)/shard_map/dot_general | solution.py:613
  307.4 16.0 %fusion.160 = (f32[1024]{0:T(1024)S(1)}, f32[1024,1024]{0,1:T(8,128)}) fusion(f32[1024]{0:T(1024)S(1)} %bitcast.162, bf16[1024,4096]{1,0:T(8,128)(2,1)} %get-tuple-element.113, bf16[4096,1024]{1,0:T(8,128)(2,1)} %copy-done.1, f32[1024]{0:T(1024)S(1)} %bitcast.159, f32[1024]{0:T(1024)S(1)} %bitcast.150, f32[1024]{0:T(1024)S(1)} %add_rsqrt_fusion.1, ...), kind=kOutput, calls=%fused_computation.371 | convolution fusion | flops 8597273600 | bytes 25190400 | tf_op jit(solution)/shard_map/dot_general | solution.py:613
  333.6 24.4 %convert_reduce_fusion = (f32[4096]{0:T(1024)}, bf16[1024,4096]{1,0:T(8,128)(2,1)}) fusion(f32[1024,4096]{1,0:T(8,128)} %get-tuple-element.114, f32[1024,4096]{1,0:T(8,128)} %get-tuple-element.207, f32[4096]{0:T(1024)S(1)} %copy-done.135, bf16[1024,1024]{0,1:T(8,128)(2,1)} %get-tuple-element.110, bf16[4096,1024]{1,0:T(8,128)(2,1)} %copy-done.1), kind=kOutput, calls=%fused_computation.2 | convolution fusion | flops 8661233664 | bytes 52461568 | tf_op jit(solution)/shard_map/dot_general | solution.py:617
  358.0 16.9 %multiply_reduce_fusion = (f32[1024]{0:T(1024)S(1)}, f32[1024]{0:T(1024)S(1)}, f32[1024]{0:T(1024)S(1)}, f32[1024]{0:T(1024)S(1)}, f32[1024,1024]{0,1:T(8,128)S(1)}) fusion(f32[1024,1024]{0,1:T(8,128)S(1)} %copy-done.35, f32[1024]{0:T(1024)S(1)} %add_rsqrt_fusion.1, f32[1024]{0:T(1024)S(1)} %broadcast_multiply_fusion.5, f32[1024]{0:T(1024)S(1)} %bitcast.151, ...), kind=kOutput, calls=%fused_computation.58 | convolution fusion | flops 8608804864 | bytes 31506432 | tf_op jit(solution)/shard_map/dot_general | solution.py:617
  432.5 17.0 %collective-permute-start.49 = (f32[80,128]{1,0:T(8,128)S(1)}, f32[80,128]{1,0:T(8,128)S(1)}, u32[]{:S(2)}, u32[]{:S(2)}) collective-permute-start(f32[80,128]{1,0:T(8,128)S(1)} %bitcast_add_fusion), channel_id=1, source_target_pairs={{0,8},{1,9},{2,10},{3,11},{4,12},{5,13},{6,14},{7,15},{8,0},{9,1},... | collective-permute-start | bytes 122888 | tf_op jit(solution)/shard_map/ppermute | solution.py:657
  470.2 21.8 %attn_bwd.4.refs_11_ = bf16[2048,1536]{1,0:T(8,128)(2,1)S(1)} custom-call(s32[8]{0:T(128)S(1)} %get-tuple-element.214.lo_ref.refs_0_, s32[8]{0:T(128)S(1)} %get-tuple-element.213.hi_ref.refs_1_, s32[1]{0:T(128)} %bitcast.2.shift_ref.refs_2_, bf16[2048,1536]{1,0:T(8,128)(2,1)S(1)} %copy-done.32, bf16[2048,1536]{1,0:T(8,128)(2,1)S(1)} %copy-done.32, ...), custom_call_target="tpu_custom_call" | custom-call | flops 24999999488 | bytes 4194304 | tf_op jit(solution)/shard_map/attn_bwd/pallas_call | solution.py:524
  492.1 21.8 %attn_bwd.5.refs_11_ = bf16[2048,1536]{1,0:T(8,128)(2,1)S(1)} custom-call(s32[8]{0:T(128)S(1)} %get-tuple-element.214.lo_ref.refs_0_, s32[8]{0:T(128)S(1)} %get-tuple-element.213.hi_ref.refs_1_, s32[1]{0:T(128)} %bitcast.2.shift_ref.refs_2_, bf16[2048,1536]{1,0:T(8,128)(2,1)S(1)} %copy-done.32, ...), custom_call_target="tpu_custom_call", output_to_operand_aliasing={{}: (11, {})} | custom-call | flops 24999999488 | bytes 4194304 | tf_op jit(solution)/shard_map/attn_bwd/pallas_call | solution.py:524
  517.0 8.1 %collective-permute-done.50 = f32[80,128]{1,0:T(8,128)S(1)} collective-permute-done((f32[80,128]{1,0:T(8,128)S(1)}, f32[80,128]{1,0:T(8,128)S(1)}, u32[]{:S(2)}, u32[]{:S(2)}) %collective-permute-start.50) | collective-permute-done | bytes 40992 | tf_op jit(solution)/shard_map/ppermute | solution.py:657
  558.7 22.0 %attn_bwd.6.refs_11_ = bf16[2048,1536]{1,0:T(8,128)(2,1)S(1)} custom-call(s32[8]{0:T(128)S(1)} %get-tuple-element.214.lo_ref.refs_0_, s32[8]{0:T(128)S(1)} %get-tuple-element.213.hi_ref.refs_1_, s32[1]{0:T(128)} %bitcast.2.shift_ref.refs_2_, bf16[2048,1536]{1,0:T(8,128)(2,1)S(1)} %copy-done.33, ...), custom_call_target="tpu_custom_call", output_to_operand_aliasing={{}: (11, {})} | custom-call | flops 24999999488 | bytes 4194304 | tf_op jit(solution)/shard_map/attn_bwd/pallas_call | solution.py:524
  580.8 21.8 %attn_bwd.7 = bf16[2048,1536]{1,0:T(8,128)(2,1)S(1)} custom-call(s32[8]{0:T(128)S(1)} %get-tuple-element.214.lo_ref.refs_0_, s32[8]{0:T(128)S(1)} %get-tuple-element.213.hi_ref.refs_1_, s32[1]{0:T(128)} %bitcast.2.shift_ref.refs_2_, bf16[2048,1536]{1,0:T(8,128)(2,1)S(1)} %copy-done.33, ...), custom_call_target="tpu_custom_call", output_to_operand_aliasing={{}: (11, {})} | custom-call | flops 24999999488 | bytes 4194304 | tf_op jit(solution)/shard_map/attn_bwd/pallas_call | solution.py:524
  631.9 7.3 collective-permute-done.31
  646.9 9.9 %collective-permute-done.23 = bf16[256,1024]{0,1:T(8,128)(2,1)} collective-permute-done((bf16[256,1024]{0,1:T(8,128)(2,1)}, bf16[256,1024]{0,1:T(8,128)(2,1)}, u32[]{:S(2)}, u32[]{:S(2)}) %collective-permute-start.23) | collective-permute-done | bytes 524320 | tf_op jit(solution)/shard_map/ppermute | solution.py:657
  656.8 11.2 %collective-permute-done.24 = bf16[256,1024]{0,1:T(8,128)(2,1)} collective-permute-done((bf16[256,1024]{0,1:T(8,128)(2,1)}, bf16[256,1024]{0,1:T(8,128)(2,1)}, u32[]{:S(2)}, u32[]{:S(2)}) %collective-permute-start.24) | collective-permute-done | bytes 524320 | tf_op jit(solution)/shard_map/ppermute | solution.py:657
  668.0 7.2 collective-permute-done.25
  684.9 18.4 %collective-permute-done.33 = bf16[64,768]{1,0:T(8,128)(2,1)S(1)} collective-permute-done((bf16[64,768]{1,0:T(8,128)(2,1)S(1)}, bf16[64,768]{1,0:T(8,128)(2,1)S(1)}, u32[]{:S(2)}, u32[]{:S(2)}) %collective-permute-start.33) | collective-permute-done | bytes 98336 | tf_op jit(solution)/shard_map/ppermute | solution.py:657
  747.3 9.1 %collective-permute-done.47 = bf16[64,4608]{1,0:T(8,128)(2,1)S(1)} collective-permute-done((bf16[64,4608]{1,0:T(8,128)(2,1)}, bf16[64,4608]{1,0:T(8,128)(2,1)S(1)}, u32[]{:S(2)}, u32[]{:S(2)}) %collective-permute-start.47) | collective-permute-done | bytes 589856 | tf_op jit(solution)/shard_map/ppermute | solution.py:657
  (617 shorter events, 324.1 us)
Async XLA Ops:
  7.2 143.2 %all-gather.8.cloned.1.call-start = ((), (), s32[]{:S(2)}) async-start(), calls=%async_computation.2 | async-start | bytes 1179648 | tf_op jit(solution)/shard_map/all_gather | solution.py:764
  7.9 223.7 %all-gather.10.cloned.1.call-start = ((), (), s32[]{:S(2)}) async-start(), calls=%async_computation.3 | async-start | bytes 4718592 | tf_op jit(solution)/shard_map/all_gather | solution.py:764
  8.7 240.3 %all-gather.12.cloned.1.call-start = ((), (), s32[]{:S(2)}) async-start(), calls=%async_computation.4 | async-start | bytes 4718592 | tf_op jit(solution)/shard_map/all_gather | solution.py:764
  9.9 70.0 %collective-permute-start.2 = (bf16[128,1536]{1,0:T(8,128)(2,1)S(1)}, bf16[128,1536]{1,0:T(8,128)(2,1)S(1)}, u32[]{:S(2)}, u32[]{:S(2)}) collective-permute-start(bf16[128,1536]{1,0:T(8,128)(2,1)S(1)} %slice_dynamic-update-slice_fusion.8), channel_id=1, source_target_pairs={{0,1},{3,2},{4,5},{7,6},{8,9},{11,10},{12,13},{15,14},{16,17},{19,... | collective-permute-start | bytes 1179656 | tf_op jit(solution)/shard_map/ppermute | solution.py:657
  26.0 124.8 %collective-permute-start.1 = (bf16[1024,1024]{0,1:T(8,128)(2,1)}, bf16[1024,1024]{0,1:T(8,128)(2,1)}, u32[]{:S(2)}, u32[]{:S(2)}) collective-permute-start(bf16[1024,1024]{0,1:T(8,128)(2,1)} %select_bitcast_fusion), channel_id=1, source_target_pairs={{0,2},{1,3},{2,0},{3,1},{4,6},{5,7},{6,4},{7,5},{8,10},{9,11},{10,... | collective-permute-start | bytes 6291464 | tf_op jit(solution)/shard_map/ppermute | solution.py:657
  29.8 56.5 %collective-permute-start = (s32[1024]{0:T(1024)S(1)}, s32[1024]{0:T(1024)S(1)}, u32[]{:S(2)}, u32[]{:S(2)}) collective-permute-start(s32[1024]{0:T(1024)S(1)} %bitcast.160), channel_id=1, source_target_pairs={{0,2},{1,3},{2,0},{3,1},{4,6},{5,7},{6,4},{7,5},{8,10},{9,11},{10,... | collective-permute-start | bytes 12296 | tf_op jit(solution)/shard_map/ppermute | solution.py:657
  29.9 716.3 %reduce-scatter.2.cloned.1.call-start = ((), (), s32[]{:S(2)}) async-start(), calls=%async_computation.1 | async-start | bytes 10027008 | tf_op jit(solution)/shard_map/reduce_scatter | solution.py:869
  84.4 57.1 %collective-permute-start.4 = (bf16[128,1536]{1,0:T(8,128)(2,1)S(1)}, bf16[128,1536]{1,0:T(8,128)(2,1)S(1)}, u32[]{:S(2)}, u32[]{:S(2)}) collective-permute-start(bf16[128,1536]{1,0:T(8,128)(2,1)S(1)} %broadcast_select_fusion.28), channel_id=1, source_target_pairs={{0,16},{1,17},{2,18},{3,19},{4,20},{5,21},{6,22},{7,23},{8,24},{9,... | collective-permute-start | bytes 1179656 | tf_op jit(solution)/shard_map/ppermute | solution.py:657
  84.4 57.9 %collective-permute-start.5 = (bf16[128,1536]{1,0:T(8,128)(2,1)S(1)}, bf16[128,1536]{1,0:T(8,128)(2,1)S(1)}, u32[]{:S(2)}, u32[]{:S(2)}) collective-permute-start(bf16[128,1536]{1,0:T(8,128)(2,1)S(1)} %broadcast_select_fusion.28), channel_id=1, source_target_pairs={{0,24},{1,25},{2,26},{3,27},{4,28},{5,29},{6,30},{7,31},{8,0},{9,1... | collective-permute-start | bytes 1179656 | tf_op jit(solution)/shard_map/ppermute | solution.py:657
  86.3 57.6 %collective-permute-start.6 = (bf16[128,1536]{1,0:T(8,128)(2,1)S(1)}, bf16[128,1536]{1,0:T(8,128)(2,1)S(1)}, u32[]{:S(2)}, u32[]{:S(2)}) collective-permute-start(bf16[128,1536]{1,0:T(8,128)(2,1)S(1)} %broadcast_select_fusion.28), channel_id=1, source_target_pairs={{0,4},{1,5},{2,6},{3,7},{4,0},{5,1},{6,2},{7,3},{8,12},{9,13},{10,... | collective-permute-start | bytes 1179656 | tf_op jit(solution)/shard_map/ppermute | solution.py:657
  101.2 42.8 %collective-permute-start.7 = (bf16[128,1536]{1,0:T(8,128)(2,1)S(1)}, bf16[128,1536]{1,0:T(8,128)(2,1)S(1)}, u32[]{:S(2)}, u32[]{:S(2)}) collective-permute-start(bf16[128,1536]{1,0:T(8,128)(2,1)S(1)} %collective-permute-done.3), channel_id=1, source_target_pairs={{0,4},{1,5},{2,6},{3,7},{4,0},{5,1},{6,2},{7,3},{8,12},{9,13},{10,... | collective-permute-start | bytes 1179656 | tf_op jit(solution)/shard_map/ppermute | solution.py:657
  150.4 86.5 %collective-permute-start.14 = (bf16[8,512,128]{2,1,0:T(8,128)(2,1)}, bf16[8,512,128]{2,1,0:T(8,128)(2,1)}, u32[]{:S(2)}, u32[]{:S(2)}) collective-permute-start(bf16[8,512,128]{2,1,0:T(8,128)(2,1)} %bitcast.137), channel_id=1, source_target_pairs={{0,4},{1,5},{2,6},{3,7},{4,0},{5,1},{6,2},{7,3},{8,12},{9,13},{10,... | collective-permute-start | bytes 3145736 | tf_op jit(solution)/shard_map/ppermute | solution.py:657
  191.4 38.7 %collective-permute-start.10 = (bf16[1024,128]{1,0:T(8,128)(2,1)S(1)}, bf16[1024,128]{1,0:T(8,128)(2,1)S(1)}, u32[]{:S(2)}, u32[]{:S(2)}) collective-permute-start(bf16[1024,128]{1,0:T(8,128)(2,1)S(1)} %slice.494), channel_id=1, source_target_pairs={{0,2},{1,3},{2,0},{3,1},{4,6},{5,7},{6,4},{7,5},{8,10},{9,11},{10,... | collective-permute-start | bytes 786440 | tf_op jit(solution)/shard_map/ppermute | solution.py:657
  249.0 51.8 %collective-permute-start.16 = (bf16[8,2048,128]{2,1,0:T(8,128)(2,1)}, bf16[8,2048,128]{2,1,0:T(8,128)(2,1)S(1)}, u32[]{:S(2)}, u32[]{:S(2)}) collective-permute-start(bf16[8,2048,128]{2,1,0:T(8,128)(2,1)} %bitcast.134), channel_id=1, source_target_pairs={{0,4},{1,5},{2,6},{3,7},{4,0},{5,1},{6,2},{7,3},{8,12},{9,13},{10,... | collective-permute-start | bytes 12582920 | tf_op jit(solution)/shard_map/ppermute | solution.py:657
  399.6 50.1 %collective-permute-start.21 = (bf16[1024,512]{1,0:T(8,128)(2,1)}, bf16[1024,512]{1,0:T(8,128)(2,1)}, u32[]{:S(2)}, u32[]{:S(2)}) collective-permute-start(bf16[1024,512]{1,0:T(8,128)(2,1)} %pad_maximum_fusion.14), channel_id=1, source_target_pairs={{0,4},{1,5},{2,6},{3,7},{4,0},{5,1},{6,2},{7,3},{8,12},{9,13},{10,... | collective-permute-start | bytes 3145736 | tf_op jit(solution)/shard_map/ppermute | solution.py:657
  400.4 51.7 %collective-permute-start.20 = (bf16[1024,2048]{1,0:T(8,128)(2,1)S(1)}, bf16[1024,2048]{1,0:T(8,128)(2,1)S(1)}, u32[]{:S(2)}, u32[]{:S(2)}) collective-permute-start(bf16[1024,2048]{1,0:T(8,128)(2,1)S(1)} %pad_maximum_fusion.4), channel_id=1, source_target_pairs={{0,4},{1,5},{2,6},{3,7},{4,0},{5,1},{6,2},{7,3},{8,12},{9,13},{10,... | collective-permute-start | bytes 12582920 | tf_op jit(solution)/shard_map/ppermute | solution.py:657
  406.0 49.5 %collective-permute-start.19 = (bf16[1024,2048]{1,0:T(8,128)(2,1)S(1)}, bf16[1024,2048]{1,0:T(8,128)(2,1)S(1)}, u32[]{:S(2)}, u32[]{:S(2)}) collective-permute-start(bf16[1024,2048]{1,0:T(8,128)(2,1)S(1)} %pad_maximum_fusion.3), channel_id=1, source_target_pairs={{0,4},{1,5},{2,6},{3,7},{4,0},{5,1},{6,2},{7,3},{8,12},{9,13},{10,... | collective-permute-start | bytes 12582920 | tf_op jit(solution)/shard_map/ppermute | solution.py:657
  431.5 106.2 %collective-permute-start.17 = (bf16[1024,1024]{0,1:T(8,128)(2,1)}, bf16[1024,1024]{0,1:T(8,128)(2,1)}, u32[]{:S(2)}, u32[]{:S(2)}) collective-permute-start(bf16[1024,1024]{0,1:T(8,128)(2,1)} %get-tuple-element.117), channel_id=1, source_target_pairs={{0,1},{1,0},{2,3},{3,2},{4,5},{5,4},{6,7},{7,6},{8,9},{9,8},{10,11... | collective-permute-start | bytes 6291464 | tf_op jit(solution)/shard_map/ppermute | solution.py:657
  432.5 84.3 %collective-permute-start.49 = (f32[80,128]{1,0:T(8,128)S(1)}, f32[80,128]{1,0:T(8,128)S(1)}, u32[]{:S(2)}, u32[]{:S(2)}) collective-permute-start(f32[80,128]{1,0:T(8,128)S(1)} %bitcast_add_fusion), channel_id=1, source_target_pairs={{0,8},{1,9},{2,10},{3,11},{4,12},{5,13},{6,14},{7,15},{8,0},{9,1},... | collective-permute-start | bytes 122888 | tf_op jit(solution)/shard_map/ppermute | solution.py:657
  629.1 38.9 %collective-permute-start.24 = (bf16[256,1024]{0,1:T(8,128)(2,1)}, bf16[256,1024]{0,1:T(8,128)(2,1)}, u32[]{:S(2)}, u32[]{:S(2)}) collective-permute-start(bf16[256,1024]{0,1:T(8,128)(2,1)} %get-tuple-element.138), channel_id=1, source_target_pairs={{0,2},{1,3},{2,0},{3,1},{4,6},{5,7},{6,4},{7,5},{8,10},{9,11},{10,... | collective-permute-start | bytes 1572872 | tf_op jit(solution)/shard_map/ppermute | solution.py:657
  629.7 45.5 %collective-permute-start.25 = (bf16[256,1024]{0,1:T(8,128)(2,1)}, bf16[256,1024]{0,1:T(8,128)(2,1)}, u32[]{:S(2)}, u32[]{:S(2)}) collective-permute-start(bf16[256,1024]{0,1:T(8,128)(2,1)} %get-tuple-element.137), channel_id=1, source_target_pairs={{0,2},{1,3},{2,0},{3,1},{4,6},{5,7},{6,4},{7,5},{8,10},{9,11},{10,... | collective-permute-start | bytes 1572872 | tf_op jit(solution)/shard_map/ppermute | solution.py:657
  639.2 43.6 %collective-permute-start.36 = (bf16[512,768]{1,0:T(8,128)(2,1)}, bf16[512,768]{1,0:T(8,128)(2,1)S(1)}, u32[]{:S(2)}, u32[]{:S(2)}) collective-permute-start(bf16[512,768]{1,0:T(8,128)(2,1)} %fusion.72), channel_id=1, source_target_pairs={{0,4},{1,5},{2,6},{3,7},{4,0},{5,1},{6,2},{7,3},{8,12},{9,13},{10,... | collective-permute-start | bytes 2359304 | tf_op jit(solution)/shard_map/ppermute | solution.py:657
  678.5 45.1 %collective-permute-start.26 = (bf16[256,1024]{0,1:T(8,128)(2,1)S(1)}, bf16[256,1024]{0,1:T(8,128)(2,1)S(1)}, u32[]{:S(2)}, u32[]{:S(2)}) collective-permute-start(bf16[256,1024]{0,1:T(8,128)(2,1)S(1)} %get-tuple-element.126), channel_id=1, source_target_pairs={{0,1},{1,0},{2,3},{3,2},{4,5},{5,4},{6,7},{7,6},{8,9},{9,8},{10,11... | collective-permute-start | bytes 1572872 | tf_op jit(solution)/shard_map/ppermute | solution.py:657
  680.6 43.0 %collective-permute-start.27 = (bf16[256,1024]{0,1:T(8,128)(2,1)S(1)}, bf16[256,1024]{0,1:T(8,128)(2,1)S(1)}, u32[]{:S(2)}, u32[]{:S(2)}) collective-permute-start(bf16[256,1024]{0,1:T(8,128)(2,1)S(1)} %get-tuple-element.129), channel_id=1, source_target_pairs={{0,1},{1,0},{2,3},{3,2},{4,5},{5,4},{6,7},{7,6},{8,9},{9,8},{10,11... | collective-permute-start | bytes 1572872 | tf_op jit(solution)/shard_map/ppermute | solution.py:657
  (190 other events, 2373.7 us)
Sparse Core Ops, SparseCore 0:
  10.1 39.6 all-gather.7
  51.9 96.8 all-gather.9
  150.9 75.8 all-gather.11
  465.3 182.0 reduce-scatter.1

commit v2 on v1

--- a/solution.py
+++ b/solution.py
@@ -548,41 +548,6 @@
     )(*operands)
 
 
-def assemble_kernel(*refs, per, place):
-    stacks = len(refs) - 4
-    out, buf, in_sem, out_sem = refs[stacks:]
-    count = stacks * per
-    blocks = [refs[i // per].at[i % per] for i in range(count)]
-    for i in range(count):
-        pltpu.make_async_copy(blocks[i], buf.at[i], in_sem.at[i]).start()
-    outs = []
-    for i in range(count):
-        pltpu.make_async_copy(blocks[i], buf.at[i], in_sem.at[i]).wait()
-        outs.append(pltpu.make_async_copy(buf.at[i], place(out, i), out_sem.at[i]))
-        outs[-1].start()
-    for one in outs:
-        one.wait()
-
-
-def assemble(stacks, shape, place):
-    per = stacks[0].shape[0]
-    count = per * len(stacks)
-    return pl.pallas_call(
-        functools.partial(assemble_kernel, per=per, place=place),
-        out_shape=jax.ShapeDtypeStruct(shape, stacks[0].dtype),
-        in_specs=[pl.BlockSpec(memory_space=pl.ANY)] * len(stacks),
-        out_specs=pl.BlockSpec(memory_space=pl.ANY),
-        scratch_shapes=[
-            pltpu.VMEM((count,) + stacks[0].shape[1:], stacks[0].dtype),
-            pltpu.SemaphoreType.DMA((count,)),
-            pltpu.SemaphoreType.DMA((count,)),
-        ],
-        compiler_params=pltpu.CompilerParams(vmem_limit_bytes=32 << 20),
-        cost_estimate=pl.CostEstimate(flops=0, bytes_accessed=2 * 2 * shape[0] * shape[1], transcendentals=0),
-        name="assemble",
-    )(*stacks)
-
-
 def segment_bounds(seg_rows, row_block, col_block):
     blocks = seg_rows.reshape(-1, row_block)
     low = jnp.sum(seg_rows[None, :] < blocks[:, :1], axis=1) // col_block
@@ -619,6 +584,941 @@
 
 def mm_tn(a, b):
     return lax.dot_general(a, b, (((0,), (0,)), ((), ())), preferred_element_type=F32)
+
+
+def remote(src, dst, send_sem, recv_sem, device):
+    return pltpu.make_async_remote_copy(
+        src_ref=src,
+        dst_ref=dst,
+        send_sem=send_sem,
+        recv_sem=recv_sem,
+        device_id=device,
+        device_id_type=pl.DeviceIdType.MESH,
+    )
+
+
+def greet(devices):
+    barrier = pltpu.get_barrier_semaphore()
+    for device in devices:
+        pl.semaphore_signal(barrier, inc=1, device_id=device, device_id_type=pl.DeviceIdType.MESH)
+    pl.semaphore_wait(barrier, len(devices))
+
+
+def aligned(start, size):
+    return pl.ds(pl.multiple_of(start, size), size)
+
+
+def open_kernel(
+    tokens, weight, small, xt_out, w_out, qkv_out, small_out,
+    x, xt, w, qkv, smalls, fill_x, fill_w, x_send, x_recv, s_send, s_recv, y_sems, z_send, z_recv,
+    c_send, c_recv, out_sems,
+    *, nz, nt, heads, head_size, group, chunk,
+):
+    z, k, c, t = (lax.axis_index(name) for name in AXES)
+    f = z * 2 + k
+    nf = nz * 2
+    span, width = tokens.shape[1:]
+    dblk = weight.shape[1]
+    cols = heads * head_size
+    gw = group * 2 * head_size
+    chunks = span // chunk
+    peers = [
+        (dz, dk, dt) for dz in range(nz) for dk in range(2) for dt in range(nt) if (dz, dk, dt) != (0, 0, 0)
+    ]
+
+    def peer(offset):
+        dz, dk, dt = offset
+        return {"z": lax.rem(z + dz, nz), "core": lax.rem(k + dk, 2), "tensor": lax.rem(t + dt, nt)}
+
+    def block(index):
+        return w.at[aligned(index * dblk, dblk), :]
+
+    for i in range(chunks):
+        r = pl.ds(i * chunk, chunk)
+        pltpu.make_async_copy(tokens.at[t, r], x.at[r], fill_x.at[i]).start()
+    fills = []
+    for g in range(cols // gw):
+        for which in range(3):
+            at = (g * 3 + which) * gw
+            fills.append(
+                pltpu.make_async_copy(
+                    weight.at[which, :, pl.ds(g * gw, gw)],
+                    w.at[aligned(f * dblk, dblk), pl.ds(at, gw)],
+                    fill_w.at[len(fills)],
+                )
+            )
+
+    @pl.when(c == t)
+    def _():
+        for one in fills:
+            one.start()
+
+    greet([{"context": 1 - c}] + [peer(offset) for offset in peers])
+    x_copies = [
+        remote(
+            tokens.at[t, pl.ds(i * chunk, chunk)],
+            x.at[pl.ds(span + i * chunk, chunk)],
+            x_send.at[i],
+            x_recv.at[i],
+            {"context": 1 - c},
+        )
+        for i in range(chunks)
+    ]
+    for one in x_copies:
+        one.start()
+    y_copy = remote(block(f), block(f), y_sems.at[0], y_sems.at[1], {"tensor": 1 - t})
+
+    @pl.when(c == t)
+    def _():
+        for one in fills:
+            one.wait()
+        y_copy.start()
+
+    def small_copy(i, source):
+        return remote(small, smalls.at[source], s_send.at[i], s_recv.at[source], peer(peers[i]))
+
+    me = f * nt + t
+    for i in range(len(peers)):
+        small_copy(i, me).start()
+    smalls[me] = small[...]
+
+    @pl.when(c != t)
+    def _():
+        y_copy.wait_recv()
+
+    def z_copy(d, owner):
+        return remote(
+            block(owner * 2 + k), block(owner * 2 + k), z_send.at[d - 1], z_recv.at[owner], {"z": lax.rem(z + d, nz)}
+        )
+
+    def c_copy(owner, core):
+        return remote(
+            block(owner * 2 + core), block(owner * 2 + core), c_send.at[owner], c_recv.at[owner], {"core": 1 - k}
+        )
+
+    for d in range(1, nz):
+        z_copy(d, z).start()
+    c_copy(z, k).start()
+
+    for i in range(chunks):
+        r = pl.ds(i * chunk, chunk)
+        pltpu.make_async_copy(tokens.at[t, r], x.at[r], fill_x.at[i]).wait()
+        xt[:, i * chunk : (i + 1) * chunk] = x[i * chunk : (i + 1) * chunk, :].T
+
+    for i in range(len(peers)):
+        dz, dk, dt = peers[i]
+        source = (lax.rem(z + nz - dz, nz) * 2 + lax.rem(k + dk, 2)) * nt + lax.rem(t + nt - dt, nt)
+        small_copy(i, source).wait_recv()
+
+    edge = head_size // nf
+    lanes = small.shape[1]
+    rows = jnp.concatenate([smalls[fi * nt + c, 0:1, :] for fi in range(nf)], axis=0)
+    col = lax.broadcasted_iota(jnp.int32, (lanes, cols), 1)
+    source = lax.broadcasted_iota(jnp.int32, (lanes, cols), 0)
+    fcol = lax.broadcasted_iota(jnp.int32, (nf, cols), 1)
+    mine = lax.rem(fcol, head_size) // edge == lax.broadcasted_iota(jnp.int32, (nf, cols), 0)
+    biases = []
+    for kind in range(2):
+        pick = source == col // head_size * edge + lax.rem(col, edge) + kind * heads * edge
+        spread_out = mm(rows, jnp.where(pick, 1.0, 0.0).astype(BF))
+        biases.append(jnp.sum(jnp.where(mine, spread_out, 0.0), axis=0, keepdims=True))
+    parts = [biases[0], jnp.zeros_like(biases[0]), biases[1]]
+    bias = jnp.concatenate(
+        [parts[which][:, g * gw : (g + 1) * gw] for g in range(cols // gw) for which in range(3)], axis=1
+    )
+
+    for d in range(1, nz):
+        owner = lax.rem(z + nz - d, nz)
+        z_copy(d, owner).wait_recv()
+        c_copy(owner, k).start()
+    for owner in range(nz):
+        c_copy(owner, 1 - k).wait_recv()
+
+    w_done = pltpu.make_async_copy(w, w_out, out_sems.at[0, 0])
+    w_done.start()
+    small_done = pltpu.make_async_copy(smalls, small_out, out_sems.at[0, 1])
+    small_done.start()
+
+    def project(i):
+        r = aligned(i * chunk, chunk)
+        acc = mm(x[r, :], w[...]) + bias
+        qkv[r, :] = acc.astype(BF)
+        pltpu.make_async_copy(qkv.at[r], qkv_out.at[r], out_sems.at[1, i]).start()
+
+    @pl.loop(0, chunks)
+    def _(i):
+        project(i)
+
+    @pl.loop(0, chunks)
+    def _(i):
+        remote(
+            tokens.at[t, aligned(i * chunk, chunk)],
+            x.at[aligned(span + i * chunk, chunk)],
+            x_send.at[i],
+            x_recv.at[i],
+            {"context": 1 - c},
+        ).wait_recv()
+        r = aligned(span + i * chunk, chunk)
+        xt[:, r] = x[r, :].T
+        project(chunks + i)
+
+    xt_done = pltpu.make_async_copy(xt, xt_out, out_sems.at[0, 2])
+    xt_done.start()
+    for i in range(2 * chunks):
+        r = pl.ds(i * chunk, chunk)
+        pltpu.make_async_copy(qkv.at[r], qkv_out.at[r], out_sems.at[1, i]).wait()
+    for one in (w_done, small_done, xt_done):
+        one.wait()
+    for one in x_copies:
+        one.wait_send()
+    for i in range(len(peers)):
+        small_copy(i, me).wait_send()
+    for d in range(1, nz):
+        z_copy(d, z).wait_send()
+    for owner in range(nz):
+        c_copy(owner, k).wait_send()
+
+    @pl.when(c == t)
+    def _():
+        y_copy.wait_send()
+
+
+def open_layer(tokens, weight, small, nz, nt, heads, head_size, group):
+    span, width = tokens.shape[1:]
+    cols = heads * head_size
+    chunk = 256
+    chunks = span // chunk
+    nf = nz * 2
+    dma = pltpu.SemaphoreType.DMA
+    hbm = pl.BlockSpec(memory_space=pl.ANY)
+    moved = 2 * (span * width * 2 + 4 * width * cols * 3)
+    return pl.pallas_call(
+        functools.partial(
+            open_kernel, nz=nz, nt=nt, heads=heads, head_size=head_size, group=group, chunk=chunk
+        ),
+        out_shape=(
+            jax.ShapeDtypeStruct((width, 2 * span), BF),
+            jax.ShapeDtypeStruct((width, 3 * cols), BF),
+            jax.ShapeDtypeStruct((2 * span, 3 * cols), BF),
+            jax.ShapeDtypeStruct((nf * nt,) + small.shape, BF),
+        ),
+        in_specs=[hbm, hbm, pl.BlockSpec(memory_space=pltpu.VMEM)],
+        out_specs=(hbm,) * 4,
+        scratch_shapes=[
+            pltpu.VMEM((2 * span, width), BF),
+            pltpu.VMEM((width, 2 * span), BF),
+            pltpu.VMEM((width, 3 * cols), BF),
+            pltpu.VMEM((2 * span, 3 * cols), BF),
+            pltpu.VMEM((nf * nt,) + small.shape, BF),
+            dma((chunks,)),
+            dma((heads // 2 // group * 3,)),
+            dma((chunks,)),
+            dma((chunks,)),
+            dma((nf * nt,)),
+            dma((nf * nt,)),
+            dma((2,)),
+            dma((nz,)),
+            dma((nz,)),
+            dma((nz,)),
+            dma((nz,)),
+            dma((2, max(3, 2 * chunks))),
+        ],
+        compiler_params=pltpu.CompilerParams(
+            collective_id=0, has_side_effects=True, vmem_limit_bytes=40 << 20
+        ),
+        cost_estimate=pl.CostEstimate(
+            flops=2 * 2 * span * width * 3 * cols, bytes_accessed=moved, transcendentals=0
+        ),
+        name="open_layer",
+    )(tokens, weight, small)
+
+
+def close_kernel(
+    dqkv_in, w_in, xt_in, grad_in, vec_in, tokens_out, grad_out, sums_out,
+    dqkv, w, xt, dres, own, xs, xr, fin, away, near, zs, zr, piece, last, sums, sums_near, sums_z, sums_last,
+    fill, x_send, x_recv, y_send, y_recv, c_sems, z_send, z_recv, p_send, p_recv, o_sems,
+    *, nz, chunk, tile,
+):
+    z, k, c, t = (lax.axis_index(name) for name in AXES)
+    rows, wide = dqkv.shape
+    span = rows // 2
+    dblk = xt.shape[2]
+    chunks = span // chunk
+    steps = wide // tile
+    x_dev, y_dev, core_dev = {"context": 1 - c}, {"tensor": 1 - t}, {"core": 1 - k}
+    diag = {"context": 1 - c, "tensor": 1 - t}
+
+    loads = [
+        pltpu.make_async_copy(w_in, w, fill.at[0]),
+        pltpu.make_async_copy(dqkv_in.at[pl.ds(span, span)], dqkv.at[pl.ds(span, span)], fill.at[1]),
+        pltpu.make_async_copy(dqkv_in.at[pl.ds(0, span)], dqkv.at[pl.ds(0, span)], fill.at[2]),
+        pltpu.make_async_copy(grad_in, dres, fill.at[3]),
+        pltpu.make_async_copy(vec_in, sums.at[pl.ds(sums.shape[0] - vec_in.shape[0], vec_in.shape[0])], fill.at[4]),
+    ]
+    for kk in range(2):
+        for zi in range(nz):
+            source = zi * 2 + lax.rem(1 - k + kk, 2)
+            loads.append(
+                pltpu.make_async_copy(
+                    xt_in.at[aligned(source * dblk, dblk)], xt.at[kk, zi], fill.at[len(loads)]
+                )
+            )
+    for one in loads:
+        one.start()
+    greet([x_dev, y_dev, diag, core_dev] + [{"z": lax.rem(z + d, nz)} for d in range(1, nz)])
+
+    def x_copy(i):
+        return remote(xs.at[i], xr.at[i], x_send.at[i], x_recv.at[i], x_dev)
+
+    def y_copy(i):
+        return remote(fin.at[i], tokens_out.at[t, aligned(i * chunk, chunk)], y_send.at[i], y_recv.at[i], y_dev)
+
+    loads[0].wait()
+    loads[1].wait()
+
+    @pl.loop(0, chunks)
+    def _(i):
+        xs[i] = mm_nt(dqkv[aligned(span + i * chunk, chunk), :], w[...]).astype(BF)
+        x_copy(i).start()
+
+    for one in loads[2:]:
+        one.wait()
+    ones = jnp.ones((8, rows), BF)
+    vec_at = sums.shape[0] - vec_in.shape[0]
+    sums[0:vec_at, :] = jnp.zeros((vec_at, 128), F32)
+
+    @pl.loop(0, steps)
+    def _(j):
+        part = dqkv[:, aligned(j * tile, tile)]
+        for zi in range(nz):
+            away[zi, :, aligned(j * tile, tile)] = mm(xt[0, zi], part).astype(BF)
+        total = mm(ones, part)
+        for u in range(tile // 128):
+            sums[pl.ds(j * (tile // 128) + u, 1), :] = total[0:1, u * 128 : (u + 1) * 128]
+
+    core_copy = remote(away, near, c_sems.at[0], c_sems.at[1], core_dev)
+    core_copy.start()
+    core_sum = remote(sums, sums_near, c_sems.at[2], c_sems.at[3], core_dev)
+    core_sum.start()
+
+    @pl.loop(0, chunks)
+    def _(i):
+        r = aligned(i * chunk, chunk)
+        own[r, :] = mm_nt(dqkv[r, :], w[...]) + dres[r, :]
+
+    def finish(i):
+        x_copy(i).wait_recv()
+        r = aligned(i * chunk, chunk)
+        fin[i] = (own[r, :] + xr[i].astype(F32)).astype(BF)
+        pltpu.make_async_copy(fin.at[i], tokens_out.at[t, r], o_sems.at[i]).start()
+        y_copy(i).start()
+
+    core_copy.wait_recv()
+    core_sum.wait_recv()
+    sums_z[z] = sums[...] + sums_near[...]
+
+    @pl.loop(0, steps)
+    def _(j):
+        cut = aligned(j * tile, tile)
+        part = dqkv[:, cut]
+        for zi in range(nz):
+            zs[zi, :, cut] = (mm(xt[1, zi], part) + near[zi, :, cut].astype(F32)).astype(BF)
+
+    def z_copy(d, owner, target):
+        return remote(zs.at[target], zr.at[owner], z_send.at[0, d - 1], z_recv.at[0, owner], {"z": lax.rem(z + d, nz)})
+
+    def z_sum(d, owner):
+        return remote(
+            sums_z.at[owner], sums_z.at[owner], z_send.at[1, d - 1], z_recv.at[1, owner], {"z": lax.rem(z + d, nz)}
+        )
+
+    for d in range(1, nz):
+        z_copy(d, z, lax.rem(z + d, nz)).start()
+        z_sum(d, z).start()
+
+    half = chunks // 2
+
+    @pl.loop(0, half)
+    def _(i):
+        finish(i)
+
+    for d in range(1, nz):
+        owner = lax.rem(z + nz - d, nz)
+        z_copy(d, owner, z).wait_recv()
+        z_sum(d, owner).wait_recv()
+    total = zs[z].astype(F32)
+    for d in range(1, nz):
+        total = total + zr[lax.rem(z + nz - d, nz)].astype(F32)
+    piece[...] = total.astype(BF)
+    sums_last[0] = jnp.sum(sums_z[...], axis=0)
+
+    p_x = remote(piece, last.at[0], p_send.at[0], p_recv.at[0], x_dev)
+    p_y = remote(piece, last.at[1], p_send.at[1], p_recv.at[1], y_dev)
+    p_d = remote(piece, last.at[2], p_send.at[2], p_recv.at[2], diag)
+    s_x = remote(sums_last.at[0], sums_last.at[1], p_send.at[3], p_recv.at[3], x_dev)
+    s_y = remote(sums_last.at[0], sums_last.at[2], p_send.at[4], p_recv.at[4], y_dev)
+    s_d = remote(sums_last.at[0], sums_last.at[3], p_send.at[5], p_recv.at[5], diag)
+
+    for one in (s_x, s_y, s_d):
+        one.start()
+
+    @pl.when(c == t)
+    def _():
+        p_x.start()
+
+    @pl.when(c != t)
+    def _():
+        p_y.start()
+        p_d.start()
+
+    @pl.loop(half, chunks)
+    def _(i):
+        finish(i)
+
+    for one in (s_x, s_y, s_d):
+        one.wait()
+    near_pair = sums_last[0] + sums_last[2]
+    far_pair = sums_last[1] + sums_last[3]
+    sums_out[0:vec_at, :] = jnp.where(c == t, near_pair, far_pair)[0:vec_at]
+    sums_out[vec_at:, :] = (near_pair + far_pair)[vec_at:]
+
+    @pl.when(c == t)
+    def _():
+        p_y.wait_recv()
+        grad_out[...] = piece[...].astype(F32) + last[1].astype(F32)
+        p_x.wait_send()
+
+    @pl.when(c != t)
+    def _():
+        p_x.wait_recv()
+        p_d.wait_recv()
+        grad_out[...] = last[0].astype(F32) + last[2].astype(F32)
+        p_y.wait_send()
+        p_d.wait_send()
+
+    core_copy.wait_send()
+    core_sum.wait_send()
+    for d in range(1, nz):
+        z_copy(d, z, lax.rem(z + d, nz)).wait_send()
+        z_sum(d, z).wait_send()
+
+    @pl.loop(0, chunks)
+    def _(i):
+        r = aligned(i * chunk, chunk)
+        x_copy(i).wait_send()
+        pltpu.make_async_copy(fin.at[i], tokens_out.at[t, r], o_sems.at[i]).wait()
+        y_copy(i).wait_send()
+        remote(fin.at[i], tokens_out.at[1 - t, r], y_send.at[i], y_recv.at[i], y_dev).wait_recv()
+
+
+def close_layer(dqkv, w, xt, grad_in, vectors, nz):
+    rows, wide = dqkv.shape
+    width = w.shape[0]
+    span = rows // 2
+    dblk = width // (2 * nz)
+    chunk, tile = 128, 256
+    chunks = span // chunk
+    dma = pltpu.SemaphoreType.DMA
+    hbm = pl.BlockSpec(memory_space=pl.ANY)
+    sum_rows = wide // 128 + -(wide // 128) % 8 + vectors.shape[0]
+    return pl.pallas_call(
+        functools.partial(close_kernel, nz=nz, chunk=chunk, tile=tile),
+        out_shape=(
+            jax.ShapeDtypeStruct((2, span, width), BF),
+            jax.ShapeDtypeStruct((dblk, wide), F32),
+            jax.ShapeDtypeStruct((sum_rows, 128), F32),
+        ),
+        in_specs=[hbm] * 5,
+        out_specs=(hbm, pl.BlockSpec(memory_space=pltpu.VMEM), pl.BlockSpec(memory_space=pltpu.VMEM)),
+        scratch_shapes=[
+            pltpu.VMEM((rows, wide), BF),
+            pltpu.VMEM((width, wide), BF),
+            pltpu.VMEM((2, nz, dblk, rows), BF),
+            pltpu.VMEM((span, width), F32),
+            pltpu.VMEM((span, width), F32),
+            pltpu.VMEM((chunks, chunk, width), BF),
+            pltpu.VMEM((chunks, chunk, width), BF),
+            pltpu.VMEM((chunks, chunk, width), BF),
+            pltpu.VMEM((nz, dblk, wide), BF),
+            pltpu.VMEM((nz, dblk, wide), BF),
+            pltpu.VMEM((nz, dblk, wide), BF),
+            pltpu.VMEM((nz, dblk, wide), BF),
+            pltpu.VMEM((dblk, wide), BF),
+            pltpu.VMEM((3, dblk, wide), BF),
+            pltpu.VMEM((sum_rows, 128), F32),
+            pltpu.VMEM((sum_rows, 128), F32),
+            pltpu.VMEM((nz, sum_rows, 128), F32),
+            pltpu.VMEM((4, sum_rows, 128), F32),
+            dma((5 + 2 * nz,)),
+            dma((chunks,)),
+            dma((chunks,)),
+            dma((chunks,)),
+            dma((chunks,)),
+            dma((4,)),
+            dma((2, nz)),
+            dma((2, nz)),
+            dma((6,)),
+            dma((6,)),
+            dma((chunks,)),
+        ],
+        compiler_params=pltpu.CompilerParams(
+            collective_id=1, has_side_effects=True, vmem_limit_bytes=56 << 20
+        ),
+        cost_estimate=pl.CostEstimate(
+            flops=4 * rows * width * wide, bytes_accessed=30 << 20, transcendentals=0
+        ),
+        name="close_layer",
+    )(dqkv, w, xt, grad_in, vectors)
+
+
+def mean_of(rows):
+    return jnp.mean(rows, axis=-1, keepdims=True)
+
+
+def load_blocks(stack, start, dest, sems, nt, rows_by_f):
+    count, rows = stack.shape[:2]
+    columns = dest.shape[1] // nt if rows_by_f else stack.shape[2]
+    copies = []
+    for b in range(count):
+        first, second = (b // nt, b % nt) if rows_by_f else (b % nt, b // nt)
+        spot = dest.at[pl.ds(first * rows, rows), pl.ds(second * columns, columns)]
+        copies.append(pltpu.make_async_copy(stack.at[b, :, pl.ds(start, columns)], spot, sems.at[b]))
+    return copies
+
+
+def up_kernel(
+    t_ref, ctx, tok, vecs, up_add, up_in, first, norm_one, inv_one, first_t, act, slope,
+    up, proj, low, u, fill,
+    *, nt, tile,
+):
+    i = pl.program_id(0)
+    width, hidden = up.shape
+    tiles = hidden // tile
+    up_fill = load_blocks(up_in, 0, up, fill.at[0], nt, True)
+    proj_fill = load_blocks(up_in, hidden // nt, proj, fill.at[1], nt, True)
+
+    @pl.when(i == 0)
+    def _():
+        for one in proj_fill + up_fill:
+            one.start()
+        for one in proj_fill:
+            one.wait()
+
+    def vec(row):
+        return vecs[row : row + 1, :]
+
+    h = tok[0].astype(F32) + (mm_nt(ctx[...], proj[...]) + vec(0))
+    centred = h - mean_of(h)
+    inv = lax.rsqrt(mean_of(centred * centred) + NORM_EPS)
+    normed = centred * inv
+    norm_one[...] = normed
+    inv_one[...] = jnp.broadcast_to(inv, inv_one.shape)
+    normed = normed * vec(1) + vec(2)
+    first[...] = normed
+    low[...] = normed.astype(BF)
+    first_t[...] = low[...].T
+
+    @pl.when(i == 0)
+    def _():
+        for one in up_fill:
+            one.wait()
+
+    u[0] = mm(low[...], up[:, :tile])
+
+    def activate(j, slot):
+        cut = aligned(j * tile, tile)
+        value = u[slot] + up_add[0:1, cut]
+        phi = 0.5 + 0.5 * lax.erf(value * (0.5**0.5))
+        act[:, cut] = (value * phi).astype(BF)
+        slope[:, cut] = (phi + value * (jnp.exp(-0.5 * value * value) * ((2.0 * jnp.pi) ** -0.5))).astype(BF)
+
+    @pl.loop(0, tiles - 1)
+    def _(j):
+        slot = lax.rem(j, 2)
+        following = mm(low[...], up[:, aligned((j + 1) * tile, tile)])
+        activate(j, slot)
+        u[1 - slot] = following
+
+    activate(tiles - 1, (tiles - 1) % 2)
+
+
+def up_layer(t, ctx, tokens, vecs, up_add, up_all, nt):
+    span, width = ctx.shape
+    hidden = up_add.shape[1]
+    block, tile = 256, 512
+    hbm = pl.BlockSpec(memory_space=pl.ANY)
+    rows = pl.BlockSpec((block, width), lambda i, _: (i, 0))
+    wide = pl.BlockSpec((block, hidden), lambda i, _: (i, 0))
+    whole = lambda shape: pl.BlockSpec(shape, lambda i, _: (0,) * len(shape))
+    picked = pl.BlockSpec((1, block, width), lambda i, t_ref: (t_ref[0], i, 0))
+    sds = jax.ShapeDtypeStruct
+    return pl.pallas_call(
+        functools.partial(up_kernel, nt=nt, tile=tile),
+        out_shape=(
+            sds((span, width), F32),
+            sds((span, width), F32),
+            sds((span, 128), F32),
+            sds((width, span), BF),
+            sds((span, hidden), BF),
+            sds((span, hidden), BF),
+        ),
+        grid_spec=pltpu.PrefetchScalarGridSpec(
+            num_scalar_prefetch=1,
+            grid=(span // block,),
+            in_specs=[rows, picked, whole(vecs.shape), whole(up_add.shape), hbm],
+            out_specs=(
+                rows,
+                rows,
+                pl.BlockSpec((block, 128), lambda i, _: (i, 0)),
+                pl.BlockSpec((width, block), lambda i, _: (0, i)),
+                wide,
+                wide,
+            ),
+            scratch_shapes=[
+                pltpu.VMEM((width, hidden), BF),
+                pltpu.VMEM((width, width), BF),
+                pltpu.VMEM((block, width), BF),
+                pltpu.VMEM((2, block, tile), F32),
+                pltpu.SemaphoreType.DMA((2, up_all.shape[0])),
+            ],
+        ),
+        compiler_params=pltpu.CompilerParams(vmem_limit_bytes=60 << 20),
+        cost_estimate=pl.CostEstimate(
+            flops=2 * span * width * (width + hidden), bytes_accessed=40 << 20, transcendentals=2 * span * hidden
+        ),
+        name="up_layer",
+    )(t, ctx, tokens, vecs, up_add, up_all)
+
+
+def add_rows(sums, row, value):
+    sums[row] += jnp.sum(value.reshape(-1, 8, value.shape[1]), axis=0)
+
+
+def down_kernel(
+    t_ref, cot, vecs, first, act, down_in, out, branch, branch_t, grad_second, vec_sums,
+    down, acc, sums, fill,
+    *, nt,
+):
+    i = pl.program_id(0)
+    hidden, width = down.shape
+    down_fill = load_blocks(down_in, 0, down, fill, nt, False)
+
+    @pl.when(i == 0)
+    def _():
+        for one in down_fill:
+            one.start()
+        sums[...] = jnp.zeros(sums.shape, F32)
+        for one in down_fill:
+            one.wait()
+
+    def vec(row):
+        return vecs[row : row + 1, :]
+
+    tile = 256
+
+    @pl.loop(0, width // tile)
+    def _(j):
+        cut = aligned(j * tile, tile)
+        acc[:, cut] = mm(act[...], down[:, cut])
+
+    h = first[...] + (acc[...] + vec(3))
+    centred = h - mean_of(h)
+    inv = lax.rsqrt(mean_of(centred * centred) + NORM_EPS)
+    normed = centred * inv
+    out[...] = (normed * vec(4) + vec(5)).astype(BF)
+    grad = cot[0].astype(F32)
+    add_rows(sums, 1, grad * normed)
+    add_rows(sums, 2, grad)
+    grad = grad * vec(4)
+    grad = inv * (grad - mean_of(grad) - normed * mean_of(grad * normed))
+    grad_second[...] = grad
+    low = grad.astype(BF)
+    branch[...] = low
+    add_rows(sums, 0, low.astype(F32))
+    branch_t[...] = low.T
+
+    @pl.when(i == pl.num_programs(0) - 1)
+    def _():
+        for row in range(3):
+            vec_sums[row : row + 1, :] = jnp.sum(sums[row], axis=0, keepdims=True)
+        vec_sums[3:8, :] = jnp.zeros((5, width), F32)
+
+
+def down_layer(t, out_grad, vecs, first, act, down_all, nt):
+    span, width = first.shape
+    hidden = act.shape[1]
+    block = 256
+    rows = pl.BlockSpec((block, width), lambda i, _: (i, 0))
+    whole = lambda shape: pl.BlockSpec(shape, lambda i, _: (0,) * len(shape))
+    sds = jax.ShapeDtypeStruct
+    return pl.pallas_call(
+        functools.partial(down_kernel, nt=nt),
+        out_shape=(
+            sds((span, width), BF),
+            sds((span, width), BF),
+            sds((width, span), BF),
+            sds((span, width), F32),
+            sds((8, width), F32),
+        ),
+        grid_spec=pltpu.PrefetchScalarGridSpec(
+            num_scalar_prefetch=1,
+            grid=(span // block,),
+            in_specs=[
+                pl.BlockSpec((1, block, width), lambda i, t_ref: (t_ref[0], i, 0)),
+                whole(vecs.shape),
+                rows,
+                pl.BlockSpec((block, hidden), lambda i, _: (i, 0)),
+                pl.BlockSpec(memory_space=pl.ANY),
+            ],
+            out_specs=(rows, rows, pl.BlockSpec((width, block), lambda i, _: (0, i)), rows, whole((8, width))),
+            scratch_shapes=[
+                pltpu.VMEM((hidden, width), BF),
+                pltpu.VMEM((block, width), F32),
+                pltpu.VMEM((3, 8, width), F32),
+                pltpu.SemaphoreType.DMA((down_all.shape[0],)),
+            ],
+        ),
+        compiler_params=pltpu.CompilerParams(vmem_limit_bytes=60 << 20),
+        cost_estimate=pl.CostEstimate(
+            flops=2 * span * width * hidden, bytes_accessed=30 << 20, transcendentals=0
+        ),
+        name="down_layer",
+    )(t, out_grad, vecs, first, act, down_all)
+
+
+def back_kernel(
+    vecs, branch, grad_second, slope, norm_one, inv_one, up_in, down_in,
+    hid, attn_t, grad_in, grad_ctx, vec_sums, up_sums,
+    up, down, proj, acc, sums, sums_u, fill,
+    *, nt, tile,
+):
+    i = pl.program_id(0)
+    width, hidden = up.shape
+    down_fill = load_blocks(down_in, 0, down, fill.at[0], nt, False)
+    up_fill = load_blocks(up_in, 0, up, fill.at[1], nt, True)
+    proj_fill = load_blocks(up_in, hidden // nt, proj, fill.at[2], nt, True)
+
+    @pl.when(i == 0)
+    def _():
+        for one in down_fill + up_fill + proj_fill:
+            one.start()
+        sums[...] = jnp.zeros(sums.shape, F32)
+        sums_u[...] = jnp.zeros(sums_u.shape, F32)
+        for one in down_fill + up_fill + proj_fill:
+            one.wait()
+
+    ones = jnp.ones((8, branch.shape[0]), BF)
+    acc[...] = grad_second[...]
+
+    @pl.loop(0, hidden // tile)
+    def _(j):
+        cut = aligned(j * tile, tile)
+        low_hid = (mm_nt(branch[...], down[cut, :]) * slope[:, cut].astype(F32)).astype(BF)
+        hid[:, cut] = low_hid
+        sums_u[:, cut] += mm(ones, low_hid)
+        acc[...] += mm_nt(low_hid, up[:, cut])
+
+    grad = acc[...]
+    normed = norm_one[...]
+    add_rows(sums, 1, grad * normed)
+    add_rows(sums, 2, grad)
+    grad = grad * vecs[1:2, :]
+    grad = inv_one[:, 0:1] * (grad - mean_of(grad) - normed * mean_of(grad * normed))
+    grad_in[...] = grad
+    low = grad.astype(BF)
+    add_rows(sums, 0, low.astype(F32))
+    attn_t[...] = low.T
+    grad_ctx[...] = mm(low, proj[...]).astype(BF)
+
+    @pl.when(i == pl.num_programs(0) - 1)
+    def _():
+        for row in range(3):
+            vec_sums[row : row + 1, :] = jnp.sum(sums[row], axis=0, keepdims=True)
+        vec_sums[3:8, :] = jnp.zeros((5, width), F32)
+        up_sums[...] = sums_u[...]
+
+
+def back_layer(vecs, branch, grad_second, slope, norm_one, inv_one, up_all, down_all, nt):
+    span, width = branch.shape
+    hidden = slope.shape[1]
+    block, tile = 256, 512
+    hbm = pl.BlockSpec(memory_space=pl.ANY)
+    rows = pl.BlockSpec((block, width), lambda i: (i, 0))
+    wide = pl.BlockSpec((block, hidden), lambda i: (i, 0))
+    whole = lambda shape: pl.BlockSpec(shape, lambda i: (0,) * len(shape))
+    sds = jax.ShapeDtypeStruct
+    return pl.pallas_call(
+        functools.partial(back_kernel, nt=nt, tile=tile),
+        out_shape=(
+            sds((span, hidden), BF),
+            sds((width, span), BF),
+            sds((span, width), F32),
+            sds((span, width), BF),
+            sds((8, width), F32),
+            sds((8, hidden), F32),
+        ),
+        grid=(span // block,),
+        in_specs=[
+            whole(vecs.shape),
+            rows,
+            rows,
+            wide,
+            rows,
+            pl.BlockSpec((block, 128), lambda i: (i, 0)),
+            hbm,
+            hbm,
+        ],
+        out_specs=(
+            wide, pl.BlockSpec((width, block), lambda i: (0, i)), rows, rows, whole((8, width)), whole((8, hidden)),
+        ),
+        scratch_shapes=[
+            pltpu.VMEM((width, hidden), BF),
+            pltpu.VMEM((hidden, width), BF),
+            pltpu.VMEM((width, width), BF),
+            pltpu.VMEM((block, width), F32),
+            pltpu.VMEM((3, 8, width), F32),
+            pltpu.VMEM((8, hidden), F32),
+            pltpu.SemaphoreType.DMA((3, up_all.shape[0])),
+        ],
+        compiler_params=pltpu.CompilerParams(vmem_limit_bytes=60 << 20),
+        cost_estimate=pl.CostEstimate(
+            flops=2 * span * width * (width + 2 * hidden), bytes_accessed=60 << 20, transcendentals=0
+        ),
+        name="back_layer",
+    )(vecs, branch, grad_second, slope, norm_one, inv_one, up_all, down_all)
+
+
+def grads_kernel(*refs, pairs, nz, nt, chunk):
+    lefts, rights = refs[0 : 2 * pairs : 2], refs[1 : 2 * pairs : 2]
+    packed, left, right, away, near, stage, l_fill, r_fill, send, recv, out_sems = refs[2 * pairs :]
+    k = lax.axis_index("core")
+    core_dev = {"core": 1 - k}
+    dblk = left.shape[3]
+    span = right.shape[1]
+    plan = []
+    base = 0
+    for which in range(pairs):
+        size = rights[which].shape[1] // nt
+        for ti in range(nt):
+            for at in range(0, size, min(chunk, size)):
+                step = min(chunk, size)
+                plan.append((which, ti * size + at, ti, base + at, step))
+        base += size
+
+    l_copies = [
+        [
+            pltpu.make_async_copy(
+                lefts[which].at[aligned((zi * 2 + lax.rem(k + 1 + kk, 2)) * dblk, dblk)],
+                left.at[which, kk, zi],
+                l_fill.at[which, kk, zi],
+            )
+            for kk in range(2)
+            for zi in range(nz)
+        ]
+        for which in range(pairs)
+    ]
+    r_copies = [
+        pltpu.make_async_copy(
+            rights[which].at[:, pl.ds(col, step)], right.at[n, :, pl.ds(0, step)], r_fill.at[n]
+        )
+        for n, (which, col, _ti, _out, step) in enumerate(plan)
+    ]
+    for n, (which, _col, _ti, _out, _step) in enumerate(plan):
+        if n == 0 or plan[n - 1][0] != which:
+            for one in l_copies[which]:
+                one.start()
+        r_copies[n].start()
+    greet([core_dev])
+
+    def exchange(n):
+        step = plan[n][4]
+        cut = pl.ds(0, step)
+        return remote(away.at[n, :, :, cut], near.at[n, :, :, cut], send.at[n], recv.at[n], core_dev)
+
+    sub = 256
+    for n, (which, _col, _ti, _out, step) in enumerate(plan):
+        if n == 0 or plan[n - 1][0] != which:
+            for one in l_copies[which]:
+                one.wait()
+        r_copies[n].wait()
+
+        @pl.loop(0, step // sub)
+        def _(j, n=n, which=which):
+            cut = aligned(j * sub, sub)
+            for zi in range(nz):
+                away[n, zi, :, cut] = mm(left[which, 0, zi], right[n, :, cut]).astype(BF)
+
+        exchange(n).start()
+
+    outs = []
+    for n, (which, _col, ti, out, step) in enumerate(plan):
+        exchange(n).wait_recv()
+        slot = n % 2
+        if n >= 2:
+            for one in outs[n - 2]:
+                one.wait()
+
+        @pl.loop(0, step // sub)
+        def _(j, n=n, which=which, slot=slot):
+            cut = aligned(j * sub, sub)
+            for zi in range(nz):
+                stage[slot, zi, :, cut] = (
+                    mm(left[which, 1, zi], right[n, :, cut]) + near[n, zi, :, cut].astype(F32)
+                ).astype(BF)
+
+        outs.append(
+            [
+                pltpu.make_async_copy(
+                    stage.at[slot, zi, :, pl.ds(0, step)],
+                    packed.at[pl.ds((ti * nz + zi) * dblk, dblk), pl.ds(out, step)],
+                    out_sems.at[slot, zi],
+                )
+                for zi in range(nz)
+            ]
+        )
+        for one in outs[n]:
+            one.start()
+    for group in outs[-2:]:
+        for one in group:
+            one.wait()
+    for n in range(len(plan)):
+        exchange(n).wait_send()
+
+
+def grads_layer(operands, nz, nt, collective_id):
+    pairs = len(operands) // 2
+    width, span = operands[0].shape
+    chunk = 1024
+    dblk = width // (2 * nz)
+    sizes = [one.shape[1] // nt for one in operands[1::2]]
+    count = sum(nt * max(1, size // chunk) for size in sizes)
+    dma = pltpu.SemaphoreType.DMA
+    hbm = pl.BlockSpec(memory_space=pl.ANY)
+    return pl.pallas_call(
+        functools.partial(grads_kernel, pairs=pairs, nz=nz, nt=nt, chunk=chunk),
+        out_shape=jax.ShapeDtypeStruct((nt * nz * dblk, sum(sizes)), BF),
+        in_specs=[hbm] * len(operands),
+        out_specs=hbm,
+        scratch_shapes=[
+            pltpu.VMEM((pairs, 2, nz, dblk, span), BF),
+            pltpu.VMEM((count, span, chunk), BF),
+            pltpu.VMEM((count, nz, dblk, chunk), BF),
+            pltpu.VMEM((count, nz, dblk, chunk), BF),
+            pltpu.VMEM((2, nz, dblk, chunk), BF),
+            dma((pairs, 2, nz)),
+            dma((count,)),
+            dma((count,)),
+            dma((count,)),
+            dma((2, nz)),
+        ],
+        compiler_params=pltpu.CompilerParams(
+            collective_id=collective_id, has_side_effects=True, vmem_limit_bytes=60 << 20
+        ),
+        cost_estimate=pl.CostEstimate(
+            flops=2 * span * width * nt * sum(sizes), bytes_accessed=40 << 20, transcendentals=0
+        ),
+        name="grads_layer",
+    )(*operands)
 
 
 def on_device_rows(
@@ -699,31 +1599,11 @@
     pieces = [qv_bias, up_bias, proj_bias, first_gain, first_shift, down_bias, second_gain, second_shift]
     small = jnp.concatenate([p.reshape(-1, 128) for p in pieces])
     up_at, vec_at = qv_bias.size // 128, (qv_bias.size + up_bias.size) // 128
-    small = jnp.pad(small, ((0, -small.shape[0] % 16), (0, 0)))
-    small = lax.all_gather(small, AXES[:2] + AXES[3:])
+    small = jnp.pad(small, ((0, -(small.shape[0] + 2) % 16 + 2), (0, 0)))
+    own_seg = jnp.where(t == 0, segment_ids[0], segment_ids[1])
+    other_seg = over_x(own_seg)
+    rows_t, qkv_full, qkv, small = open_layer(tokens, qkv_weight, small, nz, nt, heads, head_size, group)
     small = small.reshape(nf, nt, -1, 128)
-
-    own_rows = jnp.where(t == 0, tokens[0], tokens[1])
-    own_seg = jnp.where(t == 0, segment_ids[0], segment_ids[1])
-    other_rows = over_x(own_rows)
-    other_seg = over_x(own_seg)
-    columns = []
-    for first in range(0, pairs, group):
-        for which in range(3):
-            columns.append(qkv_weight[which][:, first * wide : (first + group) * wide])
-    qkv_shard = jnp.concatenate(columns, axis=1)
-    swapped = send(qkv_shard, lambda zi, ki, ci, ti: (zi, ki, ci, 1 - ti) if ti == ci else None)
-    qkv_shard = jnp.where(t == c, qkv_shard, swapped)
-    qkv_near = z_all(qkv_shard)
-    qkv_blocks = qkv_near + [over_core(b) for b in qkv_near]
-
-    def place_rows(out, i):
-        kk, d = i // nz, i % nz
-        src = lax.rem(lax.axis_index("z") + nz - d, nz) * 2 + lax.rem(lax.axis_index("core") + kk, 2)
-        return out.at[pl.ds(pl.multiple_of(src * dblk, dblk), dblk), :]
-
-    qkv_full = assemble([b[None] for b in qkv_blocks], (width, 3 * cols), place_rows)
-
     edge = head_size // nf
 
     def interleave(rows, columns):
@@ -734,50 +1614,18 @@
         mine = col % head_size // edge == lax.broadcasted_iota(jnp.int32, (nf, columns), 0)
         return jnp.sum(jnp.where(mine, spread_out, 0.0), axis=0)
 
-    qv_rows = jnp.where(c == 0, small[:, 0, :up_at], small[:, 1, :up_at]).reshape(nf, -1)
-    per_kind = qv_rows.shape[1] // 2
-    qv_all = [interleave(qv_rows[:, i * per_kind : (i + 1) * per_kind], cols) for i in range(2)]
     up_add = jnp.concatenate(
         [interleave(small[:, i, up_at:vec_at].reshape(nf, -1), hidden // nt) for i in range(nt)]
-    )
-    proj_add, gain_one, shift_one, down_add, gain_two, shift_two = (
-        small[:, 0, vec_at + i].reshape(width).astype(F32) for i in range(6)
-    )
-    add_parts = [qv_all[0], jnp.zeros_like(qv_all[0]), qv_all[1]]
-    qkv_add = jnp.concatenate(
-        [add_parts[w][i * wide : (i + group) * wide] for i in range(0, pairs, group) for w in range(3)]
-    )
-
-    def place_grid(rows_by_f, rows, columns):
-        def place(out, i):
-            kk, zi, ti = i // (nz * nt), i // nt % nz, i % nt
-            src = zi * 2 + lax.rem(lax.axis_index("core") + kk, 2)
-            first, second = (src, ti) if rows_by_f else (ti, src)
-            return out.at[
-                pl.ds(pl.multiple_of(first * rows, rows), rows),
-                pl.ds(pl.multiple_of(second * columns, columns), columns),
-            ]
-
-        return place
-
-    def spread(shard):
-        mine = lax.all_gather(shard, ("z", "tensor"))
-        return mine, over_core(mine)
-
-    def settle(halves, shape, place):
-        return assemble(halves, shape, place)
-
-    proj_all = spread(proj_weight)
-    up_all = spread(up_weight)
-    down_all = spread(down_weight)
-    proj_full = settle(proj_all, (width, width), place_grid(False, *proj_weight.shape))
-    up_full = settle(up_all, (width, hidden), place_grid(True, *up_weight.shape))
-    down_full = settle(down_all, (hidden, width), place_grid(False, *down_weight.shape))
-
-    rows_all = jnp.concatenate([own_rows, other_rows])
+    ).reshape(1, hidden)
+    vecs = small[:, 0, vec_at : vec_at + 8].transpose(1, 0, 2).reshape(8, width).astype(F32)
+
+    every = AXES[:2] + AXES[3:]
+    up_shard = jnp.concatenate([up_weight, proj_weight.T], axis=1)
+    up_all = lax.all_gather(up_shard, every).reshape((-1,) + up_shard.shape)
+    down_all = lax.all_gather(after(down_weight, up_shard), every).reshape((-1,) + down_weight.shape)
+
     seg_store = jnp.concatenate([own_seg, other_seg])
     seg_global = ordered(c, own_seg, other_seg)
-    qkv = (mm(rows_all, qkv_full) + qkv_add).astype(BF)
     total = 2 * span
     blk = 256
     low, high = segment_bounds(seg_global, blk, blk)
@@ -791,97 +1639,46 @@
         mixed.append(out)
         lse.append(one)
         mixed_other.append(over_x(out[span:]))
+    up_all, _last = lax.optimization_barrier((up_all, mixed[-1]))
     context_rows = ordered(
         c, jnp.concatenate([m[:span] for m in mixed], 1), jnp.concatenate(mixed_other, 1), 1
     )
 
-    token_f32 = own_rows.astype(F32)
-    n_one, inv_one = norm_forward(token_f32 + (mm(context_rows, proj_full) + proj_add))
-    first = n_one * gain_one + shift_one
-    first_low = first.astype(BF)
-    hidden_pre = mm(first_low, up_full) + up_add
-    act, gelu_pull = jax.vjp(exact_gelu, hidden_pre)
-    act_low = act.astype(BF)
-    n_two, inv_two = norm_forward(first + (mm(act_low, down_full) + down_add))
-    out_low = (n_two * gain_two + shift_two).astype(BF)
+    which = t.reshape(1)
+    first, norm_one, inv_one, first_t, act_low, slope = up_layer(
+        which, context_rows, tokens, vecs, up_add, up_all, nt
+    )
+    down_all, first = lax.optimization_barrier((down_all, first))
+    out_low, branch, branch_t, grad_second, vec_two = down_layer(
+        which, out_grad, vecs, first, act_low, down_all, nt
+    )
+    down_sum = grads_layer([branch_t, act_low], nz, nt, 2)
+    branch, down_sum = lax.optimization_barrier((branch, down_sum))
+    hidden_low, attn_t, grad_in, grad_context, vec_one, up_sums = back_layer(
+        vecs, branch, grad_second, slope, norm_one, inv_one, up_all, down_all, nt
+    )
     layer_output = ordered(t, out_low[None], over_y(out_low)[None])
-
-    cot = jnp.where(t == 0, out_grad[0], out_grad[1]).astype(F32)
-    grad_gain_two = jnp.sum(cot * n_two, axis=0)
-    grad_shift_two = jnp.sum(cot, axis=0)
-    grad_second = norm_backward(cot * gain_two, n_two, inv_two)
-    branch_low = grad_second.astype(BF)
-    grad_down_bias = jnp.sum(branch_low.astype(F32), axis=0)
-    hidden_low = gelu_pull(mm_nt(branch_low, down_full))[0].astype(BF)
-    grad_up_bias = jnp.sum(hidden_low.astype(F32), axis=0)
-    grad_first = grad_second + mm_nt(hidden_low, up_full)
-    grad_gain_one = jnp.sum(grad_first * n_one, axis=0)
-    grad_shift_one = jnp.sum(grad_first, axis=0)
-    grad_in = norm_backward(grad_first * gain_one, n_one, inv_one)
-    attn_low = grad_in.astype(BF)
-    grad_proj_bias = jnp.sum(attn_low.astype(F32), axis=0)
-    grad_context = mm_nt(attn_low, proj_full).astype(BF)
     halves = grad_context[:, :cols], grad_context[:, cols:]
     dctx_own = jnp.where(c == 0, halves[0], halves[1])
     dctx_other = over_x(jnp.where(c == 0, halves[1], halves[0]))
     dctx = jnp.concatenate([dctx_own, dctx_other])
 
-    zorder = sorted(range(nz), key=lambda zi: int(format(zi, "0%db" % zbits)[::-1], 2)) if zbits else [0]
-
-    def pick_k(a, kk):
-        even = jnp.concatenate([a[:, (2 * zi) * dblk : (2 * zi + 1) * dblk] for zi in zorder], axis=1)
-        odd = jnp.concatenate([a[:, (2 * zi + 1) * dblk : (2 * zi + 2) * dblk] for zi in zorder], axis=1)
-        return jnp.where(kk == 0, even, odd)
-
-    def pick_plain(a, kk):
-        even = jnp.concatenate([a[:, (2 * zi) * dblk : (2 * zi + 1) * dblk] for zi in range(nz)], axis=1)
-        odd = jnp.concatenate([a[:, (2 * zi + 1) * dblk : (2 * zi + 2) * dblk] for zi in range(nz)], axis=1)
-        return jnp.where(kk == 0, even, odd)
-
-    def half(a, index, axis):
-        size = a.shape[axis] // 2
-        return lax.dynamic_slice_in_dim(a, index * size, size, axis)
-
-    def halve(a, index, axis, across):
-        got = across(half(a, 1 - index, axis))
-        return (half(a, index, axis).astype(F32) + got.astype(F32)).astype(BF)
-
-    def z_halve(a, axis):
-        for bit in range(zbits):
-            a = halve(a, (z >> bit) & 1, axis, functools.partial(over_zbit, bit=bit))
-        return a
-
-    def tensor_sum(left, right):
-        out = []
-        for kk in (1 - k, k):
-            mine = pick_plain(left, kk)
-            size = right.shape[1] // nt
-            out.append([mm_tn(mine, right[:, i * size : (i + 1) * size]) for i in range(nt)])
-        got = over_core(jnp.concatenate(out[0]).astype(BF))
-        return (jnp.concatenate(out[1]) + got.astype(F32)).astype(BF)
-
-    down_sum = tensor_sum(branch_low, act_low)
-    up_sum = tensor_sum(first_low, hidden_low)
-    proj_sum = tensor_sum(attn_low, context_rows)
-    dctx, down_sum, up_sum, proj_sum = lax.optimization_barrier((dctx, down_sum, up_sum, proj_sum))
-    widths = [p.shape[1] for p in (down_sum, up_sum, proj_sum)]
-    packed = jnp.concatenate([down_sum, up_sum, proj_sum], axis=1)
-    gather = lax.psum_scatter(packed, ("tensor", "z", "context"), scatter_dimension=0, tiled=True)
-    gather = ordered(c, gather, over_x(gather), 0).astype(F32)
-    grad_down = gather[:, : widths[0]].T
-    grad_up = gather[:, widths[0] : widths[0] + widths[1]]
-    grad_proj = gather[:, widths[0] + widths[1] :].T
-
-    def total_sum(v):
-        v = v + over_core(v)
-        for bit in range(zbits):
-            v = v + over_zbit(v, bit)
-        return v + over_y(v)
-
-    vectors = [grad_proj_bias, grad_gain_one, grad_shift_one, grad_down_bias, grad_gain_two, grad_shift_two]
-    sums = jnp.concatenate(vectors + [grad_up_bias]).reshape(-1, 128)
-    sums = total_sum(sums)
-    sums = (sums + over_x(sums)).reshape(-1)
+    other_sum = grads_layer([first_t, hidden_low, attn_t, context_rows], nz, nt, 3)
+    dctx, other_sum = lax.optimization_barrier((dctx, other_sum))
+    part = lax.psum_scatter(down_sum, ("tensor", "z"), scatter_dimension=0, tiled=True)
+    grad_down = (part.astype(F32) + over_x(part).astype(F32)).T
+    part = lax.psum_scatter(other_sum, ("tensor", "z", "context"), scatter_dimension=0, tiled=True)
+    part = ordered(c, part, over_x(part), 0).astype(F32)
+    grad_up = part[:, : hidden // nt]
+    grad_proj = part[:, hidden // nt :].T
+
+    sums = jnp.concatenate([vec_one[:3].reshape(-1, 128), vec_two[:3].reshape(-1, 128), up_sums[0].reshape(-1, 128)])
+    dqkv = None
+    for p in range(pairs):
+        dqkv = attn_bwd(dqkv, qkv, mixed[p], dctx, lse[p], *attn_args, p, pairs, group, head_size, blk, blk)
+    tokens_grad, qkv_rows, qv_sum = close_layer(dqkv, qkv_full, rows_t, grad_in, sums, nz)
+    sums = qv_sum[-sums.shape[0] :].reshape(-1)
+    qv_sum = qv_sum[: 3 * cols // 128].reshape(-1)
     vector_out = [
         lax.dynamic_slice_in_dim(sums[i * width : (i + 1) * width], f * dblk, dblk) for i in range(6)
     ]
@@ -889,39 +1686,6 @@
     bias_up = sums[6 * width :].reshape(nt * up_rows, nf * up_cols)
     bias_up = lax.dynamic_slice(bias_up, (t * up_rows, f * up_cols), (up_rows, up_cols))
 
-    def reduce_qkv(part):
-        sent = mm_tn(pick_k(rows_all, 1 - k), part).astype(BF)
-        kept = mm_tn(pick_k(rows_all, k), part)
-        g = (kept + over_core(sent).astype(F32)).astype(BF)
-        g = z_halve(g, 0)
-        g = halve(g, t, 0, over_y)
-        near = send(g, lambda zi, ki, ci, ti: (zi, ki, 1 - ci, ci) if ci == ti else (zi, ki, ci, ci))
-        far = send(g, lambda zi, ki, ci, ti: (zi, ki, 1 - ci, ci) if ci != ti else None)
-        return jnp.where(
-            c == t,
-            jnp.where(t == 0, jnp.concatenate([g, near]), jnp.concatenate([near, g])),
-            jnp.where(t == 0, jnp.concatenate([near, far]), jnp.concatenate([far, near])),
-        )
-
-    dqkv, qkv_parts = None, []
-    for p in range(pairs):
-        dqkv = attn_bwd(dqkv, qkv, mixed[p], dctx, lse[p], *attn_args, p, pairs, group, head_size, blk, blk)
-        if (p + 1) % group == 0 and p + 1 < pairs:
-            lo_col = (p + 1 - group) * 3 * wide
-            part = reduce_qkv(dqkv[:, lo_col : lo_col + 3 * group * wide])
-            qkv_parts.append(part)
-    chunks = 4
-    step = span // chunks
-    away = mm_nt(dqkv[span:], qkv_full).astype(BF)
-    got = [over_x(away[i * step : (i + 1) * step]) for i in range(chunks)]
-    stay = mm_nt(dqkv[:span], qkv_full) + grad_in
-    final = [
-        (stay[i * step : (i + 1) * step] + got[i].astype(F32)).astype(BF) for i in range(chunks)
-    ]
-    final_other = [over_y(part) for part in final]
-    tokens_grad = ordered(t, jnp.concatenate(final)[None], jnp.concatenate(final_other)[None])
-    qkv_parts.append(reduce_qkv(dqkv[:, (pairs - group) * 3 * wide :]))
-    qkv_rows = jnp.concatenate(qkv_parts, axis=1)
 
     def unpack(rows, which):
         return jnp.concatenate(
@@ -929,10 +1693,8 @@
             axis=-1,
         )
 
-    grad_qkv = jnp.stack([unpack(qkv_rows, which) for which in range(3)]).astype(F32)
-    qv_sum = jnp.sum(dqkv.astype(F32), axis=0)
-    qv_sum = total_sum(jnp.concatenate([unpack(qv_sum, 0), unpack(qv_sum, 2)]).reshape(-1, 128))
-    qv_sum = jnp.where(t == c, qv_sum, over_x(qv_sum)).reshape(2, heads, head_size)
+    grad_qkv = jnp.stack([unpack(qkv_rows, which) for which in range(3)])
+    qv_sum = jnp.concatenate([unpack(qv_sum, 0), unpack(qv_sum, 2)]).reshape(2, heads, head_size)
     grad_qv = lax.dynamic_slice_in_dim(qv_sum, f * (head_size // nf), head_size // nf, 2)
 
     return (

time: 779 us -> 601 us (0.77)
  Pallas kernels: 160 us -> 491 us
  matrix products: 184 us -> 0.91 us
  waiting for transfers between devices: 157 us -> 16.3 us
  starting transfers between devices: 70 us -> 11.5 us
  local copies, waits for them, and re-layouts: 94.5 us -> 36.1 us
  other arithmetic: 60.7 us -> 17.8 us
  blocking collectives: 25.5 us -> 0 us
    pallas_call x4 -> x7, Pallas kernels: 12.5 us -> 334 us  [the longest x1 107 us: close_layer(): pl.pallas_call(functools.partial(close_kernel, nz=nz, chunk=chunk, tile=t...]
    ppermute x53 -> x9, waiting for transfers between devices: 155 us -> 15.5 us  [send(): return lax.ppermute(value, AXES, pairs)]
    dot_general x21 -> x0, matrix products: 105 us -> none  [the longest x5 53.7 us: mm_nt(): lax.dot_general(a, b, (((1,), (1,)), ((), ())), preferred_element_type=F32)]
    dot_general x8 -> x2, matrix products: 78.8 us -> 0.91 us  [mm(): return jnp.dot(a, b, preferred_element_type=F32)]
    ppermute x53 -> x9, starting transfers between devices: 69.8 us -> 11.3 us  [send(): return lax.ppermute(value, AXES, pairs)]
    unnamed x351 -> x75, local copies, waits for them, and re-layouts: 71.1 us -> 24.5 us
    all_gather x1 -> x0, blocking collectives: 25.5 us -> none  [on_device_rows(): small = lax.all_gather(small, AXES[:2] + AXES[3:])]
    convert_element_type x14 -> x2, other arithmetic: 18.4 us -> 0.75 us  [the longest x1 0.62 us: on_device_rows(): small[:, 0, vec_at:vec_at + 8].transpose(1, 0, 2).reshape(8, width)]
  transfers between devices with their start and end apart: 57 -> 13, of which waited for: 23 -> 3; matrix products, arithmetic and copies ran while one was open for 28% -> 5% of each run, Pallas kernels for 20% -> 76%
where the time goes in v2:
time: 601 us; the launch traced here: 589 us
  Pallas kernels  491 us (82%)
  local copies, waits for them, and re-layouts  36.1 us (6%)
  other arithmetic  17.8 us (3%)
  waiting for transfers between devices  16.3 us (3%)
  between operations  14.8 us (2%)
  starting transfers between devices  11.5 us (2%)
    pallas_call x1, Pallas kernels, close_layer(): pl.pallas_call(functools.partial(close_kernel, nz=nz, chunk=chunk, tile=t...  107 us
    pallas_call x4, Pallas kernels, attn_bwd(): pl.pallas_call(body, out_shape=jax.ShapeDtypeStruct(qkv.shape, BF), grid_...  91.7 us
    pallas_call x1, Pallas kernels, open_layer(): pl.pallas_call(functools.partial(open_kernel, nz=nz, nt=nt, heads=heads,...  79.7 us
    pallas_call x4, Pallas kernels, attn_fwd(): pl.pallas_call(functools.partial(attn_fwd_kernel, bq=bq, bk=bk, hd=head_s...  65.5 us
    pallas_call x1, Pallas kernels, back_layer(): pl.pallas_call(functools.partial(back_kernel, nt=nt, tile=tile), out_shap...  47.8 us
    pallas_call x2, Pallas kernels, grads_layer(): pl.pallas_call(functools.partial(grads_kernel, pairs=pairs, nz=nz, nt=nt,...  41.5 us
    pallas_call x1, Pallas kernels, up_layer(): pl.pallas_call(functools.partial(up_kernel, nt=nt, tile=tile), out_shape=...  33.5 us
    unnamed x75, local copies, waits for them, and re-layouts  24.5 us
  transfers between devices with their start and end apart: 13, of which 3 were waited for; matrix products, arithmetic and copies ran while one was open for 5% of the time, Pallas kernels for 76%

profile of v2, /device:TPU:28, one launch (start us, length us, event | category | flops | bytes accessed | tf_op | source)
XLA Modules:
  0.0 588.6 jit_solution(147166627569705968)
XLA Ops:
  16.6 79.7 %open_layer.1 = (bf16[1024,2048]{1,0:T(8,128)(2,1)S(1)}, bf16[1024,1536]{1,0:T(8,128)(2,1)S(1)}, bf16[2048,1536]{1,0:T(8,128)(2,1)}, bf16[16,16,128]{2,1,0:T(8,128)(2,1)S(1)}) custom-call(bf16[2,1024,1024]{2,1,0:T(8,128)(2,1)S(1)} %copy-done.8, bf16[3,128,512]{2,1,0:T(8,128)(2,1)S(1)} %copy-done.9, bf16[16,128]{1,0:T(8,128)(2,1)S(1)} %pad.4.small), custom_call_target="tpu_custom_call" | custom-call | flops 6442450944 | bytes 16777216 | tf_op jit(solution)/shard_map/open_layer/pallas_call | solution.py:795
  101.3 2.8 copy-done.10
  104.1 16.4 %attn_fwd.4 = (bf16[2048,128]{1,0:T(8,128)(2,1)S(1)}, f32[1,2,2048]{2,1,0:T(2,128)S(1)}) custom-call(s32[8]{0:T(128)S(1)} %get-tuple-element.187.lo_ref.refs_0_, s32[8]{0:T(128)S(1)} %get-tuple-element.186.hi_ref.refs_1_, s32[1]{0:T(128)} %bitcast.14.shift_ref.refs_2_, bf16[2048,1536]{1,0:T(8,128)(2,1)S(1)} %copy-done.10, bf16[2048,1536]{1,0:T(8,128)(2,1)S(1)} %copy-done.10, ...), custom_call_target="tpu_custom_call" | custom-call | flops 15000000512 | bytes 2097152 | tf_op jit(solution)/shard_map/attn_fwd/pallas_call | solution.py:466
  120.6 16.4 %attn_fwd.5 = (bf16[2048,128]{1,0:T(8,128)(2,1)S(1)}, f32[1,2,2048]{2,1,0:T(2,128)S(1)}) custom-call(s32[8]{0:T(128)S(1)} %get-tuple-element.187.lo_ref.refs_0_, s32[8]{0:T(128)S(1)} %get-tuple-element.186.hi_ref.refs_1_, s32[1]{0:T(128)} %bitcast.14.shift_ref.refs_2_, bf16[2048,1536]{1,0:T(8,128)(2,1)S(1)} %copy-done.10, bf16[2048,1536]{1,0:T(8,128)(2,1)S(1)} %copy-done.10, ...), custom_call_target="tpu_custom_call" | custom-call | flops 15000000512 | bytes 2097152 | tf_op jit(solution)/shard_map/attn_fwd/pallas_call | solution.py:466
  139.1 16.4 %attn_fwd.6 = (bf16[2048,128]{1,0:T(8,128)(2,1)S(1)}, f32[1,2,2048]{2,1,0:T(2,128)S(1)}) custom-call(s32[8]{0:T(128)S(1)} %get-tuple-element.187.lo_ref.refs_0_, s32[8]{0:T(128)S(1)} %get-tuple-element.186.hi_ref.refs_1_, s32[1]{0:T(128)} %bitcast.14.shift_ref.refs_2_, bf16[2048,1536]{1,0:T(8,128)(2,1)S(1)} %copy-done.10, bf16[2048,1536]{1,0:T(8,128)(2,1)S(1)} %copy-done.10, ...), custom_call_target="tpu_custom_call" | custom-call | flops 15000000512 | bytes 2097152 | tf_op jit(solution)/shard_map/attn_fwd/pallas_call | solution.py:466
  155.7 16.4 %attn_fwd.7 = (bf16[2048,128]{1,0:T(8,128)(2,1)S(1)}, f32[1,2,2048]{2,1,0:T(2,128)S(1)}) custom-call(s32[8]{0:T(128)S(1)} %get-tuple-element.187.lo_ref.refs_0_, s32[8]{0:T(128)S(1)} %get-tuple-element.186.hi_ref.refs_1_, s32[1]{0:T(128)} %bitcast.14.shift_ref.refs_2_, bf16[2048,1536]{1,0:T(8,128)(2,1)S(1)} %copy-done.10, bf16[2048,1536]{1,0:T(8,128)(2,1)S(1)} %copy-done.10, ...), custom_call_target="tpu_custom_call" | custom-call | flops 15000000512 | bytes 2097152 | tf_op jit(solution)/shard_map/attn_fwd/pallas_call | solution.py:466
  174.5 4.1 collective-permute-done.4
  181.3 33.5 %up_layer.1 = (f32[1024,1024]{1,0:T(8,128)}, f32[1024,1024]{1,0:T(8,128)}, f32[1024,128]{1,0:T(8,128)}, bf16[1024,1024]{1,0:T(8,128)(2,1)}, bf16[1024,4096]{1,0:T(8,128)(2,1)}, /*index=5*/bf16[1024,4096]{1,0:T(8,128)(2,1)}) custom-call(s32[1]{0:T(128)} %bitcast.t_ref, bf16[1024,1024]{1,0:T(8,128)(2,1)} %broadcast_select_fusion.ctx.refs_3_, ...), custom_call_target="tpu_custom_call" | custom-call | flops 10737418240 | bytes 41943040 | tf_op jit(solution)/shard_map/up_layer/pallas_call | solution.py:1155
  214.8 24.2 %down_layer.1 = (bf16[1024,1024]{1,0:T(8,128)(2,1)}, bf16[1024,1024]{1,0:T(8,128)(2,1)}, bf16[1024,1024]{1,0:T(8,128)(2,1)}, f32[1024,1024]{1,0:T(8,128)}, f32[8,1024]{1,0:T(8,128)}) custom-call(s32[1]{0:T(128)} %bitcast.t_ref, bf16[2,1024,1024]{2,1,0:T(8,128)(2,1)} %cot.1, f32[8,1024]{1,0:T(8,128)} %convert_bitcast_fusion.vecs, ...), custom_call_target="tpu_custom_call" | custom-call | flops 8589934592 | bytes 31457280 | tf_op jit(solution)/shard_map/down_layer/pallas_call | solution.py:1254
  238.9 19.4 %grads_layer.2 = bf16[1024,2048]{1,0:T(8,128)(2,1)} custom-call(bf16[1024,1024]{1,0:T(8,128)(2,1)} %get-tuple-element.68.refs_0_, bf16[1024,4096]{1,0:T(8,128)(2,1)} %get-tuple-element.64.act.refs_1_), custom_call_target="tpu_custom_call" | custom-call | flops 8589934592 | bytes 41943040 | tf_op jit(solution)/shard_map/grads_layer/pallas_call | solution.py:1497
  258.4 47.8 %back_layer.1 = (bf16[1024,4096]{1,0:T(8,128)(2,1)}, bf16[1024,1024]{1,0:T(8,128)(2,1)}, f32[1024,1024]{1,0:T(8,128)}, bf16[1024,1024]{1,0:T(8,128)(2,1)}, f32[8,1024]{1,0:T(8,128)}, /*index=5*/f32[8,4096]{1,0:T(8,128)}) custom-call(f32[8,1024]{1,0:T(8,128)} %convert_bitcast_fusion.vecs, bf16[1024,1024]{1,0:T(8,128)(2,1)} %get-tuple-element.69.branch, ...), custom_call_target="tpu_custom_call" | custom-call | flops 19327352832 | bytes 62914560 | tf_op jit(solution)/shard_map/back_layer/pallas_call | solution.py:1350
  313.2 22.1 %grads_layer.3 = bf16[1024,2560]{1,0:T(8,128)(2,1)} custom-call(bf16[1024,1024]{1,0:T(8,128)(2,1)} %get-tuple-element.75.refs_0_, bf16[1024,4096]{1,0:T(8,128)(2,1)} %get-tuple-element.76.refs_1_, bf16[1024,1024]{1,0:T(8,128)(2,1)} %get-tuple-element.77.refs_2_, bf16[1024,1024]{1,0:T(8,128)(2,1)} %broadcast_select_fusion.ctx.refs_3_), custom_call_target="tpu_custom_call" | custom-call | flops 10737418240 | bytes 41943040 | tf_op jit(solution)/shard_map/grads_layer/pallas_call | solution.py:1497
  339.1 3.1 copy-done.11
  342.2 22.9 %attn_bwd.4.refs_11_ = bf16[2048,1536]{1,0:T(8,128)(2,1)S(1)} custom-call(s32[8]{0:T(128)S(1)} %get-tuple-element.187.lo_ref.refs_0_, s32[8]{0:T(128)S(1)} %get-tuple-element.186.hi_ref.refs_1_, s32[1]{0:T(128)} %bitcast.14.shift_ref.refs_2_, bf16[2048,1536]{1,0:T(8,128)(2,1)S(1)} %copy-done.11, bf16[2048,1536]{1,0:T(8,128)(2,1)S(1)} %copy-done.11, ...), custom_call_target="tpu_custom_call" | custom-call | flops 24999999488 | bytes 4194304 | tf_op jit(solution)/shard_map/attn_bwd/pallas_call | solution.py:524
  365.1 22.9 %attn_bwd.5.refs_11_ = bf16[2048,1536]{1,0:T(8,128)(2,1)S(1)} custom-call(s32[8]{0:T(128)S(1)} %get-tuple-element.187.lo_ref.refs_0_, s32[8]{0:T(128)S(1)} %get-tuple-element.186.hi_ref.refs_1_, s32[1]{0:T(128)} %bitcast.14.shift_ref.refs_2_, bf16[2048,1536]{1,0:T(8,128)(2,1)S(1)} %copy-done.11, ...), custom_call_target="tpu_custom_call", output_to_operand_aliasing={{}: (11, {})} | custom-call | flops 24999999488 | bytes 4194304 | tf_op jit(solution)/shard_map/attn_bwd/pallas_call | solution.py:524
  388.0 23.0 %attn_bwd.6.refs_11_ = bf16[2048,1536]{1,0:T(8,128)(2,1)S(1)} custom-call(s32[8]{0:T(128)S(1)} %get-tuple-element.187.lo_ref.refs_0_, s32[8]{0:T(128)S(1)} %get-tuple-element.186.hi_ref.refs_1_, s32[1]{0:T(128)} %bitcast.14.shift_ref.refs_2_, bf16[2048,1536]{1,0:T(8,128)(2,1)S(1)} %copy-done.11, ...), custom_call_target="tpu_custom_call", output_to_operand_aliasing={{}: (11, {})} | custom-call | flops 24999999488 | bytes 4194304 | tf_op jit(solution)/shard_map/attn_bwd/pallas_call | solution.py:524
  411.1 22.9 %attn_bwd.7.dqkv_in = bf16[2048,1536]{1,0:T(8,128)(2,1)S(1)} custom-call(s32[8]{0:T(128)S(1)} %get-tuple-element.187.lo_ref.refs_0_, s32[8]{0:T(128)S(1)} %get-tuple-element.186.hi_ref.refs_1_, s32[1]{0:T(128)} %bitcast.14.shift_ref.refs_2_, bf16[2048,1536]{1,0:T(8,128)(2,1)S(1)} %copy-done.11, ...), custom_call_target="tpu_custom_call", output_to_operand_aliasing={{}: (11, {})} | custom-call | flops 24999999488 | bytes 4194304 | tf_op jit(solution)/shard_map/attn_bwd/pallas_call | solution.py:524
  434.0 2.7 copy-done.14
  436.6 107.4 %close_layer.1 = (bf16[2,1024,1024]{2,1,0:T(8,128)(2,1)}, f32[128,1536]{1,0:T(8,128)}, f32[96,128]{1,0:T(8,128)}) custom-call(bf16[2048,1536]{1,0:T(8,128)(2,1)} %copy-done.14, bf16[1024,1536]{1,0:T(8,128)(2,1)} %copy-done.13, bf16[1024,2048]{1,0:T(8,128)(2,1)} %copy-done.12, f32[1024,1024]{1,0:T(8,128)} %get-tuple-element.85.grad_in, ...), custom_call_target="tpu_custom_call" | custom-call | flops 12884901888 | bytes 31457280 | tf_op jit(solution)/shard_map/close_layer/pallas_call | solution.py:1024
  553.0 2.7 collective-permute-start.8
  556.3 5.9 %maximum_select_fusion = bf16[2,1024,1024]{2,1,0:T(8,128)(2,1)} fusion(bf16[1,1024,1024]{2,1,0:T(8,128)(2,1)} %bitcast.20, bf16[1,1024,1024]{2,1,0:T(8,128)(2,1)} %bitcast.19, pred[]{:T(512)S(6)} %eq.29), kind=kLoop, calls=%fused_computation | loop fusion | flops 6291456 | bytes 8388609 | tf_op jit(solution)/shard_map/jit(_where)/select_n | solution.py:1586
  562.4 6.2 %collective-permute-done.8 = bf16[128,2048]{1,0:T(8,128)(2,1)S(1)} collective-permute-done((bf16[128,2048]{1,0:T(8,128)(2,1)}, bf16[128,2048]{1,0:T(8,128)(2,1)S(1)}, u32[]{:S(2)}, u32[]{:S(2)}) %collective-permute-start.8) | collective-permute-done | bytes 524320 | tf_op jit(solution)/shard_map/ppermute | solution.py:1557
  570.0 5.2 collective-permute-done.7
  577.3 4.6 copy.88
  (160 shorter events, 45.2 us)
Async XLA Ops:
  7.2 7.0 %copy-start.23 = (bf16[128]{0:T(256)(128)(2,1)S(1)}, bf16[128]{0:T(256)(128)(2,1)}, u32[]{:S(2)}) copy-start(bf16[128]{0:T(256)(128)(2,1)} %param.20) | copy-start | bytes 772
  7.3 7.1 %copy-start.9 = (bf16[3,128,512]{2,1,0:T(8,128)(2,1)S(1)}, bf16[3,128,512]{2,1,0:T(8,128)(2,1)}, u32[]{:S(2)}) copy-start(bf16[3,128,512]{2,1,0:T(8,128)(2,1)} %weight.1) | copy-start | bytes 1179652
  7.3 174.0 %all-gather.7.cloned.1.call-start = ((), (), s32[]{:S(2)}) async-start(), calls=%async_computation.5 | async-start | bytes 11141120 | tf_op jit(solution)/shard_map/all_gather | solution.py:1624
  10.4 204.4 %all-gather.5.cloned.1.call-start = ((), (), s32[]{:S(2)}) async-start(), calls=%async_computation.4 | async-start | bytes 8912896 | tf_op jit(solution)/shard_map/all_gather | solution.py:1625
  11.1 541.8 %reduce-scatter.5.cloned.1.call-start = ((), (), s32[]{:S(2)}) async-start(), calls=%async_computation.3 | async-start | bytes 4718592 | tf_op jit(solution)/shard_map/reduce_scatter | solution.py:1668
  12.4 88.1 %collective-permute-start = (s32[1024]{0:T(1024)S(1)}, s32[1024]{0:T(1024)S(1)}, u32[]{:S(2)}, u32[]{:S(2)}) collective-permute-start(s32[1024]{0:T(1024)S(1)} %bitcast.74), channel_id=1, source_target_pairs={{0,2},{1,3},{2,0},{3,1},{4,6},{5,7},{6,4},{7,5},{8,10},{9,11},{10,... | collective-permute-start | bytes 12296 | tf_op jit(solution)/shard_map/ppermute | solution.py:1557
  120.5 58.1 %copy-start = (bf16[2048,128]{1,0:T(8,128)(2,1)}, bf16[2048,128]{1,0:T(8,128)(2,1)S(1)}, u32[]{:S(2)}) copy-start(bf16[2048,128]{1,0:T(8,128)(2,1)S(1)} %get-tuple-element.57.o_ref) | copy-start | bytes 1572868
  120.5 53.6 %collective-permute-start.1 = (bf16[1024,128]{1,0:T(8,128)(2,1)S(1)}, bf16[1024,128]{1,0:T(8,128)(2,1)S(1)}, u32[]{:S(2)}, u32[]{:S(2)}) collective-permute-start(bf16[1024,128]{1,0:T(8,128)(2,1)S(1)} %slice.184), channel_id=1, source_target_pairs={{0,2},{1,3},{2,0},{3,1},{4,6},{5,7},{6,4},{7,5},{8,10},{9,11},{10,... | collective-permute-start | bytes 786440 | tf_op jit(solution)/shard_map/ppermute | solution.py:1557
  137.0 41.8 %copy-start.2 = (bf16[2048,128]{1,0:T(8,128)(2,1)}, bf16[2048,128]{1,0:T(8,128)(2,1)S(1)}, u32[]{:S(2)}) copy-start(bf16[2048,128]{1,0:T(8,128)(2,1)S(1)} %get-tuple-element.58.refs_6_) | copy-start | bytes 1572868
  137.1 37.2 %collective-permute-start.2 = (bf16[1024,128]{1,0:T(8,128)(2,1)S(1)}, bf16[1024,128]{1,0:T(8,128)(2,1)S(1)}, u32[]{:S(2)}, u32[]{:S(2)}) collective-permute-start(bf16[1024,128]{1,0:T(8,128)(2,1)S(1)} %slice.185), channel_id=1, source_target_pairs={{0,2},{1,3},{2,0},{3,1},{4,6},{5,7},{6,4},{7,5},{8,10},{9,11},{10,... | collective-permute-start | bytes 786440 | tf_op jit(solution)/shard_map/ppermute | solution.py:1557
  155.5 23.4 %copy-start.6 = (bf16[2048,128]{1,0:T(8,128)(2,1)}, bf16[2048,128]{1,0:T(8,128)(2,1)S(1)}, u32[]{:S(2)}) copy-start(bf16[2048,128]{1,0:T(8,128)(2,1)S(1)} %get-tuple-element.59.refs_6_) | copy-start | bytes 1572868
  155.6 18.8 %collective-permute-start.3 = (bf16[1024,128]{1,0:T(8,128)(2,1)S(1)}, bf16[1024,128]{1,0:T(8,128)(2,1)S(1)}, u32[]{:S(2)}, u32[]{:S(2)}) collective-permute-start(bf16[1024,128]{1,0:T(8,128)(2,1)S(1)} %slice.186), channel_id=1, source_target_pairs={{0,2},{1,3},{2,0},{3,1},{4,6},{5,7},{6,4},{7,5},{8,10},{9,11},{10,... | collective-permute-start | bytes 786440 | tf_op jit(solution)/shard_map/ppermute | solution.py:1557
  172.1 7.1 %copy-start.4 = (bf16[2048,128]{1,0:T(8,128)(2,1)}, bf16[2048,128]{1,0:T(8,128)(2,1)S(1)}, u32[]{:S(2)}) copy-start(bf16[2048,128]{1,0:T(8,128)(2,1)S(1)} %get-tuple-element.60.refs_6_) | copy-start | bytes 1572868
  172.1 6.4 %collective-permute-start.4 = (bf16[1024,128]{1,0:T(8,128)(2,1)S(1)}, bf16[1024,128]{1,0:T(8,128)(2,1)S(1)}, u32[]{:S(2)}, u32[]{:S(2)}) collective-permute-start(bf16[1024,128]{1,0:T(8,128)(2,1)S(1)} %slice.187), channel_id=1, source_target_pairs={{0,2},{1,3},{2,0},{3,1},{4,6},{5,7},{6,4},{7,5},{8,10},{9,11},{10,... | collective-permute-start | bytes 786440 | tf_op jit(solution)/shard_map/ppermute | solution.py:1557
  258.3 304.0 %reduce-scatter.3.cloned.1.call-start = ((), (), s32[]{:S(2)}) async-start(), calls=%async_computation.2 | async-start | bytes 5570560 | tf_op jit(solution)/shard_map/reduce_scatter | solution.py:1670
  308.9 26.4 %collective-permute-start.6 = (bf16[1024,512]{1,0:T(8,128)(2,1)S(1)}, bf16[1024,512]{1,0:T(8,128)(2,1)S(1)}, u32[]{:S(2)}, u32[]{:S(2)}) collective-permute-start(bf16[1024,512]{1,0:T(8,128)(2,1)S(1)} %get-tuple-element.157), channel_id=1, source_target_pairs={{0,2},{1,3},{2,0},{3,1},{4,6},{5,7},{6,4},{7,5},{8,10},{9,11},{10,... | collective-permute-start | bytes 3145736 | tf_op jit(solution)/shard_map/ppermute | solution.py:1557
  312.5 243.8 %collective-permute-start.5 = (bf16[1024,1024]{1,0:T(8,128)(2,1)}, bf16[1024,1024]{1,0:T(8,128)(2,1)}, u32[]{:S(2)}, u32[]{:S(2)}) collective-permute-start(bf16[1024,1024]{1,0:T(8,128)(2,1)} %get-tuple-element.66), channel_id=1, source_target_pairs={{0,1},{1,0},{2,3},{3,2},{4,5},{5,4},{6,7},{7,6},{8,9},{9,8},{10,11... | collective-permute-start | bytes 6291464 | tf_op jit(solution)/shard_map/ppermute | solution.py:1557
  342.2 22.9 %copy-start.3 = (bf16[2048,128]{1,0:T(8,128)(2,1)S(1)}, bf16[2048,128]{1,0:T(8,128)(2,1)}, u32[]{:S(2)}) copy-start(bf16[2048,128]{1,0:T(8,128)(2,1)} %copy-done.2) | copy-start | bytes 1572868
  365.1 22.9 %copy-start.7 = (bf16[2048,128]{1,0:T(8,128)(2,1)S(1)}, bf16[2048,128]{1,0:T(8,128)(2,1)}, u32[]{:S(2)}) copy-start(bf16[2048,128]{1,0:T(8,128)(2,1)} %copy-done.6) | copy-start | bytes 1572868
  388.0 23.1 %copy-start.5 = (bf16[2048,128]{1,0:T(8,128)(2,1)S(1)}, bf16[2048,128]{1,0:T(8,128)(2,1)}, u32[]{:S(2)}) copy-start(bf16[2048,128]{1,0:T(8,128)(2,1)} %copy-done.4) | copy-start | bytes 1572868
  553.0 15.6 %collective-permute-start.8 = (bf16[128,2048]{1,0:T(8,128)(2,1)}, bf16[128,2048]{1,0:T(8,128)(2,1)S(1)}, u32[]{:S(2)}, u32[]{:S(2)}) collective-permute-start(bf16[128,2048]{1,0:T(8,128)(2,1)} %reduce-scatter.5.cloned.1.call-done), channel_id=1, source_target_pairs={{0,2},{1,3},{2,0},{3,1},{4,6},{5,7},{6,4},{7,5},{8,10},{9,11},{10,... | collective-permute-start | bytes 1572872 | tf_op jit(solution)/shard_map/ppermute | solution.py:1557
  556.3 12.2 %copy-start.16 = (bf16[128,2048]{1,0:T(8,128)(2,1)S(1)}, bf16[128,2048]{1,0:T(8,128)(2,1)}, u32[]{:S(2)}) copy-start(bf16[128,2048]{1,0:T(8,128)(2,1)} %reduce-scatter.5.cloned.1.call-done) | copy-start | bytes 1572868
  562.3 12.9 %copy-start.17 = (bf16[64,2560]{1,0:T(8,128)(2,1)S(1)}, bf16[64,2560]{1,0:T(8,128)(2,1)}, u32[]{:S(2)}) copy-start(bf16[64,2560]{1,0:T(8,128)(2,1)} %reduce-scatter.3.cloned.1.call-done) | copy-start | bytes 983044
  562.3 12.9 %collective-permute-start.7 = (bf16[64,2560]{1,0:T(8,128)(2,1)}, bf16[64,2560]{1,0:T(8,128)(2,1)S(1)}, u32[]{:S(2)}, u32[]{:S(2)}) collective-permute-start(bf16[64,2560]{1,0:T(8,128)(2,1)} %reduce-scatter.3.cloned.1.call-done), channel_id=1, source_target_pairs={{0,2},{1,3},{2,0},{3,1},{4,6},{5,7},{6,4},{7,5},{8,10},{9,11},{10,... | collective-permute-start | bytes 983048 | tf_op jit(solution)/shard_map/ppermute | solution.py:1557
  (18 other events, 82.5 us)
Sparse Core Ops, SparseCore 0:
  11.0 113.6 all-gather.6
  126.9 73.2 all-gather.4
  258.5 103.4 reduce-scatter.4
  364.3 135.1 reduce-scatter.2

commit v3 on v2

--- a/solution.py
+++ b/solution.py
@@ -326,126 +326,137 @@
 AXES = ("z", "core", "context", "tensor")
 BF = jnp.bfloat16
 F32 = jnp.float32
-SUB = 2
+FINE = 128
 MASKED = -1e30
 NT = (((1,), (1,)), ((), ()))
-NN = (((1,), (0,)), ((), ()))
-
-def _dot(a, b, dims):
-    return lax.dot_general(a, b, dims, preferred_element_type=jnp.float32)
-
-def attn_fwd_kernel(lo_ref, hi_ref, shift_ref, q_ref, k_ref, v_ref, segk_ref, segq_ref, o_ref, lse_ref, vt_ref, *, bq, bk, hd, scale, nblk):
-    qb = pl.program_id(0)
+
+def attn_fwd_kernel(
+    lo_ref, hi_ref, shift_ref, q_ref, k_ref, v_ref, segk_ref, segq_ref, o_ref, lse_ref, vt_ref,
+    *, fine, many, hd, scale,
+):
+    block = pl.program_id(0)
     shift = shift_ref[0]
-    pair = q_ref.shape[1]
+    bq, pair = q_ref.shape
+    pieces = k_ref.shape[0] // fine
     heads = pair // hd
 
-    @pl.when(qb == 0)
+    @pl.when(block == 0)
     def _():
-        for j in range(nblk):
-            vt_ref[j] = v_ref[j * bk:(j + 1) * bk, :].T
-
-    gq = lax.rem(qb + shift // (bq // bk), nblk * bk // bq)
+        for j in range(pieces):
+            vt_ref[j] = v_ref[j * fine : (j + 1) * fine, :].T
+
+    at = lax.rem(block + shift // (bq // fine), pieces * fine // bq)
+    low, high = lo_ref[at], hi_ref[at]
     lane = lax.broadcasted_iota(jnp.int32, (bq, pair), 1) // hd
-    q = q_ref[...] * jnp.asarray(scale, q_ref.dtype)
+    q = q_ref[...] * jnp.asarray(scale, BF)
     qs = [jnp.where(lane == h, q, jnp.zeros_like(q)) for h in range(heads)]
-    segq = segq_ref[0:1, :]
+    seg_q = segq_ref[0:1, :]
 
     def body(i, carry):
-        j = lo_ref[gq] + i * SUB
-        sbs = [lax.rem(j + u + shift, nblk) for u in range(SUB)]
-        sc = [[None] * SUB for _ in range(heads)]
-        for u in range(SUB):
-            ks = pl.multiple_of(sbs[u] * bk, bk)
-            kb = k_ref[pl.ds(ks, bk), :]
-            same = segk_ref[pl.ds(ks, bk), :]
-            same = jnp.concatenate([same] * (bq // same.shape[1]), axis=1) == segq
-            for h in range(heads):
-                sc[h][u] = jnp.where(same, _dot(kb, qs[h], NT), MASKED)
+        j = low + i * many
+        spots = [lax.rem(j + u + shift, pieces) for u in range(many)]
+        keys = jnp.concatenate([k_ref[aligned(spot * fine, fine), :] for spot in spots])
+        values_t = jnp.concatenate([vt_ref[spot] for spot in spots], axis=1)
+        seg_k = jnp.concatenate(
+            [
+                jnp.where(j + u < high, segk_ref[aligned(spot * fine, fine), :], -1)
+                for u, spot in enumerate(spots)
+            ]
+        )
+        same = jnp.concatenate([seg_k] * (bq // seg_k.shape[1]), axis=1) == seg_q
+        scores = [jnp.where(same, mm_nt(keys, qs[h]), MASKED) for h in range(heads)]
         out = []
         for h in range(heads):
-            m, l, acc = carry[h]
-            mn = m
-            for u in range(SUB):
-                mn = jnp.maximum(mn, jnp.max(sc[h][u], axis=0, keepdims=True))
-            a = jnp.exp(m - mn)
-            l = l * a
-            acc = acc * a
-            for u in range(SUB):
-                p = jnp.exp(sc[h][u] - mn)
-                l = l + jnp.sum(p, axis=0, keepdims=True)
-                acc = acc + _dot(vt_ref[sbs[u], h * hd:(h + 1) * hd, :], p.astype(jnp.bfloat16), NN)
-            out.append((mn, l, acc))
+            top, total, acc = carry[h]
+            new_top = jnp.maximum(top, jnp.max(scores[h], axis=0, keepdims=True))
+            weights = jnp.exp(scores[h] - new_top)
+            fade = jnp.exp(top - new_top)
+            total = total * fade + jnp.sum(weights, axis=0, keepdims=True)
+            acc = acc * fade + mm(values_t[h * hd : (h + 1) * hd, :], weights.astype(BF))
+            out.append((new_top, total, acc))
         return tuple(out)
 
-    init = tuple((jnp.full((1, bq), MASKED, jnp.float32), jnp.zeros((1, bq), jnp.float32), jnp.zeros((hd, bq), jnp.float32)) for _ in range(heads))
-    res = lax.fori_loop(0, (hi_ref[gq] - lo_ref[gq] + SUB - 1) // SUB, body, init)
-    o_ref[...] = jnp.concatenate([acc / l for (m, l, acc) in res], axis=0).T.astype(o_ref.dtype)
-    lse_ref[0] = jnp.concatenate([m + jnp.log(l) for (m, l, acc) in res], axis=0)
-
-def attn_bwd_kernel(lo_ref, hi_ref, shift_ref, q_ref, k_ref, v_ref, o_ref, do_ref, lse_ref, segk_ref, segq_ref, out_ref,
-                    qs_ref, dos_ref, kt_ref, delta_ref, dqt_ref, dk_ref, dv_ref, *, bq, bk, hd, scale, nblk):
-    w = pl.program_id(0)
+    init = (jnp.full((1, bq), MASKED, F32), jnp.zeros((1, bq), F32), jnp.zeros((hd, bq), F32))
+    done = lax.fori_loop(0, (high - low + many - 1) // many, body, (init,) * heads)
+    o_ref[...] = jnp.concatenate([acc / total for _, total, acc in done], axis=0).T.astype(BF)
+    lse_ref[0] = jnp.concatenate([top + jnp.log(total) for top, total, _ in done], axis=0)
+
+
+def attn_bwd_kernel(
+    lo_ref, hi_ref, shift_ref, q_ref, k_ref, v_ref, o_ref, do_ref, lse_ref, segk_ref, segq_ref, out_ref,
+    qs_ref, dos_ref, kt_ref, delta_ref, dqt_ref, dk_ref, dv_ref,
+    *, bk, fine, many, hd, scale,
+):
+    w = pl.program_id(1)
     shift = shift_ref[0]
     rows, pair = q_ref.shape
+    pieces = rows // fine
+    blocks = rows // bk
     heads = pair // hd
 
     @pl.when(w == 0)
     def _():
         lane = lax.broadcasted_iota(jnp.int32, (bk, pair), 1) // hd
-        pick = (lax.broadcasted_iota(jnp.int32, (8, pair), 0) == lax.broadcasted_iota(jnp.int32, (8, pair), 1) // hd).astype(jnp.float32)
-        sc = jnp.asarray(scale, q_ref.dtype)
-        for j in range(nblk):
+        head = lax.broadcasted_iota(jnp.int32, (8, pair), 0)
+        pick = (head == lax.broadcasted_iota(jnp.int32, (8, pair), 1) // hd).astype(F32)
+        factor = jnp.asarray(scale, BF)
+        for j in range(blocks):
             r = slice(j * bk, (j + 1) * bk)
-            q = q_ref[r, :] * sc
+            q = q_ref[r, :] * factor
             do = do_ref[r, :]
             for h in range(heads):
                 qs_ref[h, r, :] = jnp.where(lane == h, q, jnp.zeros_like(q))
                 dos_ref[h, r, :] = jnp.where(lane == h, do, jnp.zeros_like(do))
-            kt_ref[j] = (k_ref[r, :] * sc).T
-            prod = do.astype(jnp.float32) * o_ref[r, :].astype(jnp.float32)
-            delta_ref[:, r] = lax.dot_general(pick, prod, NT, preferred_element_type=jnp.float32, precision=lax.Precision.HIGHEST)
-
-
-        dqt_ref[...] = jnp.zeros(dqt_ref.shape, jnp.float32)
-
-        def outer(kb, _):
-            gk = lax.rem(kb + shift, nblk)
-            nq = nblk * bk // bq
-            ks = pl.multiple_of(kb * bk, bk)
-            kblk = k_ref[pl.ds(ks, bk), :]
-            vblk = v_ref[pl.ds(ks, bk), :]
-            segk = segk_ref[pl.ds(ks, bk), :]
-            segk = jnp.concatenate([segk] * (bq // segk.shape[1]), axis=1)
-
-            def inner(j, carry):
+            kt_ref[j] = (k_ref[r, :] * factor).T
+            prod = do.astype(F32) * o_ref[r, :].astype(F32)
+            delta_ref[:, r] = lax.dot_general(
+                pick, prod, NT, preferred_element_type=F32, precision=lax.Precision.HIGHEST
+            )
+        dqt_ref[...] = jnp.zeros(dqt_ref.shape, F32)
+
+        def outer(block, _):
+            at = lax.rem(block + shift // (bk // fine), blocks)
+            low, high = lo_ref[at], hi_ref[at]
+            r = aligned(block * bk, bk)
+            keys, values = k_ref[r, :], v_ref[r, :]
+            seg_k = jnp.concatenate([segk_ref[r, :]] * (many * fine // segk_ref.shape[1]), axis=1)
+
+            def inner(i, carry):
                 dk, dv = carry
-                sb = lax.rem(j + shift // (bq // bk) if bq >= bk else j + shift * (bk // bq), nq)
-                qo = pl.multiple_of(sb * bq, bq)
-                same = segk == segq_ref[0:1, pl.ds(qo, bq)]
-                qh = [qs_ref[h, pl.ds(qo, bq), :] for h in range(heads)]
-                doh = [dos_ref[h, pl.ds(qo, bq), :] for h in range(heads)]
-                s = [_dot(kblk, qh[h], NT) for h in range(heads)]
-                dp = [_dot(vblk, doh[h], NT) for h in range(heads)]
-                p = [jnp.exp(jnp.where(same, s[h] - lse_ref[0, h:h + 1, pl.ds(qo, bq)], MASKED)) for h in range(heads)]
-                pb = [p[h].astype(jnp.bfloat16) for h in range(heads)]
-                ds = [(p[h] * (dp[h] - delta_ref[h:h + 1, pl.ds(qo, bq)])).astype(jnp.bfloat16) for h in range(heads)]
+                j = low + i * many
+                spots = [lax.rem(j + u + shift, pieces) for u in range(many)]
+                cuts = [aligned(spot * fine, fine) for spot in spots]
+                seg_q = jnp.concatenate(
+                    [jnp.where(j + u < high, segq_ref[0:1, cut], -1) for u, cut in enumerate(cuts)], axis=1
+                )
+                same = seg_k == seg_q
+                q = [jnp.concatenate([qs_ref[h, cut, :] for cut in cuts]) for h in range(heads)]
+                do = [jnp.concatenate([dos_ref[h, cut, :] for cut in cuts]) for h in range(heads)]
+                lse = jnp.concatenate([lse_ref[0, :, cut] for cut in cuts], axis=1)
+                delta = jnp.concatenate([delta_ref[:, cut] for cut in cuts], axis=1)
+                scores = [mm_nt(keys, q[h]) for h in range(heads)]
+                dp = [mm_nt(values, do[h]) for h in range(heads)]
+                p = [jnp.exp(jnp.where(same, scores[h] - lse[h : h + 1, :], MASKED)) for h in range(heads)]
+                p_low = [p[h].astype(BF) for h in range(heads)]
+                ds = [(p[h] * (dp[h] - delta[h : h + 1, :])).astype(BF) for h in range(heads)]
                 for h in range(heads):
                     hs = slice(h * hd, (h + 1) * hd)
-                    dv = dv + _dot(pb[h], doh[h], NN)
-                    dk = dk + _dot(ds[h], qh[h], NN)
-                    dqt_ref[sb, hs, :] += _dot(kt_ref[kb, hs, :], ds[h], NN)
+                    dv = dv + mm(p_low[h], do[h])
+                    dk = dk + mm(ds[h], q[h])
+                    dq = mm(kt_ref[block, hs, :], ds[h])
+                    for u in range(many):
+                        dqt_ref[spots[u], hs, :] += dq[:, u * fine : (u + 1) * fine]
                 return dk, dv
 
-            zero = jnp.zeros((bk, pair), jnp.float32)
-            dk, dv = lax.fori_loop(lo_ref[gk], hi_ref[gk], inner, (zero, zero))
-            dk_ref[pl.ds(ks, bk), :] = dk.astype(jnp.bfloat16)
-            dv_ref[pl.ds(ks, bk), :] = dv.astype(jnp.bfloat16)
+            zero = jnp.zeros((bk, pair), F32)
+            dk, dv = lax.fori_loop(0, (high - low + many - 1) // many, inner, (zero, zero))
+            dk_ref[r, :] = dk.astype(BF)
+            dv_ref[r, :] = dv.astype(BF)
             return 0
 
-        lax.fori_loop(0, nblk, outer, 0)
-        for j in range(nblk * bk // bq):
-            out_ref[j * bq:(j + 1) * bq, :] = dqt_ref[j].T.astype(out_ref.dtype)
+        lax.fori_loop(0, blocks, outer, 0)
+        for j in range(pieces):
+            out_ref[j * fine : (j + 1) * fine, :] = dqt_ref[j].T.astype(BF)
 
     @pl.when(w == 1)
     def _():
@@ -455,16 +466,18 @@
     def _():
         out_ref[...] = dv_ref[...]
 
+
 def pair_block(which, pair, group):
     return (pair // group) * 3 * group + which * group + pair % group
 
 
-def attn_fwd(qkv, seg_k, seg_q, low, high, shift, pair, pairs, group, head_size, bq, bk):
+def attn_fwd(qkv, seg_k, seg_q, low, high, shift, pair, pairs, group, head_size, bq, many):
     rows, wide = qkv.shape[0], 2 * head_size
-    blocks = rows // bk
     spec = lambda which: pair_block(which, pair, group)
     return pl.pallas_call(
-        functools.partial(attn_fwd_kernel, bq=bq, bk=bk, hd=head_size, scale=float(head_size) ** -0.5, nblk=blocks),
+        functools.partial(
+            attn_fwd_kernel, fine=FINE, many=many, hd=head_size, scale=float(head_size) ** -0.5
+        ),
         out_shape=(
             jax.ShapeDtypeStruct((rows, wide), BF),
             jax.ShapeDtypeStruct((1, 2, rows), F32),
@@ -483,7 +496,7 @@
                 pl.BlockSpec((bq, wide), lambda i, *_: (i, 0)),
                 pl.BlockSpec((1, 2, bq), lambda i, *_: (0, 0, i)),
             ),
-            scratch_shapes=[pltpu.VMEM((blocks, wide, bk), BF)],
+            scratch_shapes=[pltpu.VMEM((rows // FINE, wide, FINE), BF)],
         ),
         compiler_params=pltpu.CompilerParams(vmem_limit_bytes=24 << 20),
         cost_estimate=pl.CostEstimate(
@@ -493,59 +506,46 @@
     )(low, high, shift, qkv, qkv, qkv, seg_k, seg_q)
 
 
-def attn_bwd(before, qkv, mixed, dctx, lse, seg_k, seg_q, low, high, shift, pair, pairs, group, head_size, bq, bk):
+def attn_bwd(qkv, mixed, dctx, lse, seg_k, seg_q, low, high, shift, pairs, group, head_size, bk, many):
     rows, wide = qkv.shape[0], 2 * head_size
     blocks = rows // bk
-    column = lambda which: pl.BlockSpec((rows, wide), lambda w, *_: (0, pair_block(which, pair, group)))
-    in_specs = [
-        column(0),
-        column(1),
-        column(2),
-        pl.BlockSpec((rows, wide), lambda w, *_: (0, 0)),
-        pl.BlockSpec((rows, wide), lambda w, *_: (0, pair)),
-        pl.BlockSpec((1, 2, rows), lambda w, *_: (0, 0, 0)),
-        pl.BlockSpec((rows, 128), lambda w, *_: (0, 0)),
-        pl.BlockSpec((8, rows), lambda w, *_: (0, 0)),
-    ]
-    operands = [low, high, shift, qkv, qkv, qkv, mixed, dctx, lse, seg_k, seg_q]
-    aliases = {}
-    kernel = functools.partial(
-        attn_bwd_kernel, bq=bq, bk=bk, hd=head_size, scale=float(head_size) ** -0.5, nblk=blocks
-    )
-    body = kernel
-    if before is not None:
-        aliases = {len(operands): 0}
-        in_specs.append(pl.BlockSpec(memory_space=pl.ANY))
-        operands.append(before)
-
-        def body(*refs):
-            kernel(*refs[:11], *refs[12:])
-
+    column = lambda which: pl.BlockSpec((rows, wide), lambda p, w, *_: (0, pair_block(which, p, group)))
+    own = pl.BlockSpec((rows, wide), lambda p, w, *_: (0, p))
     return pl.pallas_call(
-        body,
+        functools.partial(
+            attn_bwd_kernel, bk=bk, fine=FINE, many=many, hd=head_size, scale=float(head_size) ** -0.5
+        ),
         out_shape=jax.ShapeDtypeStruct(qkv.shape, BF),
         grid_spec=pltpu.PrefetchScalarGridSpec(
             num_scalar_prefetch=3,
-            grid=(3,),
-            in_specs=in_specs,
-            out_specs=pl.BlockSpec((rows, wide), lambda w, *_: (0, (pair // group) * 3 * group + w * group + pair % group)),
+            grid=(pairs, 3),
+            in_specs=[
+                column(0),
+                column(1),
+                column(2),
+                own,
+                own,
+                pl.BlockSpec((1, 2, rows), lambda p, w, *_: (p, 0, 0)),
+                pl.BlockSpec((rows, 128), lambda p, w, *_: (0, 0)),
+                pl.BlockSpec((8, rows), lambda p, w, *_: (0, 0)),
+            ],
+            out_specs=pl.BlockSpec((rows, wide), lambda p, w, *_: (0, pair_block(w, p, group))),
             scratch_shapes=[
                 pltpu.VMEM((2, rows, wide), BF),
                 pltpu.VMEM((2, rows, wide), BF),
                 pltpu.VMEM((blocks, wide, bk), BF),
                 pltpu.VMEM((8, rows), F32),
-                pltpu.VMEM((rows // bq, wide, bq), F32),
+                pltpu.VMEM((rows // FINE, wide, FINE), F32),
                 pltpu.VMEM((rows, wide), BF),
                 pltpu.VMEM((rows, wide), BF),
             ],
         ),
-        input_output_aliases=aliases,
-        compiler_params=pltpu.CompilerParams(vmem_limit_bytes=32 << 20),
+        compiler_params=pltpu.CompilerParams(vmem_limit_bytes=58 << 20),
         cost_estimate=pl.CostEstimate(
-            flops=25_000_000_000, bytes_accessed=rows * wide * 16, transcendentals=rows * rows // 2
+            flops=100_000_000_000, bytes_accessed=rows * wide * 64, transcendentals=2 * rows * rows
         ),
         name="attn_bwd",
-    )(*operands)
+    )(low, high, shift, qkv, qkv, qkv, mixed, dctx, lse, seg_k, seg_q)
 
 
 def segment_bounds(seg_rows, row_block, col_block):
@@ -791,6 +791,7 @@
     nf = nz * 2
     dma = pltpu.SemaphoreType.DMA
     hbm = pl.BlockSpec(memory_space=pl.ANY)
+    fixed = pl.BlockSpec(memory_space=pltpu.HBM)
     moved = 2 * (span * width * 2 + 4 * width * cols * 3)
     return pl.pallas_call(
         functools.partial(
@@ -802,7 +803,7 @@
             jax.ShapeDtypeStruct((2 * span, 3 * cols), BF),
             jax.ShapeDtypeStruct((nf * nt,) + small.shape, BF),
         ),
-        in_specs=[hbm, hbm, pl.BlockSpec(memory_space=pltpu.VMEM)],
+        in_specs=[fixed, fixed, pl.BlockSpec(memory_space=pltpu.VMEM)],
         out_specs=(hbm,) * 4,
         scratch_shapes=[
             pltpu.VMEM((2 * span, width), BF),
@@ -824,7 +825,7 @@
             dma((2, max(3, 2 * chunks))),
         ],
         compiler_params=pltpu.CompilerParams(
-            collective_id=0, has_side_effects=True, vmem_limit_bytes=40 << 20
+            collective_id=0, has_side_effects=True, vmem_limit_bytes=58 << 20
         ),
         cost_estimate=pl.CostEstimate(
             flops=2 * 2 * span * width * 3 * cols, bytes_accessed=moved, transcendentals=0
@@ -834,15 +835,16 @@
 
 
 def close_kernel(
-    dqkv_in, w_in, xt_in, grad_in, vec_in, tokens_out, grad_out, sums_out,
-    dqkv, w, xt, dres, own, xs, xr, fin, away, near, zs, zr, piece, last, sums, sums_near, sums_z, sums_last,
-    fill, x_send, x_recv, y_send, y_recv, c_sems, z_send, z_recv, p_send, p_recv, o_sems,
-    *, nz, chunk, tile,
+    dqkv_in, w_in, xt_in, grad_in, vec_one, vec_two, tokens_out, grad_out, sums_out, vec_out,
+    dqkv, w, xt, dres, own, xs, xr, fin, away, near, zs, zr, piece, last,
+    sums, sums_near, sums_z, sums_last, vecs, vecs_near, vecs_z, vecs_last,
+    fill, x_send, x_recv, y_send, y_recv, c_send, c_recv, z_send, z_recv, p_send, p_recv, o_sems,
+    *, nz, chunk, tile, part,
 ):
     z, k, c, t = (lax.axis_index(name) for name in AXES)
     rows, wide = dqkv.shape
     span = rows // 2
-    dblk = xt.shape[2]
+    dblk = piece.shape[0]
     chunks = span // chunk
     steps = wide // tile
     x_dev, y_dev, core_dev = {"context": 1 - c}, {"tensor": 1 - t}, {"core": 1 - k}
@@ -852,17 +854,21 @@
         pltpu.make_async_copy(w_in, w, fill.at[0]),
         pltpu.make_async_copy(dqkv_in.at[pl.ds(span, span)], dqkv.at[pl.ds(span, span)], fill.at[1]),
         pltpu.make_async_copy(dqkv_in.at[pl.ds(0, span)], dqkv.at[pl.ds(0, span)], fill.at[2]),
-        pltpu.make_async_copy(grad_in, dres, fill.at[3]),
-        pltpu.make_async_copy(vec_in, sums.at[pl.ds(sums.shape[0] - vec_in.shape[0], vec_in.shape[0])], fill.at[4]),
     ]
     for kk in range(2):
         for zi in range(nz):
             source = zi * 2 + lax.rem(1 - k + kk, 2)
             loads.append(
                 pltpu.make_async_copy(
-                    xt_in.at[aligned(source * dblk, dblk)], xt.at[kk, zi], fill.at[len(loads)]
+                    xt_in.at[aligned(source * dblk, dblk)], xt.at[kk, pl.ds(zi * dblk, dblk)], fill.at[len(loads)]
                 )
             )
+    for source, dest in (
+        (grad_in, dres),
+        (vec_one, vecs.at[pl.ds(0, 8)]),
+        (vec_two, vecs.at[pl.ds(8, 8)]),
+    ):
+        loads.append(pltpu.make_async_copy(source, dest, fill.at[len(loads)]))
     for one in loads:
         one.start()
     greet([x_dev, y_dev, diag, core_dev] + [{"z": lax.rem(z + d, nz)} for d in range(1, nz)])
@@ -873,37 +879,80 @@
     def y_copy(i):
         return remote(fin.at[i], tokens_out.at[t, aligned(i * chunk, chunk)], y_send.at[i], y_recv.at[i], y_dev)
 
+    def leave(i):
+        value = mm_nt(dqkv[aligned(span + i * 2 * chunk, 2 * chunk), :], w[...]).astype(BF)
+        xs[2 * i] = value[:chunk]
+        xs[2 * i + 1] = value[chunk:]
+        x_copy(2 * i).start()
+        x_copy(2 * i + 1).start()
+
     loads[0].wait()
     loads[1].wait()
 
-    @pl.loop(0, chunks)
+    @pl.loop(0, 1)
     def _(i):
-        xs[i] = mm_nt(dqkv[aligned(span + i * chunk, chunk), :], w[...]).astype(BF)
-        x_copy(i).start()
+        leave(i)
 
     for one in loads[2:]:
         one.wait()
     ones = jnp.ones((8, rows), BF)
-    vec_at = sums.shape[0] - vec_in.shape[0]
-    sums[0:vec_at, :] = jnp.zeros((vec_at, 128), F32)
+    sums[...] = jnp.zeros(sums.shape, F32)
 
     @pl.loop(0, steps)
     def _(j):
-        part = dqkv[:, aligned(j * tile, tile)]
-        for zi in range(nz):
-            away[zi, :, aligned(j * tile, tile)] = mm(xt[0, zi], part).astype(BF)
-        total = mm(ones, part)
+        value = dqkv[:, aligned(j * tile, tile)]
+        away[:, aligned(j * tile, tile)] = mm(xt[0], value).astype(BF)
+        total = mm(ones, value)
         for u in range(tile // 128):
             sums[pl.ds(j * (tile // 128) + u, 1), :] = total[0:1, u * 128 : (u + 1) * 128]
 
-    core_copy = remote(away, near, c_sems.at[0], c_sems.at[1], core_dev)
-    core_copy.start()
-    core_sum = remote(sums, sums_near, c_sems.at[2], c_sems.at[3], core_dev)
-    core_sum.start()
-
-    @pl.loop(0, chunks)
+    core_copies = [
+        remote(mine, theirs, c_send.at[i], c_recv.at[i], core_dev)
+        for i, (mine, theirs) in enumerate(((away, near), (sums, sums_near), (vecs, vecs_near)))
+    ]
+    for one in core_copies:
+        one.start()
+
+    @pl.loop(1, chunks // 2)
     def _(i):
-        r = aligned(i * chunk, chunk)
+        leave(i)
+
+    for one in core_copies:
+        one.wait_recv()
+    sums_z[z] = sums[...] + sums_near[...]
+    vecs_z[z] = vecs[...] + vecs_near[...]
+
+    @pl.loop(0, steps)
+    def _(j):
+        cut = aligned(j * tile, tile)
+        zs[:, cut] = (mm(xt[1], dqkv[:, cut]) + near[:, cut].astype(F32)).astype(BF)
+
+    def z_copies(d, owner):
+        dev = {"z": lax.rem(z + d, nz)}
+        return [
+            remote(buf.at[owner], buf.at[owner], z_send.at[i, d - 1], z_recv.at[i, owner], dev)
+            for i, buf in enumerate((sums_z, vecs_z))
+        ]
+
+    def ring(step):
+        source = zs.at[aligned(lax.rem(z + nz - step, nz) * dblk, dblk)]
+        return remote(source, zr.at[step - 1], z_send.at[2, step - 1], z_recv.at[2, step - 1], {"z": lax.rem(z + 1, nz)})
+
+    def arrived(step):
+        ring(step).wait_recv()
+        spot = aligned(lax.rem(z + 2 * nz - step - 1, nz) * dblk, dblk)
+        zs[spot, :] = (zs[spot, :].astype(F32) + zr[step - 1].astype(F32)).astype(BF)
+        if step + 1 < nz:
+            ring(step + 1).start()
+
+    ring(1).start()
+    for d in range(1, nz):
+        for one in z_copies(d, z):
+            one.start()
+
+    @pl.loop(0, chunks // 2)
+    def _(i):
+        r = aligned(i * 2 * chunk, 2 * chunk)
         own[r, :] = mm_nt(dqkv[r, :], w[...]) + dres[r, :]
 
     def finish(i):
@@ -913,53 +962,25 @@
         pltpu.make_async_copy(fin.at[i], tokens_out.at[t, r], o_sems.at[i]).start()
         y_copy(i).start()
 
-    core_copy.wait_recv()
-    core_sum.wait_recv()
-    sums_z[z] = sums[...] + sums_near[...]
-
-    @pl.loop(0, steps)
-    def _(j):
-        cut = aligned(j * tile, tile)
-        part = dqkv[:, cut]
-        for zi in range(nz):
-            zs[zi, :, cut] = (mm(xt[1, zi], part) + near[zi, :, cut].astype(F32)).astype(BF)
-
-    def z_copy(d, owner, target):
-        return remote(zs.at[target], zr.at[owner], z_send.at[0, d - 1], z_recv.at[0, owner], {"z": lax.rem(z + d, nz)})
-
-    def z_sum(d, owner):
-        return remote(
-            sums_z.at[owner], sums_z.at[owner], z_send.at[1, d - 1], z_recv.at[1, owner], {"z": lax.rem(z + d, nz)}
-        )
-
+    cuts = [chunks * step // nz for step in range(nz + 1)]
+    for step in range(1, nz):
+        pl.loop(cuts[step - 1], cuts[step])(finish)
+        arrived(step)
     for d in range(1, nz):
-        z_copy(d, z, lax.rem(z + d, nz)).start()
-        z_sum(d, z).start()
-
-    half = chunks // 2
-
-    @pl.loop(0, half)
-    def _(i):
-        finish(i)
-
-    for d in range(1, nz):
-        owner = lax.rem(z + nz - d, nz)
-        z_copy(d, owner, z).wait_recv()
-        z_sum(d, owner).wait_recv()
-    total = zs[z].astype(F32)
-    for d in range(1, nz):
-        total = total + zr[lax.rem(z + nz - d, nz)].astype(F32)
-    piece[...] = total.astype(BF)
+        for one in z_copies(d, lax.rem(z + nz - d, nz)):
+            one.wait_recv()
+    piece[...] = zs[aligned(z * dblk, dblk), :]
     sums_last[0] = jnp.sum(sums_z[...], axis=0)
-
-    p_x = remote(piece, last.at[0], p_send.at[0], p_recv.at[0], x_dev)
-    p_y = remote(piece, last.at[1], p_send.at[1], p_recv.at[1], y_dev)
-    p_d = remote(piece, last.at[2], p_send.at[2], p_recv.at[2], diag)
-    s_x = remote(sums_last.at[0], sums_last.at[1], p_send.at[3], p_recv.at[3], x_dev)
-    s_y = remote(sums_last.at[0], sums_last.at[2], p_send.at[4], p_recv.at[4], y_dev)
-    s_d = remote(sums_last.at[0], sums_last.at[3], p_send.at[5], p_recv.at[5], diag)
-
-    for one in (s_x, s_y, s_d):
+    vecs_last[0] = jnp.sum(vecs_z[...], axis=0)
+
+    trio = ((x_dev, 0), (y_dev, 1), (diag, 2))
+    p_x, p_y, p_d = (remote(piece, last.at[i], p_send.at[i], p_recv.at[i], dev) for dev, i in trio)
+    everywhere = [
+        remote(buf.at[0], buf.at[1 + i], p_send.at[at + i], p_recv.at[at + i], dev)
+        for dev, i in trio
+        for buf, at in ((sums_last, 3), (vecs_last, 6))
+    ]
+    for one in everywhere:
         one.start()
 
     @pl.when(c == t)
@@ -971,36 +992,41 @@
         p_y.start()
         p_d.start()
 
-    @pl.loop(half, chunks)
-    def _(i):
-        finish(i)
-
-    for one in (s_x, s_y, s_d):
+    pl.loop(cuts[nz - 1], chunks)(finish)
+
+    def give(value):
+        width = part
+        for g in range(wide // (3 * width)):
+            for which in range(3):
+                at = (g * 3 + which) * width
+                grad_out[which, :, g * width : (g + 1) * width] = value[:, at : at + width]
+
+    for one in everywhere:
         one.wait()
     near_pair = sums_last[0] + sums_last[2]
-    far_pair = sums_last[1] + sums_last[3]
-    sums_out[0:vec_at, :] = jnp.where(c == t, near_pair, far_pair)[0:vec_at]
-    sums_out[vec_at:, :] = (near_pair + far_pair)[vec_at:]
+    sums_out[...] = jnp.where(c == t, near_pair, sums_last[1] + sums_last[3])
+    vec_out[...] = (vecs_last[0] + vecs_last[2]) + (vecs_last[1] + vecs_last[3])
 
     @pl.when(c == t)
     def _():
         p_y.wait_recv()
-        grad_out[...] = piece[...].astype(F32) + last[1].astype(F32)
+        give(piece[...].astype(F32) + last[1].astype(F32))
         p_x.wait_send()
 
     @pl.when(c != t)
     def _():
         p_x.wait_recv()
         p_d.wait_recv()
-        grad_out[...] = last[0].astype(F32) + last[2].astype(F32)
+        give(last[0].astype(F32) + last[2].astype(F32))
         p_y.wait_send()
         p_d.wait_send()
 
-    core_copy.wait_send()
-    core_sum.wait_send()
+    for one in core_copies:
+        one.wait_send()
     for d in range(1, nz):
-        z_copy(d, z, lax.rem(z + d, nz)).wait_send()
-        z_sum(d, z).wait_send()
+        ring(d).wait_send()
+        for one in z_copies(d, z):
+            one.wait_send()
 
     @pl.loop(0, chunks)
     def _(i):
@@ -1011,7 +1037,7 @@
         remote(fin.at[i], tokens_out.at[1 - t, r], y_send.at[i], y_recv.at[i], y_dev).wait_recv()
 
 
-def close_layer(dqkv, w, xt, grad_in, vectors, nz):
+def close_layer(dqkv, w, xt, grad_in, vec_one, vec_two, nz, part):
     rows, wide = dqkv.shape
     width = w.shape[0]
     span = rows // 2
@@ -1020,55 +1046,63 @@
     chunks = span // chunk
     dma = pltpu.SemaphoreType.DMA
     hbm = pl.BlockSpec(memory_space=pl.ANY)
-    sum_rows = wide // 128 + -(wide // 128) % 8 + vectors.shape[0]
+    vmem = pl.BlockSpec(memory_space=pltpu.VMEM)
+    sum_shape = (wide // 128 + -(wide // 128) % 8, 128)
+    vec_shape = (16, width)
     return pl.pallas_call(
-        functools.partial(close_kernel, nz=nz, chunk=chunk, tile=tile),
+        functools.partial(close_kernel, nz=nz, chunk=chunk, tile=tile, part=part),
         out_shape=(
             jax.ShapeDtypeStruct((2, span, width), BF),
-            jax.ShapeDtypeStruct((dblk, wide), F32),
-            jax.ShapeDtypeStruct((sum_rows, 128), F32),
-        ),
-        in_specs=[hbm] * 5,
-        out_specs=(hbm, pl.BlockSpec(memory_space=pltpu.VMEM), pl.BlockSpec(memory_space=pltpu.VMEM)),
+            jax.ShapeDtypeStruct((3, dblk, wide // 3), F32),
+            jax.ShapeDtypeStruct(sum_shape, F32),
+            jax.ShapeDtypeStruct(vec_shape, F32),
+        ),
+        in_specs=[hbm] * 6,
+        out_specs=(hbm, vmem, vmem, vmem),
         scratch_shapes=[
             pltpu.VMEM((rows, wide), BF),
             pltpu.VMEM((width, wide), BF),
-            pltpu.VMEM((2, nz, dblk, rows), BF),
+            pltpu.VMEM((2, nz * dblk, rows), BF),
             pltpu.VMEM((span, width), F32),
             pltpu.VMEM((span, width), F32),
             pltpu.VMEM((chunks, chunk, width), BF),
             pltpu.VMEM((chunks, chunk, width), BF),
             pltpu.VMEM((chunks, chunk, width), BF),
-            pltpu.VMEM((nz, dblk, wide), BF),
-            pltpu.VMEM((nz, dblk, wide), BF),
-            pltpu.VMEM((nz, dblk, wide), BF),
+            pltpu.VMEM((nz * dblk, wide), BF),
+            pltpu.VMEM((nz * dblk, wide), BF),
+            pltpu.VMEM((nz * dblk, wide), BF),
             pltpu.VMEM((nz, dblk, wide), BF),
             pltpu.VMEM((dblk, wide), BF),
             pltpu.VMEM((3, dblk, wide), BF),
-            pltpu.VMEM((sum_rows, 128), F32),
-            pltpu.VMEM((sum_rows, 128), F32),
-            pltpu.VMEM((nz, sum_rows, 128), F32),
-            pltpu.VMEM((4, sum_rows, 128), F32),
-            dma((5 + 2 * nz,)),
+            pltpu.VMEM(sum_shape, F32),
+            pltpu.VMEM(sum_shape, F32),
+            pltpu.VMEM((nz,) + sum_shape, F32),
+            pltpu.VMEM((4,) + sum_shape, F32),
+            pltpu.VMEM(vec_shape, F32),
+            pltpu.VMEM(vec_shape, F32),
+            pltpu.VMEM((nz,) + vec_shape, F32),
+            pltpu.VMEM((4,) + vec_shape, F32),
+            dma((6 + 2 * nz,)),
             dma((chunks,)),
             dma((chunks,)),
             dma((chunks,)),
             dma((chunks,)),
-            dma((4,)),
-            dma((2, nz)),
-            dma((2, nz)),
-            dma((6,)),
-            dma((6,)),
+            dma((3,)),
+            dma((3,)),
+            dma((3, nz)),
+            dma((3, nz)),
+            dma((9,)),
+            dma((9,)),
             dma((chunks,)),
         ],
         compiler_params=pltpu.CompilerParams(
-            collective_id=1, has_side_effects=True, vmem_limit_bytes=56 << 20
+            collective_id=1, has_side_effects=True, vmem_limit_bytes=46 << 20
         ),
         cost_estimate=pl.CostEstimate(
             flops=4 * rows * width * wide, bytes_accessed=30 << 20, transcendentals=0
         ),
         name="close_layer",
-    )(dqkv, w, xt, grad_in, vectors)
+    )(dqkv, w, xt, grad_in, vec_one, vec_two)
 
 
 def mean_of(rows):
@@ -1145,7 +1179,7 @@
 def up_layer(t, ctx, tokens, vecs, up_add, up_all, nt):
     span, width = ctx.shape
     hidden = up_add.shape[1]
-    block, tile = 256, 512
+    block, tile = 512, 512
     hbm = pl.BlockSpec(memory_space=pl.ANY)
     rows = pl.BlockSpec((block, width), lambda i, _: (i, 0))
     wide = pl.BlockSpec((block, hidden), lambda i, _: (i, 0))
@@ -1247,7 +1281,7 @@
 def down_layer(t, out_grad, vecs, first, act, down_all, nt):
     span, width = first.shape
     hidden = act.shape[1]
-    block = 256
+    block = 512
     rows = pl.BlockSpec((block, width), lambda i, _: (i, 0))
     whole = lambda shape: pl.BlockSpec(shape, lambda i, _: (0,) * len(shape))
     sds = jax.ShapeDtypeStruct
@@ -1287,13 +1321,71 @@
 
 
 def back_kernel(
-    vecs, branch, grad_second, slope, norm_one, inv_one, up_in, down_in,
-    hid, attn_t, grad_in, grad_ctx, vec_sums, up_sums,
-    up, down, proj, acc, sums, sums_u, fill,
-    *, nt, tile,
+    vecs, branch, grad_second, slope, norm_one, inv_one, up_in, down_in, partial,
+    hid, attn_t, grad_in, grad_ctx, vec_sums, quarter,
+    up, down, proj, acc, sums, sums_u, by_y, near_y, by_x, near_x, last_x, last_y,
+    fill, own_fill, one_send, one_recv, two_send, two_recv,
+    *, nz, nt, tile,
 ):
     i = pl.program_id(0)
+    c, t = lax.axis_index("context"), lax.axis_index("tensor")
+    x_dev, y_dev = {"context": 1 - c}, {"tensor": 1 - t}
     width, hidden = up.shape
+    rest = last_x.shape[0] // nz
+    half = last_x.shape[1]
+    tall = nz * 2 * rest
+    left, right = pl.ds(0, half), pl.ds(half, half)
+    own_copies = [pltpu.make_async_copy(partial.at[aligned(t * tall, tall), left], by_y, own_fill.at[0])]
+    first_copies = [
+        remote(partial.at[aligned((1 - t) * tall, tall), left], near_y, one_send.at[0], one_recv.at[0], y_dev)
+    ]
+    for b in range(nt * nz):
+        spot = pl.ds(b * rest, rest)
+        own_copies.append(
+            pltpu.make_async_copy(
+                partial.at[aligned((b * 2 + c) * rest, rest), right], by_x.at[spot], own_fill.at[1 + b]
+            )
+        )
+        first_copies.append(
+            remote(
+                partial.at[aligned((b * 2 + 1 - c) * rest, rest), right],
+                near_x.at[spot],
+                one_send.at[1 + b],
+                one_recv.at[1 + b],
+                x_dev,
+            )
+        )
+    second_copies = [
+        remote(by_x.at[aligned((1 - t) * nz * rest, nz * rest)], last_y, two_send.at[0], two_recv.at[0], y_dev)
+    ]
+    for zi in range(nz):
+        second_copies.append(
+            remote(
+                by_y.at[aligned((zi * 2 + 1 - c) * rest, rest)],
+                last_x.at[pl.ds(zi * rest, rest)],
+                two_send.at[1 + zi],
+                two_recv.at[1 + zi],
+                x_dev,
+            )
+        )
+
+    @pl.when(i == 0)
+    def _():
+        greet([x_dev, y_dev])
+        for one in first_copies + own_copies:
+            one.start()
+
+    @pl.when(i == 2)
+    def _():
+        for one in own_copies:
+            one.wait()
+        for one in first_copies:
+            one.wait_recv()
+        by_y[...] = (by_y[...].astype(F32) + near_y[...].astype(F32)).astype(BF)
+        by_x[...] = (by_x[...].astype(F32) + near_x[...].astype(F32)).astype(BF)
+        for one in second_copies:
+            one.start()
+
     down_fill = load_blocks(down_in, 0, down, fill.at[0], nt, False)
     up_fill = load_blocks(up_in, 0, up, fill.at[1], nt, True)
     proj_fill = load_blocks(up_in, hidden // nt, proj, fill.at[2], nt, True)
@@ -1335,27 +1427,40 @@
         for row in range(3):
             vec_sums[row : row + 1, :] = jnp.sum(sums[row], axis=0, keepdims=True)
         vec_sums[3:8, :] = jnp.zeros((5, width), F32)
-        up_sums[...] = sums_u[...]
-
-
-def back_layer(vecs, branch, grad_second, slope, norm_one, inv_one, up_all, down_all, nt):
+        for row in range(hidden // width):
+            vec_sums[3 + row : 4 + row, :] = sums_u[0:1, row * width : (row + 1) * width]
+        for one in second_copies:
+            one.wait_recv()
+        for zi in range(nz):
+            spot = slice(zi * rest, (zi + 1) * rest)
+            mine = by_y[aligned((zi * 2 + c) * rest, rest), :]
+            quarter[spot, :half] = (mine.astype(F32) + last_x[spot, :].astype(F32)).astype(BF)
+        mine = by_x[aligned(t * nz * rest, nz * rest), :]
+        quarter[:, half:] = (mine.astype(F32) + last_y[...].astype(F32)).astype(BF)
+        for one in first_copies + second_copies:
+            one.wait_send()
+
+
+def back_layer(vecs, branch, grad_second, slope, norm_one, inv_one, up_all, down_all, partial, nz, nt):
     span, width = branch.shape
     hidden = slope.shape[1]
-    block, tile = 256, 512
+    block, tile = span // 4, 512
+    rest, half = partial.shape[0] // (nt * nz * 2), partial.shape[1] // 2
+    quarter = (nz * rest, 2 * half)
     hbm = pl.BlockSpec(memory_space=pl.ANY)
     rows = pl.BlockSpec((block, width), lambda i: (i, 0))
     wide = pl.BlockSpec((block, hidden), lambda i: (i, 0))
     whole = lambda shape: pl.BlockSpec(shape, lambda i: (0,) * len(shape))
     sds = jax.ShapeDtypeStruct
     return pl.pallas_call(
-        functools.partial(back_kernel, nt=nt, tile=tile),
+        functools.partial(back_kernel, nz=nz, nt=nt, tile=tile),
         out_shape=(
             sds((span, hidden), BF),
             sds((width, span), BF),
             sds((span, width), F32),
             sds((span, width), BF),
             sds((8, width), F32),
-            sds((8, hidden), F32),
+            sds(quarter, BF),
         ),
         grid=(span // block,),
         in_specs=[
@@ -1367,9 +1472,10 @@
             pl.BlockSpec((block, 128), lambda i: (i, 0)),
             hbm,
             hbm,
+            hbm,
         ],
         out_specs=(
-            wide, pl.BlockSpec((width, block), lambda i: (0, i)), rows, rows, whole((8, width)), whole((8, hidden)),
+            wide, pl.BlockSpec((width, block), lambda i: (0, i)), rows, rows, whole((8, width)), whole(quarter),
         ),
         scratch_shapes=[
             pltpu.VMEM((width, hidden), BF),
@@ -1378,22 +1484,42 @@
             pltpu.VMEM((block, width), F32),
             pltpu.VMEM((3, 8, width), F32),
             pltpu.VMEM((8, hidden), F32),
+            pltpu.VMEM((nz * 2 * rest, half), BF),
+            pltpu.VMEM((nz * 2 * rest, half), BF),
+            pltpu.VMEM((nt * nz * rest, half), BF),
+            pltpu.VMEM((nt * nz * rest, half), BF),
+            pltpu.VMEM((nz * rest, half), BF),
+            pltpu.VMEM((nz * rest, half), BF),
             pltpu.SemaphoreType.DMA((3, up_all.shape[0])),
+            pltpu.SemaphoreType.DMA((1 + nt * nz,)),
+            pltpu.SemaphoreType.DMA((1 + nt * nz,)),
+            pltpu.SemaphoreType.DMA((1 + nt * nz,)),
+            pltpu.SemaphoreType.DMA((1 + nz,)),
+            pltpu.SemaphoreType.DMA((1 + nz,)),
         ],
-        compiler_params=pltpu.CompilerParams(vmem_limit_bytes=60 << 20),
+        compiler_params=pltpu.CompilerParams(
+            collective_id=4, has_side_effects=True, vmem_limit_bytes=60 << 20
+        ),
         cost_estimate=pl.CostEstimate(
             flops=2 * span * width * (width + 2 * hidden), bytes_accessed=60 << 20, transcendentals=0
         ),
         name="back_layer",
-    )(vecs, branch, grad_second, slope, norm_one, inv_one, up_all, down_all)
+    )(vecs, branch, grad_second, slope, norm_one, inv_one, up_all, down_all, partial)
 
 
 def grads_kernel(*refs, pairs, nz, nt, chunk):
     lefts, rights = refs[0 : 2 * pairs : 2], refs[1 : 2 * pairs : 2]
-    packed, left, right, away, near, stage, l_fill, r_fill, send, recv, out_sems = refs[2 * pairs :]
+    refs = refs[2 * pairs :]
+    quarter = None
+    if len(refs) > 11:
+        quarter, dctx_in, packed, shard, dctx = refs[:5]
+        mine, others, dctx_own, mine_fill, dctx_sems, q_send, q_recv = refs[-7:]
+        refs = (packed,) + refs[5:-7]
+    packed, left, right, away, near, stage, l_fill, r_fill, send, recv, out_sems = refs
+    z = lax.axis_index("z")
     k = lax.axis_index("core")
     core_dev = {"core": 1 - k}
-    dblk = left.shape[3]
+    dblk = left.shape[2] // nz
     span = right.shape[1]
     plan = []
     base = 0
@@ -1409,7 +1535,7 @@
         [
             pltpu.make_async_copy(
                 lefts[which].at[aligned((zi * 2 + lax.rem(k + 1 + kk, 2)) * dblk, dblk)],
-                left.at[which, kk, zi],
+                left.at[which, kk, pl.ds(zi * dblk, dblk)],
                 l_fill.at[which, kk, zi],
             )
             for kk in range(2)
@@ -1428,12 +1554,43 @@
             for one in l_copies[which]:
                 one.start()
         r_copies[n].start()
-    greet([core_dev])
+    friends = [core_dev]
+    if quarter is not None:
+        c = lax.axis_index("context")
+        friends += [{"context": 1 - c}]
+        friends += [{"z": lax.rem(z + d, nz)} for d in range(1, nz)]
+    greet(friends)
+    if quarter is not None:
+        rest = mine.shape[0]
+
+        def q_copy(d, owner, target):
+            return remote(
+                quarter.at[aligned(target * rest, rest)],
+                others.at[owner],
+                q_send.at[d - 1],
+                q_recv.at[owner],
+                {"z": lax.rem(z + d, nz)},
+            )
+
+        cols = dctx.shape[1]
+        own_in = pltpu.make_async_copy(dctx_in.at[:, aligned(c * cols, cols)], dctx_own, dctx_sems.at[0])
+        own_out = pltpu.make_async_copy(dctx_own, dctx.at[pl.ds(0, span)], dctx_sems.at[1])
+        dctx_copy = remote(
+            dctx_in.at[:, aligned((1 - c) * cols, cols)],
+            dctx.at[pl.ds(span, span)],
+            dctx_sems.at[2],
+            dctx_sems.at[3],
+            {"context": 1 - c},
+        )
+        own_in.start()
+        dctx_copy.start()
+        own = pltpu.make_async_copy(quarter.at[aligned(z * rest, rest)], mine, mine_fill)
+        own.start()
 
     def exchange(n):
         step = plan[n][4]
         cut = pl.ds(0, step)
-        return remote(away.at[n, :, :, cut], near.at[n, :, :, cut], send.at[n], recv.at[n], core_dev)
+        return remote(away.at[n, :, cut], near.at[n, :, cut], send.at[n], recv.at[n], core_dev)
 
     sub = 256
     for n, (which, _col, _ti, _out, step) in enumerate(plan):
@@ -1445,47 +1602,56 @@
         @pl.loop(0, step // sub)
         def _(j, n=n, which=which):
             cut = aligned(j * sub, sub)
-            for zi in range(nz):
-                away[n, zi, :, cut] = mm(left[which, 0, zi], right[n, :, cut]).astype(BF)
+            away[n, :, cut] = mm(left[which, 0], right[n, :, cut]).astype(BF)
 
         exchange(n).start()
 
+    if quarter is not None:
+        own_in.wait()
+        own_out.start()
+        for d in range(1, nz):
+            q_copy(d, z, lax.rem(z + d, nz)).start()
     outs = []
     for n, (which, _col, ti, out, step) in enumerate(plan):
         exchange(n).wait_recv()
         slot = n % 2
         if n >= 2:
-            for one in outs[n - 2]:
-                one.wait()
+            outs[n - 2].wait()
 
         @pl.loop(0, step // sub)
         def _(j, n=n, which=which, slot=slot):
             cut = aligned(j * sub, sub)
-            for zi in range(nz):
-                stage[slot, zi, :, cut] = (
-                    mm(left[which, 1, zi], right[n, :, cut]) + near[n, zi, :, cut].astype(F32)
-                ).astype(BF)
+            stage[slot, :, cut] = (
+                mm(left[which, 1], right[n, :, cut]) + near[n, :, cut].astype(F32)
+            ).astype(BF)
 
         outs.append(
-            [
-                pltpu.make_async_copy(
-                    stage.at[slot, zi, :, pl.ds(0, step)],
-                    packed.at[pl.ds((ti * nz + zi) * dblk, dblk), pl.ds(out, step)],
-                    out_sems.at[slot, zi],
-                )
-                for zi in range(nz)
-            ]
+            pltpu.make_async_copy(
+                stage.at[slot, :, pl.ds(0, step)],
+                packed.at[pl.ds(ti * nz * dblk, nz * dblk), pl.ds(out, step)],
+                out_sems.at[slot],
+            )
         )
-        for one in outs[n]:
-            one.start()
-    for group in outs[-2:]:
-        for one in group:
-            one.wait()
+        outs[n].start()
+    for one in outs[-2:]:
+        one.wait()
     for n in range(len(plan)):
         exchange(n).wait_send()
-
-
-def grads_layer(operands, nz, nt, collective_id):
+    if quarter is not None:
+        own.wait()
+        total = mine[...].astype(F32)
+        for d in range(1, nz):
+            owner = lax.rem(z + nz - d, nz)
+            q_copy(d, owner, z).wait_recv()
+            total = total + others[owner].astype(F32)
+        shard[...] = total.astype(BF)
+        own_out.wait()
+        dctx_copy.wait()
+        for d in range(1, nz):
+            q_copy(d, z, lax.rem(z + d, nz)).wait_send()
+
+
+def grads_layer(operands, nz, nt, collective_id, quarter=None, grad_context=None):
     pairs = len(operands) // 2
     width, span = operands[0].shape
     chunk = 1024
@@ -1494,23 +1660,41 @@
     count = sum(nt * max(1, size // chunk) for size in sizes)
     dma = pltpu.SemaphoreType.DMA
     hbm = pl.BlockSpec(memory_space=pl.ANY)
+    out_shape = [jax.ShapeDtypeStruct((nt * nz * dblk, sum(sizes)), BF)]
+    out_specs, extra = [hbm], []
+    if quarter is not None:
+        rest = (quarter.shape[0] // nz, quarter.shape[1])
+        operands = operands + [quarter, grad_context]
+        dctx = (2 * span, grad_context.shape[1] // 2)
+        out_shape += [jax.ShapeDtypeStruct(rest, BF), jax.ShapeDtypeStruct(dctx, BF)]
+        out_specs += [pl.BlockSpec(memory_space=pltpu.VMEM), hbm]
+        extra = [
+            pltpu.VMEM(rest, BF),
+            pltpu.VMEM((nz,) + rest, BF),
+            pltpu.VMEM((span, dctx[1]), BF),
+            dma(()),
+            dma((4,)),
+            dma((nz,)),
+            dma((nz,)),
+        ]
     return pl.pallas_call(
         functools.partial(grads_kernel, pairs=pairs, nz=nz, nt=nt, chunk=chunk),
-        out_shape=jax.ShapeDtypeStruct((nt * nz * dblk, sum(sizes)), BF),
+        out_shape=out_shape,
         in_specs=[hbm] * len(operands),
-        out_specs=hbm,
+        out_specs=out_specs,
         scratch_shapes=[
-            pltpu.VMEM((pairs, 2, nz, dblk, span), BF),
+            pltpu.VMEM((pairs, 2, nz * dblk, span), BF),
             pltpu.VMEM((count, span, chunk), BF),
-            pltpu.VMEM((count, nz, dblk, chunk), BF),
-            pltpu.VMEM((count, nz, dblk, chunk), BF),
-            pltpu.VMEM((2, nz, dblk, chunk), BF),
+            pltpu.VMEM((count, nz * dblk, chunk), BF),
+            pltpu.VMEM((count, nz * dblk, chunk), BF),
+            pltpu.VMEM((2, nz * dblk, chunk), BF),
             dma((pairs, 2, nz)),
             dma((count,)),
             dma((count,)),
             dma((count,)),
-            dma((2, nz)),
-        ],
+            dma((2,)),
+        ]
+        + extra,
         compiler_params=pltpu.CompilerParams(
             collective_id=collective_id, has_side_effects=True, vmem_limit_bytes=60 << 20
         ),
@@ -1628,14 +1812,15 @@
     seg_global = ordered(c, own_seg, other_seg)
     total = 2 * span
     blk = 256
-    low, high = segment_bounds(seg_global, blk, blk)
-    shift = jnp.reshape(c * (total // blk // 2), (1,)).astype(jnp.int32)
+    low, high = segment_bounds(seg_global, blk, FINE)
+    shift = jnp.reshape(c * (total // FINE // 2), (1,)).astype(jnp.int32)
     seg_k = jnp.broadcast_to(seg_store[:, None], (total, 128))
     seg_q = jnp.broadcast_to(seg_store[None, :], (8, total))
     attn_args = (seg_k, seg_q, low, high, shift)
     mixed, lse, mixed_other = [], [], []
     for p in range(pairs):
-        out, one = attn_fwd(qkv, *attn_args, p, pairs, group, head_size, blk, blk)
+        source = after(qkv, mixed_other[p - 2]) if p >= 2 else qkv
+        out, one = attn_fwd(source, *attn_args, p, pairs, group, head_size, blk, 3)
         mixed.append(out)
         lse.append(one)
         mixed_other.append(over_x(out[span:]))
@@ -1652,50 +1837,40 @@
     out_low, branch, branch_t, grad_second, vec_two = down_layer(
         which, out_grad, vecs, first, act_low, down_all, nt
     )
-    down_sum = grads_layer([branch_t, act_low], nz, nt, 2)
-    branch, down_sum = lax.optimization_barrier((branch, down_sum))
-    hidden_low, attn_t, grad_in, grad_context, vec_one, up_sums = back_layer(
-        vecs, branch, grad_second, slope, norm_one, inv_one, up_all, down_all, nt
-    )
-    layer_output = ordered(t, out_low[None], over_y(out_low)[None])
-    halves = grad_context[:, :cols], grad_context[:, cols:]
-    dctx_own = jnp.where(c == 0, halves[0], halves[1])
-    dctx_other = over_x(jnp.where(c == 0, halves[1], halves[0]))
-    dctx = jnp.concatenate([dctx_own, dctx_other])
-
-    other_sum = grads_layer([first_t, hidden_low, attn_t, context_rows], nz, nt, 3)
-    dctx, other_sum = lax.optimization_barrier((dctx, other_sum))
-    part = lax.psum_scatter(down_sum, ("tensor", "z"), scatter_dimension=0, tiled=True)
-    grad_down = (part.astype(F32) + over_x(part).astype(F32)).T
+    (down_sum,) = grads_layer([branch_t, act_low], nz, nt, 2)
+    hidden_low, attn_t, grad_in, grad_context, vec_one, quarter = back_layer(
+        vecs, branch, grad_second, slope, norm_one, inv_one, up_all, down_all, down_sum, nz, nt
+    )
+    out_low = after(out_low, quarter)
+    out_other = over_y(out_low)
+    other_sum, down_part, dctx = grads_layer([first_t, hidden_low, attn_t, context_rows], nz, nt, 3, quarter, grad_context)
+    grad_down = ordered(c, down_part, over_x(down_part), 0).astype(F32).T
     part = lax.psum_scatter(other_sum, ("tensor", "z", "context"), scatter_dimension=0, tiled=True)
     part = ordered(c, part, over_x(part), 0).astype(F32)
     grad_up = part[:, : hidden // nt]
     grad_proj = part[:, hidden // nt :].T
 
-    sums = jnp.concatenate([vec_one[:3].reshape(-1, 128), vec_two[:3].reshape(-1, 128), up_sums[0].reshape(-1, 128)])
-    dqkv = None
-    for p in range(pairs):
-        dqkv = attn_bwd(dqkv, qkv, mixed[p], dctx, lse[p], *attn_args, p, pairs, group, head_size, blk, blk)
-    tokens_grad, qkv_rows, qv_sum = close_layer(dqkv, qkv_full, rows_t, grad_in, sums, nz)
-    sums = qv_sum[-sums.shape[0] :].reshape(-1)
-    qv_sum = qv_sum[: 3 * cols // 128].reshape(-1)
-    vector_out = [
-        lax.dynamic_slice_in_dim(sums[i * width : (i + 1) * width], f * dblk, dblk) for i in range(6)
+    mixed = lax.optimization_barrier(tuple(mixed) + (quarter,))[:pairs]
+    dqkv = attn_bwd(
+        qkv, jnp.concatenate(mixed, axis=1), dctx, jnp.concatenate(lse), *attn_args, pairs, group, head_size, blk, 3
+    )
+    layer_output = ordered(t, out_low[None], out_other[None])
+    dqkv, grad_down, layer_output = lax.optimization_barrier((dqkv, grad_down, layer_output))
+    tokens_grad, grad_qkv, qv_sum, vec_sums = close_layer(
+        dqkv, qkv_full, rows_t, grad_in, vec_one, vec_two, nz, group * wide
+    )
+    own_vecs = lax.dynamic_slice_in_dim(vec_sums, f * dblk, dblk, 1)
+    vector_out = [own_vecs[row] for row in (0, 1, 2, 8, 9, 10)]
+    up_rows, up_cols = up_bias.shape
+    bias_up = vec_sums[3 : 3 + hidden // width].reshape(nt * up_rows, nf * up_cols)
+    bias_up = lax.dynamic_slice(bias_up, (t * up_rows, f * up_cols), (up_rows, up_cols))
+    per = wide // 128 * group
+    kinds = [
+        jnp.concatenate([qv_sum[(3 * g + which) * per :][:per] for g in range(pairs // group)])
+        for which in (0, 2)
     ]
-    up_rows, up_cols = up_bias.shape
-    bias_up = sums[6 * width :].reshape(nt * up_rows, nf * up_cols)
-    bias_up = lax.dynamic_slice(bias_up, (t * up_rows, f * up_cols), (up_rows, up_cols))
-
-
-    def unpack(rows, which):
-        return jnp.concatenate(
-            [rows[..., (3 * i + which * group) * wide :][..., : group * wide] for i in range(0, pairs, group)],
-            axis=-1,
-        )
-
-    grad_qkv = jnp.stack([unpack(qkv_rows, which) for which in range(3)])
-    qv_sum = jnp.concatenate([unpack(qv_sum, 0), unpack(qv_sum, 2)]).reshape(2, heads, head_size)
-    grad_qv = lax.dynamic_slice_in_dim(qv_sum, f * (head_size // nf), head_size // nf, 2)
+    grad_qv = jnp.stack(kinds).reshape(2, heads, head_size)
+    grad_qv = lax.dynamic_slice_in_dim(grad_qv, f * (head_size // nf), head_size // nf, 2)
 
     return (
         layer_output,

time: 601 us -> 558 us (0.928)
  local copies, waits for them, and re-layouts: 36.1 us -> 21.5 us
  Pallas kernels: 491 us -> 480 us
  waiting for transfers between devices: 16.3 us -> 9.13 us
    pallas_call x1, Pallas kernels: 107 us -> 92.2 us  [close_layer(): pl.pallas_call(functools.partial(close_kernel, nz=nz, chunk=chunk, tile=t...]
    pallas_call x2, Pallas kernels: 41.5 us -> 55.9 us  [grads_layer(): pl.pallas_call(functools.partial(grads_kernel, pairs=pairs, nz=nz, nt=nt,...]
    pallas_call x9 -> x6, Pallas kernels: 205 us -> 191 us  [the longest x1 79.6 us: attn_bwd(): pl.pallas_call(functools.partial(attn_bwd_kernel, bk=bk, fine=FINE, many=...]
    unnamed x75 -> x60, local copies, waits for them, and re-layouts: 24.5 us -> 17.3 us
    ppermute x9 -> x8, waiting for transfers between devices: 15.5 us -> 8.38 us  [send(): return lax.ppermute(value, AXES, pairs)]
  transfers between devices with their start and end apart: 13 -> 11, of which waited for: 3 -> 2; matrix products, arithmetic and copies ran while one was open for 5% -> 4% of each run, Pallas kernels for 76% -> 63%
where the time goes in v3:
time: 558 us; the launch traced here: 549 us
  Pallas kernels  480 us (86%)
  local copies, waits for them, and re-layouts  21.5 us (4%)
  between operations  14.8 us (3%)
  other arithmetic  14 us (3%)
  waiting for transfers between devices  9.13 us (2%)
  starting transfers between devices  8.44 us (2%)
    pallas_call x1, Pallas kernels, close_layer(): pl.pallas_call(functools.partial(close_kernel, nz=nz, chunk=chunk, tile=t...  92.2 us
    pallas_call x1, Pallas kernels, open_layer(): pl.pallas_call(functools.partial(open_kernel, nz=nz, nt=nt, heads=heads,...  82.4 us
    pallas_call x1, Pallas kernels, attn_bwd(): pl.pallas_call(functools.partial(attn_bwd_kernel, bk=bk, fine=FINE, many=...  79.6 us
    pallas_call x4, Pallas kernels, attn_fwd(): pl.pallas_call(functools.partial(attn_fwd_kernel, fine=FINE, many=many, h...  59.4 us
    pallas_call x2, Pallas kernels, grads_layer(): pl.pallas_call(functools.partial(grads_kernel, pairs=pairs, nz=nz, nt=nt,...  55.9 us
    pallas_call x1, Pallas kernels, back_layer(): pl.pallas_call(functools.partial(back_kernel, nz=nz, nt=nt, tile=tile), o...  52.5 us
    pallas_call x1, Pallas kernels, up_layer(): pl.pallas_call(functools.partial(up_kernel, nt=nt, tile=tile), out_shape=...  33.6 us
    pallas_call x1, Pallas kernels, down_layer(): pl.pallas_call(functools.partial(down_kernel, nt=nt), out_shape=(sds((spa...  24.8 us
  transfers between devices with their start and end apart: 11, of which 2 were waited for; matrix products, arithmetic and copies ran while one was open for 4% of the time, Pallas kernels for 63%

profile of v3, /device:TPU:28, one launch (start us, length us, event | category | flops | bytes accessed | tf_op | source)
XLA Modules:
  0.0 549.1 jit_solution(7810189529823756879)
XLA Ops:
  8.3 1.9 pad_maximum_fusion.1
  12.3 1.6 collective-permute-start
  14.9 82.4 %open_layer.1 = (bf16[1024,2048]{1,0:T(8,128)(2,1)}, bf16[1024,1536]{1,0:T(8,128)(2,1)}, bf16[2048,1536]{1,0:T(8,128)(2,1)}, bf16[16,16,128]{2,1,0:T(8,128)(2,1)}) custom-call(bf16[2,1024,1024]{2,1,0:T(8,128)(2,1)} %tok.1, bf16[3,128,512]{2,1,0:T(8,128)(2,1)} %weight.1, bf16[16,128]{1,0:T(8,128)(2,1)} %pad.4.small), custom_call_target="tpu_custom_call" | custom-call | flops 6442450944 | bytes 16777216 | tf_op jit(solution)/shard_map/open_layer/pallas_call | solution.py:796
  101.8 3.2 copy-done.5
  105.0 14.8 %attn_fwd.4 = (bf16[2048,128]{1,0:T(8,128)(2,1)S(1)}, f32[1,2,2048]{2,1,0:T(2,128)S(1)}) custom-call(s32[8]{0:T(128)S(1)} %get-tuple-element.199.lo_ref, s32[8]{0:T(128)S(1)} %get-tuple-element.198.hi_ref, s32[1]{0:T(128)} %bitcast.1.shift_ref, bf16[2048,1536]{1,0:T(8,128)(2,1)S(1)} %copy-done.5, bf16[2048,1536]{1,0:T(8,128)(2,1)S(1)} %copy-done.5, ...), custom_call_target="tpu_custom_call" | custom-call | flops 15000000512 | bytes 2097152 | tf_op jit(solution)/shard_map/attn_fwd/pallas_call | solution.py:477
  119.9 14.8 %attn_fwd.5 = (bf16[2048,128]{1,0:T(8,128)(2,1)S(1)}, f32[1,2,2048]{2,1,0:T(2,128)S(1)}) custom-call(s32[8]{0:T(128)S(1)} %get-tuple-element.199.lo_ref, s32[8]{0:T(128)S(1)} %get-tuple-element.198.hi_ref, s32[1]{0:T(128)} %bitcast.1.shift_ref, bf16[2048,1536]{1,0:T(8,128)(2,1)S(1)} %copy-done.5, bf16[2048,1536]{1,0:T(8,128)(2,1)S(1)} %copy-done.5, ...), custom_call_target="tpu_custom_call" | custom-call | flops 15000000512 | bytes 2097152 | tf_op jit(solution)/shard_map/attn_fwd/pallas_call | solution.py:477
  134.8 2.1 collective-permute-start.2
  136.9 14.8 %attn_fwd.6 = (bf16[2048,128]{1,0:T(8,128)(2,1)S(1)}, f32[1,2,2048]{2,1,0:T(2,128)S(1)}) custom-call(s32[8]{0:T(128)S(1)} %get-tuple-element.199.lo_ref, s32[8]{0:T(128)S(1)} %get-tuple-element.198.hi_ref, s32[1]{0:T(128)} %bitcast.1.shift_ref, bf16[2048,1536]{1,0:T(8,128)(2,1)S(1)} %copy-done.5, bf16[2048,1536]{1,0:T(8,128)(2,1)S(1)} %copy-done.5, ...), custom_call_target="tpu_custom_call" | custom-call | flops 15000000512 | bytes 2097152 | tf_op jit(solution)/shard_map/attn_fwd/pallas_call | solution.py:477
  151.9 14.8 %attn_fwd.7 = (bf16[2048,128]{1,0:T(8,128)(2,1)S(1)}, f32[1,2,2048]{2,1,0:T(2,128)S(1)}) custom-call(s32[8]{0:T(128)S(1)} %get-tuple-element.199.lo_ref, s32[8]{0:T(128)S(1)} %get-tuple-element.198.hi_ref, s32[1]{0:T(128)} %bitcast.1.shift_ref, bf16[2048,1536]{1,0:T(8,128)(2,1)S(1)} %copy-done.5, bf16[2048,1536]{1,0:T(8,128)(2,1)S(1)} %copy-done.5, ...), custom_call_target="tpu_custom_call" | custom-call | flops 15000000512 | bytes 2097152 | tf_op jit(solution)/shard_map/attn_fwd/pallas_call | solution.py:477
  166.7 2.1 collective-permute-start.4
  169.7 3.9 collective-permute-done.4
  174.8 1.5 broadcast_select_fusion.ctx.refs_3_
  176.4 33.6 %up_layer.1 = (f32[1024,1024]{1,0:T(8,128)}, f32[1024,1024]{1,0:T(8,128)}, f32[1024,128]{1,0:T(8,128)}, bf16[1024,1024]{1,0:T(8,128)(2,1)}, bf16[1024,4096]{1,0:T(8,128)(2,1)}, /*index=5*/bf16[1024,4096]{1,0:T(8,128)(2,1)}) custom-call(s32[1]{0:T(128)} %bitcast.12.t_ref, bf16[1024,1024]{1,0:T(8,128)(2,1)} %broadcast_select_fusion.ctx.refs_3_, ...), custom_call_target="tpu_custom_call" | custom-call | flops 10737418240 | bytes 41943040 | tf_op jit(solution)/shard_map/up_layer/pallas_call | solution.py:1189
  210.0 24.8 %down_layer.1 = (bf16[1024,1024]{1,0:T(8,128)(2,1)}, bf16[1024,1024]{1,0:T(8,128)(2,1)}, bf16[1024,1024]{1,0:T(8,128)(2,1)}, f32[1024,1024]{1,0:T(8,128)}, f32[8,1024]{1,0:T(8,128)}) custom-call(s32[1]{0:T(128)} %bitcast.12.t_ref, bf16[2,1024,1024]{2,1,0:T(8,128)(2,1)} %cot.1, f32[8,1024]{1,0:T(8,128)} %convert_bitcast_fusion.1.vecs, ...), custom_call_target="tpu_custom_call" | custom-call | flops 8589934592 | bytes 31457280 | tf_op jit(solution)/shard_map/down_layer/pallas_call | solution.py:1288
  234.8 19.3 %grads_layer.2.partial = bf16[1024,2048]{1,0:T(8,128)(2,1)} custom-call(bf16[1024,1024]{1,0:T(8,128)(2,1)} %get-tuple-element.83.refs_0_, bf16[1024,4096]{1,0:T(8,128)(2,1)} %get-tuple-element.76.act.refs_1_), custom_call_target="tpu_custom_call" | custom-call | flops 8589934592 | bytes 41943040 | tf_op jit(solution)/shard_map/grads_layer/pallas_call | solution.py:1680
  254.1 52.5 %back_layer.1 = (bf16[1024,4096]{1,0:T(8,128)(2,1)}, bf16[1024,1024]{1,0:T(8,128)(2,1)}, f32[1024,1024]{1,0:T(8,128)}, bf16[1024,1024]{1,0:T(8,128)(2,1)}, f32[8,1024]{1,0:T(8,128)}, /*index=5*/bf16[256,2048]{1,0:T(8,128)(2,1)}) custom-call(f32[8,1024]{1,0:T(8,128)} %convert_bitcast_fusion.1.vecs, bf16[1024,1024]{1,0:T(8,128)(2,1)} %get-tuple-element.78.branch, ...), custom_call_target="tpu_custom_call" | custom-call | flops 19327352832 | bytes 62914560 | tf_op jit(solution)/shard_map/back_layer/pallas_call | solution.py:1455
  306.6 36.6 %grads_layer.3 = (bf16[1024,2560]{1,0:T(8,128)(2,1)}, bf16[64,2048]{1,0:T(8,128)(2,1)}, bf16[2048,512]{1,0:T(8,128)(2,1)}) custom-call(bf16[1024,1024]{1,0:T(8,128)(2,1)} %get-tuple-element.89.refs_0_, bf16[1024,4096]{1,0:T(8,128)(2,1)} %get-tuple-element.90.refs_1_, bf16[1024,1024]{1,0:T(8,128)(2,1)} %get-tuple-element.91.refs_2_, ...), custom_call_target="tpu_custom_call" | custom-call | flops 10737418240 | bytes 41943040 | tf_op jit(solution)/shard_map/grads_layer/pallas_call | solution.py:1680
  345.4 1.5 pad_maximum_fusion.o_ref
  347.0 79.6 %attn_bwd.1.dqkv_in = bf16[2048,1536]{1,0:T(8,128)(2,1)} custom-call(s32[8]{0:T(128)} %copy-done.4, s32[8]{0:T(128)} %copy-done.3, s32[1]{0:T(128)} %bitcast.1.shift_ref, bf16[2048,1536]{1,0:T(8,128)(2,1)} %get-tuple-element.69.q_ref.k_ref.v_ref, bf16[2048,1536]{1,0:T(8,128)(2,1)} %get-tuple-element.69.q_ref.k_ref.v_ref, ...), custom_call_target="tpu_custom_call" | custom-call | flops 99999997952 | bytes 16777216 | tf_op jit(solution)/shard_map/attn_bwd/pallas_call | solution.py:514
  426.7 4.5 maximum_select_fusion
  431.2 92.2 %close_layer.1 = (bf16[2,1024,1024]{2,1,0:T(8,128)(2,1)S(1)}, f32[3,128,512]{2,1,0:T(8,128)S(1)}, f32[16,128]{1,0:T(8,128)S(1)}, f32[16,1024]{1,0:T(8,128)S(1)}) custom-call(bf16[2048,1536]{1,0:T(8,128)(2,1)} %attn_bwd.1.dqkv_in, bf16[1024,1536]{1,0:T(8,128)(2,1)S(1)} %copy-done.6, bf16[1024,2048]{1,0:T(8,128)(2,1)} %get-tuple-element.104.xt_in, ...), custom_call_target="tpu_custom_call" | custom-call | flops 12884901888 | bytes 31457280 | tf_op jit(solution)/shard_map/close_layer/pallas_call | solution.py:1052
  523.4 2.0 copy-done
  530.2 4.4 collective-permute-done.7
  536.6 4.6 copy.83
  (122 shorter events, 20.7 us)
Async XLA Ops:
  7.2 6.8 %copy-start.13 = (bf16[2,8,8]{2,1,0:T(8,128)(2,1)S(1)}, bf16[2,8,8]{2,1,0:T(8,128)(2,1)}, u32[]{:S(2)}) copy-start(bf16[2,8,8]{2,1,0:T(8,128)(2,1)} %param.18) | copy-start | bytes 772
  7.2 6.9 %copy-start.15 = (bf16[128]{0:T(256)(128)(2,1)S(1)}, bf16[128]{0:T(256)(128)(2,1)}, u32[]{:S(2)}) copy-start(bf16[128]{0:T(256)(128)(2,1)} %param.20) | copy-start | bytes 772
  7.2 6.9 %copy-start.16 = (bf16[128]{0:T(256)(128)(2,1)S(1)}, bf16[128]{0:T(256)(128)(2,1)}, u32[]{:S(2)}) copy-start(bf16[128]{0:T(256)(128)(2,1)} %param.21) | copy-start | bytes 772
  7.2 6.9 %copy-start.17 = (bf16[128]{0:T(256)(128)(2,1)S(1)}, bf16[128]{0:T(256)(128)(2,1)}, u32[]{:S(2)}) copy-start(bf16[128]{0:T(256)(128)(2,1)} %param.22) | copy-start | bytes 772
  7.2 6.9 %copy-start.18 = (bf16[128]{0:T(256)(128)(2,1)S(1)}, bf16[128]{0:T(256)(128)(2,1)}, u32[]{:S(2)}) copy-start(bf16[128]{0:T(256)(128)(2,1)} %param.26) | copy-start | bytes 772
  7.3 6.9 %copy-start.19 = (bf16[128]{0:T(256)(128)(2,1)S(1)}, bf16[128]{0:T(256)(128)(2,1)}, u32[]{:S(2)}) copy-start(bf16[128]{0:T(256)(128)(2,1)} %param.27) | copy-start | bytes 772
  7.3 6.9 %copy-start.20 = (bf16[128]{0:T(256)(128)(2,1)S(1)}, bf16[128]{0:T(256)(128)(2,1)}, u32[]{:S(2)}) copy-start(bf16[128]{0:T(256)(128)(2,1)} %param.28) | copy-start | bytes 772
  7.3 169.1 %all-gather.7.cloned.1.call-start = ((), (), s32[]{:S(2)}) async-start(), calls=%async_computation.3 | async-start | bytes 11141120 | tf_op jit(solution)/shard_map/all_gather | solution.py:1808
  10.3 199.7 %all-gather.5.cloned.1.call-start = ((), (), s32[]{:S(2)}) async-start(), calls=%async_computation.2 | async-start | bytes 8912896 | tf_op jit(solution)/shard_map/all_gather | solution.py:1809
  11.0 514.4 %reduce-scatter.2.cloned.1.call-start = ((), (), s32[]{:S(2)}) async-start(), calls=%async_computation.1 | async-start | bytes 5570560 | tf_op jit(solution)/shard_map/reduce_scatter | solution.py:1848
  12.3 88.6 %collective-permute-start = (s32[1024]{0:T(1024)S(1)}, s32[1024]{0:T(1024)S(1)}, u32[]{:S(2)}, u32[]{:S(2)}) collective-permute-start(s32[1024]{0:T(1024)S(1)} %bitcast.57), channel_id=1, source_target_pairs={{0,2},{1,3},{2,0},{3,1},{4,6},{5,7},{6,4},{7,5},{8,10},{9,11},{10,... | collective-permute-start | bytes 12296 | tf_op jit(solution)/shard_map/ppermute | solution.py:1741
  101.4 50.4 %copy-start.3 = (s32[8]{0:T(128)}, s32[8]{0:T(128)S(1)}, u32[]{:S(2)}) copy-start(s32[8]{0:T(128)S(1)} %get-tuple-element.198.hi_ref) | copy-start | bytes 100
  101.4 50.4 %copy-start.4 = (s32[8]{0:T(128)}, s32[8]{0:T(128)S(1)}, u32[]{:S(2)}) copy-start(s32[8]{0:T(128)S(1)} %get-tuple-element.199.lo_ref) | copy-start | bytes 100
  101.7 50.1 %copy-start.1 = (s32[2048,128]{1,0:T(8,128)}, s32[2048,128]{1,0:T(8,128)S(1)}, u32[]{:S(2)}) copy-start(s32[2048,128]{1,0:T(8,128)S(1)} %broadcast_in_dim.13.segk_ref) | copy-start | bytes 3145732
  101.8 50.1 %copy-start.2 = (s32[8,2048]{1,0:T(8,128)}, s32[8,2048]{1,0:T(8,128)S(1)}, u32[]{:S(2)}) copy-start(s32[8,2048]{1,0:T(8,128)S(1)} %broadcast_in_dim.26.segq_ref) | copy-start | bytes 196612
  119.8 17.0 %collective-permute-start.1 = (bf16[1024,128]{1,0:T(8,128)(2,1)S(1)}, bf16[1024,128]{1,0:T(8,128)(2,1)S(1)}, u32[]{:S(2)}, u32[]{:S(2)}) collective-permute-start(bf16[1024,128]{1,0:T(8,128)(2,1)S(1)} %slice.94), channel_id=1, source_target_pairs={{0,2},{1,3},{2,0},{3,1},{4,6},{5,7},{6,4},{7,5},{8,10},{9,11},{10,... | collective-permute-start | bytes 786440 | tf_op jit(solution)/shard_map/ppermute | solution.py:1741
  134.8 17.0 %collective-permute-start.2 = (bf16[1024,128]{1,0:T(8,128)(2,1)S(1)}, bf16[1024,128]{1,0:T(8,128)(2,1)S(1)}, u32[]{:S(2)}, u32[]{:S(2)}) collective-permute-start(bf16[1024,128]{1,0:T(8,128)(2,1)S(1)} %slice.95), channel_id=1, source_target_pairs={{0,2},{1,3},{2,0},{3,1},{4,6},{5,7},{6,4},{7,5},{8,10},{9,11},{10,... | collective-permute-start | bytes 786440 | tf_op jit(solution)/shard_map/ppermute | solution.py:1741
  151.7 17.9 %collective-permute-start.3 = (bf16[1024,128]{1,0:T(8,128)(2,1)S(1)}, bf16[1024,128]{1,0:T(8,128)(2,1)S(1)}, u32[]{:S(2)}, u32[]{:S(2)}) collective-permute-start(bf16[1024,128]{1,0:T(8,128)(2,1)S(1)} %slice.101), channel_id=1, source_target_pairs={{0,2},{1,3},{2,0},{3,1},{4,6},{5,7},{6,4},{7,5},{8,10},{9,11},{10,... | collective-permute-start | bytes 786440 | tf_op jit(solution)/shard_map/ppermute | solution.py:1741
  166.7 6.9 %collective-permute-start.4 = (bf16[1024,128]{1,0:T(8,128)(2,1)S(1)}, bf16[1024,128]{1,0:T(8,128)(2,1)S(1)}, u32[]{:S(2)}, u32[]{:S(2)}) collective-permute-start(bf16[1024,128]{1,0:T(8,128)(2,1)S(1)} %slice.102), channel_id=1, source_target_pairs={{0,2},{1,3},{2,0},{3,1},{4,6},{5,7},{6,4},{7,5},{8,10},{9,11},{10,... | collective-permute-start | bytes 786440 | tf_op jit(solution)/shard_map/ppermute | solution.py:1741
  343.3 83.4 %collective-permute-start.6 = (bf16[1024,1024]{1,0:T(8,128)(2,1)}, bf16[1024,1024]{1,0:T(8,128)(2,1)}, u32[]{:S(2)}, u32[]{:S(2)}) collective-permute-start(bf16[1024,1024]{1,0:T(8,128)(2,1)} %get-tuple-element.100), channel_id=1, source_target_pairs={{0,1},{1,0},{2,3},{3,2},{4,5},{5,4},{6,7},{7,6},{8,9},{9,8},{10,11... | collective-permute-start | bytes 6291464 | tf_op jit(solution)/shard_map/ppermute | solution.py:1741
  344.2 82.4 %collective-permute-start.5 = (bf16[64,2048]{1,0:T(8,128)(2,1)S(1)}, bf16[64,2048]{1,0:T(8,128)(2,1)S(1)}, u32[]{:S(2)}, u32[]{:S(2)}) collective-permute-start(bf16[64,2048]{1,0:T(8,128)(2,1)S(1)} %copy-done.11), channel_id=1, source_target_pairs={{0,2},{1,3},{2,0},{3,1},{4,6},{5,7},{6,4},{7,5},{8,10},{9,11},{10,... | collective-permute-start | bytes 786440 | tf_op jit(solution)/shard_map/ppermute | solution.py:1741
  347.0 79.7 %copy-start.9 = (bf16[1024,1024]{1,0:T(8,128)(2,1)S(1)}, bf16[1024,1024]{1,0:T(8,128)(2,1)}, u32[]{:S(2)}) copy-start(bf16[1024,1024]{1,0:T(8,128)(2,1)} %get-tuple-element.100) | copy-start | bytes 6291460
  525.5 9.1 %copy-start.10 = (bf16[64,2560]{1,0:T(8,128)(2,1)S(1)}, bf16[64,2560]{1,0:T(8,128)(2,1)}, u32[]{:S(2)}) copy-start(bf16[64,2560]{1,0:T(8,128)(2,1)} %reduce-scatter.2.cloned.1.call-done) | copy-start | bytes 983044
  525.5 9.1 %collective-permute-start.7 = (bf16[64,2560]{1,0:T(8,128)(2,1)}, bf16[64,2560]{1,0:T(8,128)(2,1)S(1)}, u32[]{:S(2)}, u32[]{:S(2)}) collective-permute-start(bf16[64,2560]{1,0:T(8,128)(2,1)} %reduce-scatter.2.cloned.1.call-done), channel_id=1, source_target_pairs={{0,2},{1,3},{2,0},{3,1},{4,6},{5,7},{6,4},{7,5},{8,10},{9,11},{10,... | collective-permute-start | bytes 983048 | tf_op jit(solution)/shard_map/ppermute | solution.py:1741
  (8 other events, 30.8 us)
Sparse Core Ops, SparseCore 0:
  11.0 113.6 all-gather.6
  126.9 73.3 all-gather.4
  343.4 126.3 reduce-scatter.1
